TPU v7x, 32 devices: a whole 2x2x4 slice. The times are simulated.
32 devices in a mesh: lon: 8 (over y, x, core), lat: 4 (over z).
Axes of the slice: x: 2, y: 2, z: 4, core: 2. Of those that a mesh axis runs over, the one named last changes fastest.
Arguments:
- gradient: float32 [137, 16, 1024], P(None, 'lat', 'lon'), may hold values from -60 to 60
- obs_weight: float32 [137, 16, 1024], P(None, 'lat', 'lon'), may hold values from 0.2 to 5
- half_width: int32 [16], P('lat'), may hold values from 8 to 32
- zonal_coef: float32 [16, 33], P('lat'), may hold values from 0.2 to 1
- mirror_map: int32 [1024], P('lon'), may hold values from 0 to 1023, as said below
- merid_coef: float32 [5], replicated, may hold values from 0.2 to 1
- vertical_map: float32 [137, 137], replicated, may hold values from -0.5 to 0.5
Outputs:
- increment: float32 [137, 16, 1024], P(None, 'lat', 'lon')
- residual: float32 [137, 16, 1024], P(None, 'lat', 'lon')
Inputs may be any that keep to these rules, and one draw needn't show every extreme that they name: mirror_map[mirror_map[i]] = i, and mirror_map[i] lies in the block of 128 longitudes whose block index differs from i // 128 by 4.
All inputs are finite; a program needn't handle non-finite values.
Results may differ from a plain program's by a relative error of at most 0.04.
Values sent between devices are 32-bit elements; how exact they have to be, the bound alone decides.
No kernel may reach another device: no remote copies, remote signals or barrier semaphores. Data moves between devices by JAX's collectives and lax.ppermute only.
A program may use at most 64 MiB of HBM per device.

v0:
```python
import functools

import jax
import jax.numpy as jnp
from jax import lax
from jax.experimental import pallas as pl
from jax.experimental.pallas import tpu as pltpu
from jax.sharding import PartitionSpec as P

OUTER = 2
AXES = ("lon", "lat")
HI = lax.Precision.HIGHEST
KERNEL_PRECISION = lax.Precision.HIGH


def zonal_weights(half_width, zonal_coef):
    tap_ids = jnp.arange(zonal_coef.shape[1], dtype=jnp.int32)
    kept = jnp.where(
        tap_ids[None, :] <= half_width[:, None], zonal_coef, jnp.zeros_like(zonal_coef)
    )
    scaling = jnp.sqrt(kept[:, 0] ** 2 + 2.0 * jnp.sum(kept[:, 1:] ** 2, axis=1))
    return kept / scaling[:, None]


def merid_weights(merid_coef):
    norm_value = jnp.sqrt(merid_coef[0] ** 2 + 2.0 * jnp.sum(merid_coef[1:] ** 2))
    return merid_coef / norm_value


def zonal_tables(weights, block):
    width = weights.shape[1] - 1
    positions = jnp.arange(3 * block, dtype=jnp.int32)
    columns = jnp.arange(block, dtype=jnp.int32)
    tap_ids = jnp.arange(width + 1, dtype=jnp.int32)
    distance = jnp.abs(positions[:, None] - block - columns[None, :])
    selector = (distance[:, :, None] == tap_ids[None, None, :]).astype(jnp.float32)
    table = jnp.einsum("pct,jt->jpc", selector, weights, precision=HI)
    return table.reshape(weights.shape[0], 3, block, block)


def mirror_tables(mirror_all, block):
    return (mirror_all % block).reshape(mirror_all.shape[0] // block, block)


def _zonal_rows(src, dst, table_ref, nb):
    rows, _, lp, block = src.shape
    for j in range(rows):
        mid = src[j]
        prev = jnp.concatenate([mid[nb - 1 :], mid[: nb - 1]], axis=0) if nb > 1 else mid
        nxt = jnp.concatenate([mid[1:], mid[:1]], axis=0) if nb > 1 else mid
        acc = jnp.dot(prev.reshape(nb * lp, block), table_ref[j, 0], preferred_element_type=jnp.float32, precision=KERNEL_PRECISION)
        acc = acc + jnp.dot(mid.reshape(nb * lp, block), table_ref[j, 1], preferred_element_type=jnp.float32, precision=KERNEL_PRECISION)
        acc = acc + jnp.dot(nxt.reshape(nb * lp, block), table_ref[j, 2], preferred_element_type=jnp.float32, precision=KERNEL_PRECISION)
        dst[j] = acc.reshape(nb, lp, block)

def _merid_rows(src, dst, mir, onehot_ref, w_ref, nb, depth):
    rows, _, lp, block = src.shape
    half = nb // 2
    def mirror_block(b, carry):
        sb = lax.rem(b + half, nb)
        polar = jnp.concatenate([src[pl.ds(0, depth), pl.ds(sb, 1)], src[pl.ds(rows - depth, depth), pl.ds(sb, 1)]], axis=0)
        source = lax.broadcasted_iota(jnp.int32, (block, block), 0)
        onehot = (source == onehot_ref[pl.ds(b, 1), :]).astype(jnp.float32)
        out = jnp.dot(polar.reshape(2 * depth * lp, block), onehot, preferred_element_type=jnp.float32, precision=KERNEL_PRECISION)
        mir[:, pl.ds(b, 1)] = out.reshape(2 * depth, 1, lp, block)
        return carry
    lax.fori_loop(0, nb, mirror_block, 0)
    def row(k):
        if k < 0:
            return mir[-1 - k]
        if k >= rows:
            return mir[depth + (rows - 1 - (k - rows)) - (rows - depth)]
        return src[k]
    for j in range(rows):
        acc = w_ref[0] * src[j]
        for o in range(1, depth + 1):
            acc = acc + w_ref[o] * (row(j - o) + row(j + o))
        dst[j] = acc

def _kernel(order, depth, x_ref, table_ref, onehot_ref, w_ref, o_ref, tmp, mir):
    nb = x_ref.shape[1]
    if order == "zm":
        _zonal_rows(x_ref, tmp, table_ref, nb)
        _merid_rows(tmp, o_ref, mir, onehot_ref, w_ref, nb, depth)
    else:
        _merid_rows(x_ref, tmp, mir, onehot_ref, w_ref, nb, depth)
        _zonal_rows(tmp, o_ref, table_ref, nb)

def level_apply(order, x, table, onehot, merid_w):
    rows, nb, lp, block = x.shape
    depth = merid_w.shape[0] - 1
    vmem = pltpu.MemorySpace.VMEM
    return pl.pallas_call(
        functools.partial(_kernel, order, depth),
        out_shape=jax.ShapeDtypeStruct(x.shape, jnp.float32),
        in_specs=[pl.BlockSpec(memory_space=vmem), pl.BlockSpec(memory_space=vmem), pl.BlockSpec(memory_space=vmem), pl.BlockSpec(memory_space=pltpu.MemorySpace.SMEM)],
        out_specs=pl.BlockSpec(memory_space=vmem),
        scratch_shapes=[pltpu.VMEM(x.shape, jnp.float32), pltpu.VMEM((2 * depth, nb, lp, block), jnp.float32)],
        compiler_params=pltpu.CompilerParams(vmem_limit_bytes=60 * 1024 * 1024),
    )(x, table, onehot, merid_w)


def per_device(gradient, obs_weight, half_width, zonal_coef, mirror_map, merid_coef, vertical_map):
    n_lon = lax.axis_size("lon")
    n_lat = lax.axis_size("lat")
    n_dev = n_lon * n_lat
    lev, rows, cols = gradient.shape
    per = -(-lev // n_dev)
    padded = -(-per // 8) * 8 if per >= 4 else per
    width = zonal_coef.shape[1] - 1
    merid_w = merid_weights(merid_coef)

    def exchange(parts):
        return lax.all_to_all(parts, AXES, 0, 0, tiled=True)

    def col_parts(x):
        x = jnp.pad(x, ((0, n_dev * per - lev), (0, 0), (0, 0)))
        return x.reshape(n_dev, per, rows, cols)

    def to_level(z):
        z = z.reshape(n_lon, n_lat, per, rows, cols).transpose(1, 3, 0, 2, 4)
        z = z.reshape(n_lat * rows, n_lon, per, cols)
        return jnp.pad(z, ((0, 0), (0, 0), (0, padded - per), (0, 0)))

    def level_parts(v):
        v = v[:, :, :per].reshape(n_lat, rows, n_lon, per, cols).transpose(2, 0, 3, 1, 4)
        return v.reshape(n_dev, per, rows, cols)

    def to_column(z):
        return z.reshape(n_dev * per, rows, cols)[:lev]

    def slab(values):
        flat = jnp.zeros((rows * cols,), jnp.float32).at[: values.shape[0]].set(values)
        return jnp.broadcast_to(flat.reshape(1, 1, rows, cols), (n_dev, 1, rows, cols))

    mirror_slab = jnp.zeros((1, 1, rows, cols), jnp.float32).at[0, 0, 0].set(
        mirror_map.astype(jnp.float32)
    )
    zonal_slab = jnp.zeros((1, 1, rows, cols), jnp.float32).at[0, 0, :, : width + 1].set(
        zonal_weights(half_width, zonal_coef)
    )
    got = exchange(
        jnp.concatenate(
            [
                col_parts(gradient),
                jnp.broadcast_to(mirror_slab, (n_dev, 1, rows, cols)),
                jnp.broadcast_to(zonal_slab, (n_dev, 1, rows, cols)),
            ],
            axis=1,
        )
    )
    residual = to_level(got[:, :per])
    mirror_all = (
        got[:, per, 0, :].reshape(n_lon, n_lat, cols)[:, 0].reshape(n_lon * cols).astype(jnp.int32)
    )
    zonal_all = (
        got[:, per + 1, :, : width + 1]
        .reshape(n_lon, n_lat, rows, width + 1)[0]
        .reshape(n_lat * rows, width + 1)
    )
    table = zonal_tables(zonal_all, cols)
    onehot = mirror_tables(mirror_all, cols)

    def forward(x):
        return level_apply("zm", x, table, onehot, merid_w)

    def backward(g):
        return level_apply("mz", g, table, onehot, merid_w)

    def middle(y):
        lifted = jnp.einsum("kl,lji->kji", vertical_map, y, precision=HI)
        return jnp.einsum("lk,lji->kji", vertical_map, obs_weight * lifted, precision=HI)

    def image(x, px_col):
        return x + backward(to_level(exchange(col_parts(middle(px_col)))))

    res_col = gradient
    inc_col = jnp.zeros_like(gradient)
    pres_col = to_column(exchange(level_parts(forward(residual))))
    for outer in range(OUTER):
        last = outer == OUTER - 1
        first = image(residual, pres_col)
        got = exchange(jnp.concatenate([level_parts(forward(first)), level_parts(first)], axis=1))
        pfirst_col = to_column(got[:, :per])
        first_col = to_column(got[:, per:])
        second = image(first, pfirst_col)
        sums = jnp.stack(
            [
                jnp.sum(residual * residual),
                jnp.sum(residual * first),
                jnp.sum(first * first),
                jnp.sum(first * second),
            ]
        )
        parts = [level_parts(second)]
        if not last:
            parts.append(level_parts(forward(second)))
        got = exchange(jnp.concatenate(parts + [slab(sums)], axis=1))
        second_col = to_column(got[:, :per])
        total = jnp.sum(got[:, len(parts) * per, 0, : sums.shape[0]], axis=0)
        sum_rr, sum_rf, sum_ff, sum_fs = total[0], total[1], total[2], total[3]
        determinant = sum_rf * sum_fs - sum_ff * sum_ff
        coef_one = (sum_fs * sum_rr - sum_ff * sum_rf) / determinant
        coef_two = (sum_rf * sum_rf - sum_ff * sum_rr) / determinant
        inc_col = inc_col + coef_one * res_col + coef_two * first_col
        res_col = res_col - coef_one * first_col - coef_two * second_col
        if not last:
            psecond_col = to_column(got[:, per : 2 * per])
            residual = residual - coef_one * first - coef_two * second
            pres_col = pres_col - coef_one * pfirst_col - coef_two * psecond_col
    return (inc_col, res_col)


def solution(mesh):
    placed = (
        P(None, "lat", "lon"),
        P(None, "lat", "lon"),
        P("lat"),
        P("lat", None),
        P("lon"),
        P(),
        P(),
    )
    return jax.shard_map(
        per_device,
        mesh=mesh,
        in_specs=placed,
        out_specs=(P(None, "lat", "lon"), P(None, "lat", "lon")),
        check_vma=False,
    )
```

profile of v0, /device:TPU:1, one launch (start us, length us, event | category | flops | bytes accessed | tf_op | source)
XLA Modules:
  0.0 280.4 jit_solution(3326664569725464809)
XLA Ops:
  0.6 0.8 copy.130
  2.9 0.7 convert_bitcast_fusion
  3.6 1.0 pad.47
  4.6 0.9 pad_maximum_fusion.3
  5.5 7.1 %all-to-all-start = ((f32[32,7,4,128]{3,2,1,0:T(4,128)}), f32[32,7,4,128]{3,2,1,0:T(4,128)S(1)}, u32[]{:S(2)}, u32[]{:S(2)}) async-start(f32[32,7,4,128]{3,2,1,0:T(4,128)} %pad_maximum_fusion.3), calls=%async_computation | async-start | bytes 917504 | tf_op jit(solution)/shard_map/all_to_all | solution.py:114
  13.9 1.3 multiply_reduce_fusion.8
  15.9 1.2 broadcast_divide_fusion.w_ref
  17.2 9.3 %all-to-all-done = f32[32,7,4,128]{3,2,1,0:T(4,128)S(1)} async-done(((f32[32,7,4,128]{3,2,1,0:T(4,128)}), f32[32,7,4,128]{3,2,1,0:T(4,128)S(1)}, u32[]{:S(2)}, u32[]{:S(2)}) %all-to-all-start) | async-done | bytes 458784 | tf_op jit(solution)/shard_map/all_to_all | solution.py:114
  26.5 2.7 fusion
  29.3 2.6 copy.135.table_ref
  32.8 0.8 pad.48.x_ref
  33.7 5.7 %shard_map.86 = f32[16,8,8,128]{3,2,1,0:T(8,128)} custom-call(f32[16,8,8,128]{3,2,1,0:T(8,128)} %pad.48.x_ref, f32[16,3,128,128]{3,2,1,0:T(8,128)} %copy.135.table_ref, s32[8,128]{1,0:T(8,128)} %add_select_fusion.onehot_ref, f32[5]{0:T(128)} %broadcast_divide_fusion.w_ref), custom_call_target="tpu_custom_call" | custom-call | tf_op jit(solution)/shard_map/pallas_call | solution.py:93
  39.4 1.3 copy.136
  40.9 14.5 %all_to_all.50 = f32[32,5,4,128]{3,2,1,0:T(4,128)S(1)} all-to-all(f32[32,5,4,128]{3,2,1,0:T(4,128)S(1)} %copy.137), channel_id=1, replica_groups=mesh['lon'=8,'lat'=4] {'lon','lat'}, dimensions={0} | all-to-all | bytes 655360 | tf_op jit(solution)/shard_map/all_to_all | solution.py:114
  56.7 14.1 %all_to_all.51 = f32[32,5,4,128]{3,2,1,0:T(4,128)S(1)} all-to-all(f32[32,5,4,128]{3,2,1,0:T(4,128)S(1)} %bitcast.188), channel_id=1, replica_groups=mesh['lon'=8,'lat'=4] {'lon','lat'}, dimensions={0} | all-to-all | bytes 655360 | tf_op jit(solution)/shard_map/all_to_all | solution.py:114
  71.0 0.8 pad.50.x_ref
  71.9 5.5 %shard_map.87 = f32[16,8,8,128]{3,2,1,0:T(8,128)} custom-call(f32[16,8,8,128]{3,2,1,0:T(8,128)} %pad.50.x_ref, f32[16,3,128,128]{3,2,1,0:T(8,128)} %copy.135.table_ref, s32[8,128]{1,0:T(8,128)} %add_select_fusion.onehot_ref, f32[5]{0:T(128)} %broadcast_divide_fusion.w_ref), custom_call_target="tpu_custom_call" | custom-call | tf_op jit(solution)/shard_map/pallas_call | solution.py:93
  77.4 2.0 pad_add_fusion.x_ref
  79.3 5.7 %shard_map.88 = f32[16,8,8,128]{3,2,1,0:T(8,128)} custom-call(f32[16,8,8,128]{3,2,1,0:T(8,128)} %pad_add_fusion.x_ref, f32[16,3,128,128]{3,2,1,0:T(8,128)} %copy.135.table_ref, s32[8,128]{1,0:T(8,128)} %add_select_fusion.onehot_ref, f32[5]{0:T(128)} %broadcast_divide_fusion.w_ref), custom_call_target="tpu_custom_call" | custom-call | tf_op jit(solution)/shard_map/pallas_call | solution.py:93
  85.1 1.3 copy.146
  87.0 20.6 %all_to_all.52 = f32[32,10,4,128]{3,2,1,0:T(4,128)S(1)} all-to-all(f32[32,10,4,128]{3,2,1,0:T(4,128)S(1)} %copy.148), channel_id=1, replica_groups=mesh['lon'=8,'lat'=4] {'lon','lat'}, dimensions={0} | all-to-all | bytes 1310720 | tf_op jit(solution)/shard_map/all_to_all | solution.py:114
  109.0 14.5 %all_to_all.53 = f32[32,5,4,128]{3,2,1,0:T(4,128)S(1)} all-to-all(f32[32,5,4,128]{3,2,1,0:T(4,128)S(1)} %bitcast.190), channel_id=1, replica_groups=mesh['lon'=8,'lat'=4] {'lon','lat'}, dimensions={0} | all-to-all | bytes 655360 | tf_op jit(solution)/shard_map/all_to_all | solution.py:114
  123.8 0.8 pad.52.x_ref
  124.6 5.5 %shard_map.89 = f32[16,8,8,128]{3,2,1,0:T(8,128)} custom-call(f32[16,8,8,128]{3,2,1,0:T(8,128)} %pad.52.x_ref, f32[16,3,128,128]{3,2,1,0:T(8,128)} %copy.135.table_ref, s32[8,128]{1,0:T(8,128)} %add_select_fusion.onehot_ref, f32[5]{0:T(128)} %broadcast_divide_fusion.w_ref), custom_call_target="tpu_custom_call" | custom-call | tf_op jit(solution)/shard_map/pallas_call | solution.py:93
  130.1 2.7 multiply_reduce_fusion.7
  132.8 5.7 %shard_map.90 = f32[16,8,8,128]{3,2,1,0:T(8,128)} custom-call(f32[16,8,8,128]{3,2,1,0:T(8,128)} %get-tuple-element.65.x_ref, f32[16,3,128,128]{3,2,1,0:T(8,128)} %copy.135.table_ref, s32[8,128]{1,0:T(8,128)} %add_select_fusion.onehot_ref, f32[5]{0:T(128)} %broadcast_divide_fusion.w_ref), custom_call_target="tpu_custom_call" | custom-call | tf_op jit(solution)/shard_map/pallas_call | solution.py:93
  138.6 1.3 copy.158
  140.0 2.6 fusion.31
  143.1 22.0 %all_to_all.54 = f32[32,11,4,128]{3,2,1,0:T(4,128)S(1)} all-to-all(f32[32,11,4,128]{3,2,1,0:T(4,128)S(1)} %copy.159), channel_id=1, replica_groups=mesh['lon'=8,'lat'=4] {'lon','lat'}, dimensions={0} | all-to-all | bytes 1441792 | tf_op jit(solution)/shard_map/all_to_all | solution.py:114
  165.2 0.7 fusion.38
  174.8 14.5 %all_to_all.55 = f32[32,5,4,128]{3,2,1,0:T(4,128)S(1)} all-to-all(f32[32,5,4,128]{3,2,1,0:T(4,128)S(1)} %bitcast.192), channel_id=1, replica_groups=mesh['lon'=8,'lat'=4] {'lon','lat'}, dimensions={0} | all-to-all | bytes 655360 | tf_op jit(solution)/shard_map/all_to_all | solution.py:114
  189.5 0.8 pad.54.x_ref
  190.4 5.5 %shard_map.91 = f32[16,8,8,128]{3,2,1,0:T(8,128)} custom-call(f32[16,8,8,128]{3,2,1,0:T(8,128)} %pad.54.x_ref, f32[16,3,128,128]{3,2,1,0:T(8,128)} %copy.135.table_ref, s32[8,128]{1,0:T(8,128)} %add_select_fusion.onehot_ref, f32[5]{0:T(128)} %broadcast_divide_fusion.w_ref), custom_call_target="tpu_custom_call" | custom-call | tf_op jit(solution)/shard_map/pallas_call | solution.py:93
  195.9 2.1 fusion.33
  197.9 5.7 %shard_map.92 = f32[16,8,8,128]{3,2,1,0:T(8,128)} custom-call(f32[16,8,8,128]{3,2,1,0:T(8,128)} %get-tuple-element.63.x_ref, f32[16,3,128,128]{3,2,1,0:T(8,128)} %copy.135.table_ref, s32[8,128]{1,0:T(8,128)} %add_select_fusion.onehot_ref, f32[5]{0:T(128)} %broadcast_divide_fusion.w_ref), custom_call_target="tpu_custom_call" | custom-call | tf_op jit(solution)/shard_map/pallas_call | solution.py:93
  203.7 1.3 copy.170
  205.6 20.6 %all_to_all.56 = f32[32,10,4,128]{3,2,1,0:T(4,128)S(1)} all-to-all(f32[32,10,4,128]{3,2,1,0:T(4,128)S(1)} %copy.172), channel_id=1, replica_groups=mesh['lon'=8,'lat'=4] {'lon','lat'}, dimensions={0} | all-to-all | bytes 1310720 | tf_op jit(solution)/shard_map/all_to_all | solution.py:114
  227.6 14.5 %all_to_all.57 = f32[32,5,4,128]{3,2,1,0:T(4,128)S(1)} all-to-all(f32[32,5,4,128]{3,2,1,0:T(4,128)S(1)} %bitcast.194), channel_id=1, replica_groups=mesh['lon'=8,'lat'=4] {'lon','lat'}, dimensions={0} | all-to-all | bytes 655360 | tf_op jit(solution)/shard_map/all_to_all | solution.py:114
  242.4 0.9 pad.56.x_ref
  243.2 5.5 %shard_map.93 = f32[16,8,8,128]{3,2,1,0:T(8,128)} custom-call(f32[16,8,8,128]{3,2,1,0:T(8,128)} %pad.56.x_ref, f32[16,3,128,128]{3,2,1,0:T(8,128)} %copy.135.table_ref, s32[8,128]{1,0:T(8,128)} %add_select_fusion.onehot_ref, f32[5]{0:T(128)} %broadcast_divide_fusion.w_ref), custom_call_target="tpu_custom_call" | custom-call | tf_op jit(solution)/shard_map/pallas_call | solution.py:93
  248.7 1.9 multiply_reduce_fusion.3
  250.8 2.6 fusion.30
  253.5 1.0 copy.181
  254.5 2.7 all-to-all-start.9
  257.3 12.7 %all-to-all-done.9 = f32[32,6,4,128]{3,2,1,0:T(4,128)S(1)} async-done(((f32[32,6,4,128]{3,2,1,0:T(4,128)}), f32[32,6,4,128]{3,2,1,0:T(4,128)S(1)}, u32[]{:S(2)}, u32[]{:S(2)}) %all-to-all-start.9) | async-done | bytes 393248 | tf_op jit(solution)/shard_map/all_to_all | solution.py:114
  270.0 0.7 fusion.37
  278.8 0.8 copy.186
  279.6 0.8 copy.187
  (83 shorter events, 11.5 us)
Async XLA Ops:
  0.6 54.8 %copy-start = (f32[137,137]{1,0:T(8,128)S(1)}, f32[137,137]{1,0:T(8,128)}, u32[]{:S(2)}) copy-start(f32[137,137]{1,0:T(8,128)} %param.21) | copy-start | bytes 225232
  5.5 21.0 %all-to-all-start = ((f32[32,7,4,128]{3,2,1,0:T(4,128)}), f32[32,7,4,128]{3,2,1,0:T(4,128)S(1)}, u32[]{:S(2)}, u32[]{:S(2)}) async-start(f32[32,7,4,128]{3,2,1,0:T(4,128)} %pad_maximum_fusion.3), calls=%async_computation | async-start | bytes 917504 | tf_op jit(solution)/shard_map/all_to_all | solution.py:114
  33.7 21.8 %copy-start.4 = (f32[137,4,128]{2,1,0:T(4,128)S(1)}, f32[137,4,128]{2,1,0:T(4,128)}, u32[]{:S(2)}) copy-start(f32[137,4,128]{2,1,0:T(4,128)} %param.16) | copy-start | bytes 841732
  79.3 7.0 %copy-start.1 = (f32[16,8,8,128]{3,2,1,0:T(8,128)S(1)}, f32[16,8,8,128]{3,2,1,0:T(8,128)}, u32[]{:S(2)}) copy-start(f32[16,8,8,128]{3,2,1,0:T(8,128)} %pad_add_fusion.x_ref) | copy-start | bytes 1572868
  132.8 7.0 %copy-start.2 = (f32[16,8,8,128]{3,2,1,0:T(8,128)S(1)}, f32[16,8,8,128]{3,2,1,0:T(8,128)}, u32[]{:S(2)}) copy-start(f32[16,8,8,128]{3,2,1,0:T(8,128)} %get-tuple-element.65.x_ref) | copy-start | bytes 1572868
  197.9 7.0 %copy-start.3 = (f32[16,8,8,128]{3,2,1,0:T(8,128)S(1)}, f32[16,8,8,128]{3,2,1,0:T(8,128)}, u32[]{:S(2)}) copy-start(f32[16,8,8,128]{3,2,1,0:T(8,128)} %get-tuple-element.63.x_ref) | copy-start | bytes 1572868
  250.6 28.0 %copy-start.5 = (f32[137,4,128]{2,1,0:T(4,128)S(1)}, f32[137,4,128]{2,1,0:T(4,128)}, u32[]{:S(2)}) copy-start(f32[137,4,128]{2,1,0:T(4,128)} %param.15) | copy-start | bytes 841732
  254.5 15.5 %all-to-all-start.9 = ((f32[32,6,4,128]{3,2,1,0:T(4,128)}), f32[32,6,4,128]{3,2,1,0:T(4,128)S(1)}, u32[]{:S(2)}, u32[]{:S(2)}) async-start(f32[32,6,4,128]{3,2,1,0:T(4,128)} %copy.181), calls=%async_computation.9 | async-start | bytes 786432 | tf_op jit(solution)/shard_map/all_to_all | solution.py:114
where the time goes:
time: 282 us; the launch traced here: 280 us
  blocking collectives  135 us (48%)
  Pallas kernels  44.9 us (16%)
  local copies, waits for them, and re-layouts  22.5 us (8%)
  waiting for transfers between devices  22 us (8%)
  other arithmetic  20.4 us (7%)
  between operations  18.5 us (7%)
  starting transfers between devices  9.84 us (3%)
  matrix products  6.94 us (2%)
    all_to_all x8, blocking collectives, exchange(): return lax.all_to_all(parts, AXES, 0, 0, tiled=True)  135 us
    pallas_call x8, Pallas kernels, level_apply(): pl.pallas_call(functools.partial(_kernel, order, depth), out_shape=jax.Sh...  44.9 us
    all_to_all x2, waiting for transfers between devices, exchange(): return lax.all_to_all(parts, AXES, 0, 0, tiled=True)  22 us
    all_to_all x2, starting transfers between devices, exchange(): return lax.all_to_all(parts, AXES, 0, 0, tiled=True)  9.84 us
    reshape x8, local copies, waits for them, and re-layouts, level_parts(): v[:, :, :per].reshape(n_lat, rows, n_lon, per, cols)  5.87 us
  transfers between devices with their start and end apart: 2, of which 2 were waited for; matrix products, arithmetic and copies ran while one was open for 1% of the time, Pallas kernels for 0%

commit v1 on v0

--- a/solution.py
+++ b/solution.py
@@ -35,69 +35,105 @@
     distance = jnp.abs(positions[:, None] - block - columns[None, :])
     selector = (distance[:, :, None] == tap_ids[None, None, :]).astype(jnp.float32)
     table = jnp.einsum("pct,jt->jpc", selector, weights, precision=HI)
-    return table.reshape(weights.shape[0], 3, block, block)
+    table = table.reshape(weights.shape[0], 3, block, block)
+    half = block // 2
+    outer = jnp.concatenate([table[:, 2, :half], table[:, 0, half:]], axis=1)
+    return jnp.stack([table[:, 1], outer], axis=1)
 
 
 def mirror_tables(mirror_all, block):
     return (mirror_all % block).reshape(mirror_all.shape[0] // block, block)
 
 
-def _zonal_rows(src, dst, table_ref, nb):
-    rows, _, lp, block = src.shape
+def _dot(a, b):
+    return jnp.dot(a, b, preferred_element_type=jnp.float32, precision=KERNEL_PRECISION)
+
+
+def _zonal_rows(src, dst, table_ref, add=None):
+    rows, nb, lp, block = src.shape
+    lane = lax.broadcasted_iota(jnp.int32, (nb * lp, block), 1)
     for j in range(rows):
         mid = src[j]
         prev = jnp.concatenate([mid[nb - 1 :], mid[: nb - 1]], axis=0) if nb > 1 else mid
         nxt = jnp.concatenate([mid[1:], mid[:1]], axis=0) if nb > 1 else mid
-        acc = jnp.dot(prev.reshape(nb * lp, block), table_ref[j, 0], preferred_element_type=jnp.float32, precision=KERNEL_PRECISION)
-        acc = acc + jnp.dot(mid.reshape(nb * lp, block), table_ref[j, 1], preferred_element_type=jnp.float32, precision=KERNEL_PRECISION)
-        acc = acc + jnp.dot(nxt.reshape(nb * lp, block), table_ref[j, 2], preferred_element_type=jnp.float32, precision=KERNEL_PRECISION)
-        dst[j] = acc.reshape(nb, lp, block)
-
-def _merid_rows(src, dst, mir, onehot_ref, w_ref, nb, depth):
-    rows, _, lp, block = src.shape
+        outer = jnp.where(
+            lane >= block // 2, prev.reshape(nb * lp, block), nxt.reshape(nb * lp, block)
+        )
+        acc = _dot(mid.reshape(nb * lp, block), table_ref[j, 0]) + _dot(outer, table_ref[j, 1])
+        acc = acc.reshape(nb, lp, block)
+        if add is not None:
+            acc = acc + add[j]
+        dst[j] = acc
+
+
+def _merid_rows(src, dst, mir, index_ref, w_ref, depth):
+    rows, nb, lp, block = src.shape
     half = nb // 2
+
     def mirror_block(b, carry):
         sb = lax.rem(b + half, nb)
-        polar = jnp.concatenate([src[pl.ds(0, depth), pl.ds(sb, 1)], src[pl.ds(rows - depth, depth), pl.ds(sb, 1)]], axis=0)
+        polar = jnp.concatenate(
+            [src[pl.ds(0, depth), pl.ds(sb, 1)], src[pl.ds(rows - depth, depth), pl.ds(sb, 1)]],
+            axis=0,
+        )
         source = lax.broadcasted_iota(jnp.int32, (block, block), 0)
-        onehot = (source == onehot_ref[pl.ds(b, 1), :]).astype(jnp.float32)
-        out = jnp.dot(polar.reshape(2 * depth * lp, block), onehot, preferred_element_type=jnp.float32, precision=KERNEL_PRECISION)
+        onehot = (source == index_ref[pl.ds(b, 1), :]).astype(jnp.float32)
+        out = _dot(polar.reshape(2 * depth * lp, block), onehot)
         mir[:, pl.ds(b, 1)] = out.reshape(2 * depth, 1, lp, block)
         return carry
+
     lax.fori_loop(0, nb, mirror_block, 0)
+
     def row(k):
         if k < 0:
             return mir[-1 - k]
         if k >= rows:
             return mir[depth + (rows - 1 - (k - rows)) - (rows - depth)]
         return src[k]
+
     for j in range(rows):
         acc = w_ref[0] * src[j]
         for o in range(1, depth + 1):
             acc = acc + w_ref[o] * (row(j - o) + row(j + o))
         dst[j] = acc
 
-def _kernel(order, depth, x_ref, table_ref, onehot_ref, w_ref, o_ref, tmp, mir):
-    nb = x_ref.shape[1]
-    if order == "zm":
-        _zonal_rows(x_ref, tmp, table_ref, nb)
-        _merid_rows(tmp, o_ref, mir, onehot_ref, w_ref, nb, depth)
+
+def _kernel(mode, depth, *refs):
+    if mode == "p":
+        x_ref, table_ref, index_ref, w_ref, p_ref, tmp, mir = refs
+        _zonal_rows(x_ref, tmp, table_ref)
+        _merid_rows(tmp, p_ref, mir, index_ref, w_ref, depth)
+        return
+    a_ref, x_ref, table_ref, index_ref, w_ref = refs[:5]
+    if mode == "q":
+        f_ref, tmp, mir = refs[5:]
     else:
-        _merid_rows(x_ref, tmp, mir, onehot_ref, w_ref, nb, depth)
-        _zonal_rows(tmp, o_ref, table_ref, nb)
-
-def level_apply(order, x, table, onehot, merid_w):
-    rows, nb, lp, block = x.shape
+        f_ref, p_ref, tmp, mir = refs[5:]
+    _merid_rows(a_ref, tmp, mir, index_ref, w_ref, depth)
+    _zonal_rows(tmp, f_ref, table_ref, add=x_ref)
+    if mode == "qp":
+        _zonal_rows(f_ref, tmp, table_ref)
+        _merid_rows(tmp, p_ref, mir, index_ref, w_ref, depth)
+
+
+def level_apply(mode, fields, table, index, merid_w):
+    shape = fields[0].shape
+    rows, nb, lp, block = shape
     depth = merid_w.shape[0] - 1
-    vmem = pltpu.MemorySpace.VMEM
-    return pl.pallas_call(
-        functools.partial(_kernel, order, depth),
-        out_shape=jax.ShapeDtypeStruct(x.shape, jnp.float32),
-        in_specs=[pl.BlockSpec(memory_space=vmem), pl.BlockSpec(memory_space=vmem), pl.BlockSpec(memory_space=vmem), pl.BlockSpec(memory_space=pltpu.MemorySpace.SMEM)],
-        out_specs=pl.BlockSpec(memory_space=vmem),
-        scratch_shapes=[pltpu.VMEM(x.shape, jnp.float32), pltpu.VMEM((2 * depth, nb, lp, block), jnp.float32)],
+    vmem = pl.BlockSpec(memory_space=pltpu.MemorySpace.VMEM)
+    outs = 2 if mode == "qp" else 1
+    result = pl.pallas_call(
+        functools.partial(_kernel, mode, depth),
+        out_shape=[jax.ShapeDtypeStruct(shape, jnp.float32)] * outs,
+        in_specs=[vmem] * (len(fields) + 2) + [pl.BlockSpec(memory_space=pltpu.MemorySpace.SMEM)],
+        out_specs=[vmem] * outs,
+        scratch_shapes=[
+            pltpu.VMEM(shape, jnp.float32),
+            pltpu.VMEM((2 * depth, nb, lp, block), jnp.float32),
+        ],
         compiler_params=pltpu.CompilerParams(vmem_limit_bytes=60 * 1024 * 1024),
-    )(x, table, onehot, merid_w)
+    )(*fields, table, index, merid_w)
+    return result if outs == 2 else result[0]
 
 
 def per_device(gradient, obs_weight, half_width, zonal_coef, mirror_map, merid_coef, vertical_map):
@@ -162,28 +198,28 @@
     onehot = mirror_tables(mirror_all, cols)
 
     def forward(x):
-        return level_apply("zm", x, table, onehot, merid_w)
-
-    def backward(g):
-        return level_apply("mz", g, table, onehot, merid_w)
+        return level_apply("p", (x,), table, onehot, merid_w)
 
     def middle(y):
         lifted = jnp.einsum("kl,lji->kji", vertical_map, y, precision=HI)
         return jnp.einsum("lk,lji->kji", vertical_map, obs_weight * lifted, precision=HI)
 
-    def image(x, px_col):
-        return x + backward(to_level(exchange(col_parts(middle(px_col)))))
+    def image(x, px_col, mode):
+        return level_apply(mode, (to_level(exchange(col_parts(middle(px_col)))), x), table, onehot, merid_w)
 
     res_col = gradient
     inc_col = jnp.zeros_like(gradient)
     pres_col = to_column(exchange(level_parts(forward(residual))))
     for outer in range(OUTER):
         last = outer == OUTER - 1
-        first = image(residual, pres_col)
-        got = exchange(jnp.concatenate([level_parts(forward(first)), level_parts(first)], axis=1))
+        first, pfirst = image(residual, pres_col, "qp")
+        got = exchange(jnp.concatenate([level_parts(pfirst), level_parts(first)], axis=1))
         pfirst_col = to_column(got[:, :per])
         first_col = to_column(got[:, per:])
-        second = image(first, pfirst_col)
+        if last:
+            second = image(first, pfirst_col, "q")
+        else:
+            second, psecond = image(first, pfirst_col, "qp")
         sums = jnp.stack(
             [
                 jnp.sum(residual * residual),
@@ -194,7 +230,7 @@
         )
         parts = [level_parts(second)]
         if not last:
-            parts.append(level_parts(forward(second)))
+            parts.append(level_parts(psecond))
         got = exchange(jnp.concatenate(parts + [slab(sums)], axis=1))
         second_col = to_column(got[:, :per])
         total = jnp.sum(got[:, len(parts) * per, 0, : sums.shape[0]], axis=0)

time: 282 us -> 268 us (0.950)
  blocking collectives: 135 us -> 121 us
  waiting for transfers between devices: 22 us -> 35.2 us
  Pallas kernels: 44.9 us -> 32.3 us
  other arithmetic: 20.4 us -> 16.8 us
  starting transfers between devices: 9.84 us -> 13 us
    all_to_all x8 -> x7, blocking collectives: 135 us -> 121 us  [exchange(): return lax.all_to_all(parts, AXES, 0, 0, tiled=True)]
    all_to_all x2 -> x3, waiting for transfers between devices: 22 us -> 35.2 us  [exchange(): return lax.all_to_all(parts, AXES, 0, 0, tiled=True)]
    pallas_call x8 -> x5, Pallas kernels: 44.9 us -> 32.3 us  [level_apply(): pl.pallas_call(functools.partial(_kernel, mode, depth), out_shape=[jax.Sh...]
    add x2 -> x0, other arithmetic: 4.01 us -> none  [image(): return x + backward(to_level(exchange(col_parts(middle(px_col)))))]
    reshape x8, local copies, waits for them, and re-layouts: 5.87 us -> 9.04 us  [level_parts(): v[:, :, :per].reshape(n_lat, rows, n_lon, per, cols)]
    all_to_all x2 -> x3, starting transfers between devices: 9.84 us -> 13 us  [exchange(): return lax.all_to_all(parts, AXES, 0, 0, tiled=True)]
  transfers between devices with their start and end apart: 2 -> 3, of which waited for: 2 -> 3; matrix products, arithmetic and copies ran while one was open for 1% -> 1% of each run, Pallas kernels for 0% -> 0%
where the time goes in v1:
time: 268 us; the launch traced here: 267 us
  blocking collectives  121 us (45%)
  waiting for transfers between devices  35.2 us (13%)
  Pallas kernels  32.3 us (12%)
  local copies, waits for them, and re-layouts  24.5 us (9%)
  between operations  17.2 us (6%)
  other arithmetic  16.8 us (6%)
  starting transfers between devices  13 us (5%)
  matrix products  6.96 us (3%)
    all_to_all x7, blocking collectives, exchange(): return lax.all_to_all(parts, AXES, 0, 0, tiled=True)  121 us
    all_to_all x3, waiting for transfers between devices, exchange(): return lax.all_to_all(parts, AXES, 0, 0, tiled=True)  35.2 us
    pallas_call x5, Pallas kernels, level_apply(): pl.pallas_call(functools.partial(_kernel, mode, depth), out_shape=[jax.Sh...  32.3 us
    all_to_all x3, starting transfers between devices, exchange(): return lax.all_to_all(parts, AXES, 0, 0, tiled=True)  13 us
    reshape x8, local copies, waits for them, and re-layouts, level_parts(): v[:, :, :per].reshape(n_lat, rows, n_lon, per, cols)  9.04 us
  transfers between devices with their start and end apart: 3, of which 3 were waited for; matrix products, arithmetic and copies ran while one was open for 1% of the time, Pallas kernels for 0%

profile of v1, /device:TPU:1, one launch (start us, length us, event | category | flops | bytes accessed | tf_op | source)
XLA Modules:
  0.0 266.9 jit_solution(605052775757459074)
XLA Ops:
  0.7 0.8 copy.115
  2.2 0.7 divide_bitcast_fusion
  2.9 0.7 convert_bitcast_fusion
  3.6 1.0 pad.47
  4.7 0.9 pad_maximum_fusion.4
  5.5 7.1 %all-to-all-start = ((f32[32,7,4,128]{3,2,1,0:T(4,128)}), f32[32,7,4,128]{3,2,1,0:T(4,128)S(1)}, u32[]{:S(2)}, u32[]{:S(2)}) async-start(f32[32,7,4,128]{3,2,1,0:T(4,128)} %pad_maximum_fusion.4), calls=%async_computation | async-start | bytes 917504 | tf_op jit(solution)/shard_map/all_to_all | solution.py:150
  12.7 0.7 multiply_reduce_fusion.8
  14.7 11.9 %all-to-all-done = f32[32,7,4,128]{3,2,1,0:T(4,128)S(1)} async-done(((f32[32,7,4,128]{3,2,1,0:T(4,128)}), f32[32,7,4,128]{3,2,1,0:T(4,128)S(1)}, u32[]{:S(2)}, u32[]{:S(2)}) %all-to-all-start) | async-done | bytes 458784 | tf_op jit(solution)/shard_map/all_to_all | solution.py:150
  26.6 2.7 %fusion = f32[16,3,128,128]{3,0,2,1:T(8,128)S(1)} fusion(f32[16,33,1,1]{1,0,3,2:T(8,128)S(1)} %bitcast.210, s32[3,128,128]{2,1,0:T(8,128)S(1)} %subtract_abs_fusion), kind=kOutput, calls=%fused_computation.1 | convolution fusion | flops 313049088 | bytes 3344448 | tf_op jit(solution)/shard_map/pct,jt->jpc/dot_general | solution.py:37
  30.7 0.9 pad.48.refs_0_.refs_1_
  32.0 1.5 pad_maximum_fusion.refs_1_.refs_2_
  33.5 5.0 %shard_map.86 = f32[16,8,8,128]{3,2,1,0:T(8,128)} custom-call(f32[16,8,8,128]{3,2,1,0:T(8,128)} %pad.48.refs_0_.refs_1_, f32[16,2,128,128]{3,2,1,0:T(8,128)} %pad_maximum_fusion.refs_1_.refs_2_, s32[8,128]{1,0:T(8,128)} %add_select_fusion.refs_2_.refs_3_, f32[5]{0:T(128)} %broadcast_divide_fusion.refs_3_.refs_4_), custom_call_target="tpu_custom_call" | custom-call | tf_op jit(solution)/shard_map/pallas_call | solution.py:125
  38.5 1.3 copy.123
  40.0 14.5 %all_to_all.50 = f32[32,5,4,128]{3,2,1,0:T(4,128)S(1)} all-to-all(f32[32,5,4,128]{3,2,1,0:T(4,128)S(1)} %copy.124), channel_id=1, replica_groups=mesh['lon'=8,'lat'=4] {'lon','lat'}, dimensions={0} | all-to-all | bytes 655360 | tf_op jit(solution)/shard_map/all_to_all | solution.py:150
  55.8 14.1 %all_to_all.51 = f32[32,5,4,128]{3,2,1,0:T(4,128)S(1)} all-to-all(f32[32,5,4,128]{3,2,1,0:T(4,128)S(1)} %bitcast.190), channel_id=1, replica_groups=mesh['lon'=8,'lat'=4] {'lon','lat'}, dimensions={0} | all-to-all | bytes 655360 | tf_op jit(solution)/shard_map/all_to_all | solution.py:150
  70.1 0.8 pad.50.refs_0_
  71.0 7.4 %shard_map.87 = (f32[16,8,8,128]{3,2,1,0:T(8,128)}, f32[16,8,8,128]{3,2,1,0:T(8,128)}) custom-call(f32[16,8,8,128]{3,2,1,0:T(8,128)} %pad.50.refs_0_, f32[16,8,8,128]{3,2,1,0:T(8,128)} %pad.48.refs_0_.refs_1_, f32[16,2,128,128]{3,2,1,0:T(8,128)} %pad_maximum_fusion.refs_1_.refs_2_, s32[8,128]{1,0:T(8,128)} %add_select_fusion.refs_2_.refs_3_, ...), custom_call_target="tpu_custom_call" | custom-call | tf_op jit(solution)/shard_map/pallas_call | solution.py:125
  78.4 1.3 copy.132
  79.6 1.3 copy.131
  81.4 20.6 %all_to_all.52 = f32[32,10,4,128]{3,2,1,0:T(4,128)S(1)} all-to-all(f32[32,10,4,128]{3,2,1,0:T(4,128)S(1)} %copy.133), channel_id=1, replica_groups=mesh['lon'=8,'lat'=4] {'lon','lat'}, dimensions={0} | all-to-all | bytes 1310720 | tf_op jit(solution)/shard_map/all_to_all | solution.py:150
  103.3 14.5 %all_to_all.53 = f32[32,5,4,128]{3,2,1,0:T(4,128)S(1)} all-to-all(f32[32,5,4,128]{3,2,1,0:T(4,128)S(1)} %bitcast.192), channel_id=1, replica_groups=mesh['lon'=8,'lat'=4] {'lon','lat'}, dimensions={0} | all-to-all | bytes 655360 | tf_op jit(solution)/shard_map/all_to_all | solution.py:150
  118.1 0.9 pad.52.refs_0_
  119.0 7.4 %shard_map.88 = (f32[16,8,8,128]{3,2,1,0:T(8,128)}, f32[16,8,8,128]{3,2,1,0:T(8,128)}) custom-call(f32[16,8,8,128]{3,2,1,0:T(8,128)} %pad.52.refs_0_, f32[16,8,8,128]{3,2,1,0:T(8,128)} %get-tuple-element.57.refs_1_, f32[16,2,128,128]{3,2,1,0:T(8,128)} %pad_maximum_fusion.refs_1_.refs_2_, s32[8,128]{1,0:T(8,128)} %add_select_fusion.refs_2_.refs_3_, ...), custom_call_target="tpu_custom_call" | custom-call | tf_op jit(solution)/shard_map/pallas_call | solution.py:125
  126.3 2.0 multiply_reduce_fusion.7
  128.3 1.3 copy.140
  129.8 2.6 fusion.31
  132.9 22.0 %all_to_all.54 = f32[32,11,4,128]{3,2,1,0:T(4,128)S(1)} all-to-all(f32[32,11,4,128]{3,2,1,0:T(4,128)S(1)} %copy.142), channel_id=1, replica_groups=mesh['lon'=8,'lat'=4] {'lon','lat'}, dimensions={0} | all-to-all | bytes 1441792 | tf_op jit(solution)/shard_map/all_to_all | solution.py:150
  164.4 0.8 pad.53.clone
  165.1 3.2 %all-to-all-start.6 = ((f32[32,5,4,128]{3,2,1,0:T(4,128)}), f32[32,5,4,128]{3,2,1,0:T(4,128)S(1)}, u32[]{:S(2)}, u32[]{:S(2)}) async-start(f32[32,5,4,128]{3,2,1,0:T(4,128)} %bitcast.62), calls=%async_computation.6 | async-start | bytes 655360 | tf_op jit(solution)/shard_map/all_to_all | solution.py:150
  168.3 0.9 multiply_subtract_fusion.refs_1_
  169.2 10.6 %all-to-all-done.6 = f32[32,5,4,128]{3,2,1,0:T(4,128)S(1)} async-done(((f32[32,5,4,128]{3,2,1,0:T(4,128)}), f32[32,5,4,128]{3,2,1,0:T(4,128)S(1)}, u32[]{:S(2)}, u32[]{:S(2)}) %all-to-all-start.6) | async-done | bytes 327712 | tf_op jit(solution)/shard_map/all_to_all | solution.py:150
  180.1 0.8 pad.54.refs_0_
  181.0 7.4 %shard_map.89 = (f32[16,8,8,128]{3,2,1,0:T(8,128)}, f32[16,8,8,128]{3,2,1,0:T(8,128)}) custom-call(f32[16,8,8,128]{3,2,1,0:T(8,128)} %pad.54.refs_0_, f32[16,8,8,128]{3,2,1,0:T(8,128)} %multiply_subtract_fusion.refs_1_, f32[16,2,128,128]{3,2,1,0:T(8,128)} %pad_maximum_fusion.refs_1_.refs_2_, s32[8,128]{1,0:T(8,128)} %add_select_fusion.refs_2_.refs_3_, ...), custom_call_target="tpu_custom_call" | custom-call | tf_op jit(solution)/shard_map/pallas_call | solution.py:125
  188.4 1.3 copy.151
  189.6 1.3 copy.152
  191.4 20.6 %all_to_all.55 = f32[32,10,4,128]{3,2,1,0:T(4,128)S(1)} all-to-all(f32[32,10,4,128]{3,2,1,0:T(4,128)S(1)} %copy.153), channel_id=1, replica_groups=mesh['lon'=8,'lat'=4] {'lon','lat'}, dimensions={0} | all-to-all | bytes 1310720 | tf_op jit(solution)/shard_map/all_to_all | solution.py:150
  213.3 14.5 %all_to_all.56 = f32[32,5,4,128]{3,2,1,0:T(4,128)S(1)} all-to-all(f32[32,5,4,128]{3,2,1,0:T(4,128)S(1)} %bitcast.195), channel_id=1, replica_groups=mesh['lon'=8,'lat'=4] {'lon','lat'}, dimensions={0} | all-to-all | bytes 655360 | tf_op jit(solution)/shard_map/all_to_all | solution.py:150
  228.1 0.9 pad.56.refs_0_
  229.0 5.1 %shard_map.90 = f32[16,8,8,128]{3,2,1,0:T(8,128)} custom-call(f32[16,8,8,128]{3,2,1,0:T(8,128)} %pad.56.refs_0_, f32[16,8,8,128]{3,2,1,0:T(8,128)} %get-tuple-element.61.refs_1_, f32[16,2,128,128]{3,2,1,0:T(8,128)} %pad_maximum_fusion.refs_1_.refs_2_, s32[8,128]{1,0:T(8,128)} %add_select_fusion.refs_2_.refs_3_, f32[5]{0:T(128)} %broadcast_divide_fusion.refs_3_.refs_4_), custom_call_target="tpu_custom_call" | custom-call | tf_op jit(solution)/shard_map/pallas_call | solution.py:125
  234.1 1.9 multiply_reduce_fusion.3
  236.0 1.3 copy.160
  237.3 2.6 fusion.30
  239.9 1.0 copy.161
  240.9 2.7 %all-to-all-start.9 = ((f32[32,6,4,128]{3,2,1,0:T(4,128)}), f32[32,6,4,128]{3,2,1,0:T(4,128)S(1)}, u32[]{:S(2)}, u32[]{:S(2)}) async-start(f32[32,6,4,128]{3,2,1,0:T(4,128)} %copy.161), calls=%async_computation.9 | async-start | bytes 786432 | tf_op jit(solution)/shard_map/all_to_all | solution.py:150
  243.8 12.7 %all-to-all-done.9 = f32[32,6,4,128]{3,2,1,0:T(4,128)S(1)} async-done(((f32[32,6,4,128]{3,2,1,0:T(4,128)}), f32[32,6,4,128]{3,2,1,0:T(4,128)S(1)}, u32[]{:S(2)}, u32[]{:S(2)}) %all-to-all-start.9) | async-done | bytes 393248 | tf_op jit(solution)/shard_map/all_to_all | solution.py:150
  256.5 0.7 fusion.37
  265.2 0.8 copy.166
  266.0 0.8 copy.167
  (91 shorter events, 12.2 us)
Async XLA Ops:
  0.6 53.9 %copy-start = (f32[137,137]{1,0:T(8,128)S(1)}, f32[137,137]{1,0:T(8,128)}, u32[]{:S(2)}) copy-start(f32[137,137]{1,0:T(8,128)} %param.21) | copy-start | bytes 225232
  0.6 12.0 %copy-start.8 = (f32[5]{0:T(128)S(1)}, f32[5]{0:T(128)}, u32[]{:S(2)}) copy-start(f32[5]{0:T(128)} %param.20) | copy-start | bytes 64
  5.5 21.0 %all-to-all-start = ((f32[32,7,4,128]{3,2,1,0:T(4,128)}), f32[32,7,4,128]{3,2,1,0:T(4,128)S(1)}, u32[]{:S(2)}, u32[]{:S(2)}) async-start(f32[32,7,4,128]{3,2,1,0:T(4,128)} %pad_maximum_fusion.4), calls=%async_computation | async-start | bytes 917504 | tf_op jit(solution)/shard_map/all_to_all | solution.py:150
  38.5 16.1 %copy-start.2 = (f32[137,4,128]{2,1,0:T(4,128)S(1)}, f32[137,4,128]{2,1,0:T(4,128)}, u32[]{:S(2)}) copy-start(f32[137,4,128]{2,1,0:T(4,128)} %param.16) | copy-start | bytes 841732
  118.1 8.3 %copy-start.1 = (f32[16,8,8,128]{3,2,1,0:T(8,128)S(1)}, f32[16,8,8,128]{3,2,1,0:T(8,128)}, u32[]{:S(2)}) copy-start(f32[16,8,8,128]{3,2,1,0:T(8,128)} %get-tuple-element.57.refs_1_) | copy-start | bytes 1572868
  126.3 3.2 %copy-start.7 = (f32[16,8,8,128]{3,2,1,0:T(8,128)S(1)}, f32[16,8,8,128]{3,2,1,0:T(8,128)}, u32[]{:S(2)}) copy-start(f32[16,8,8,128]{3,2,1,0:T(8,128)} %get-tuple-element.59) | copy-start | bytes 1572868
  163.1 5.2 %copy-start.4 = (f32[16,8,8,128]{3,2,1,0:T(8,128)S(1)}, f32[16,8,8,128]{3,2,1,0:T(8,128)}, u32[]{:S(2)}) copy-start(f32[16,8,8,128]{3,2,1,0:T(8,128)} %get-tuple-element.58) | copy-start | bytes 1572868
  165.1 14.7 %all-to-all-start.6 = ((f32[32,5,4,128]{3,2,1,0:T(4,128)}), f32[32,5,4,128]{3,2,1,0:T(4,128)S(1)}, u32[]{:S(2)}, u32[]{:S(2)}) async-start(f32[32,5,4,128]{3,2,1,0:T(4,128)} %bitcast.62), calls=%async_computation.6 | async-start | bytes 655360 | tf_op jit(solution)/shard_map/all_to_all | solution.py:150
  229.0 5.1 %copy-start.3 = (f32[16,8,8,128]{3,2,1,0:T(8,128)S(1)}, f32[16,8,8,128]{3,2,1,0:T(8,128)}, u32[]{:S(2)}) copy-start(f32[16,8,8,128]{3,2,1,0:T(8,128)} %get-tuple-element.61.refs_1_) | copy-start | bytes 1572868
  229.0 5.1 %copy-start.5 = (f32[16,8,8,128]{3,2,1,0:T(8,128)S(1)}, f32[16,8,8,128]{3,2,1,0:T(8,128)}, u32[]{:S(2)}) copy-start(f32[16,8,8,128]{3,2,1,0:T(8,128)} %multiply_subtract_fusion.refs_1_) | copy-start | bytes 1572868
  239.9 25.1 %copy-start.6 = (f32[137,4,128]{2,1,0:T(4,128)S(1)}, f32[137,4,128]{2,1,0:T(4,128)}, u32[]{:S(2)}) copy-start(f32[137,4,128]{2,1,0:T(4,128)} %param.15) | copy-start | bytes 841732
  240.9 15.5 %all-to-all-start.9 = ((f32[32,6,4,128]{3,2,1,0:T(4,128)}), f32[32,6,4,128]{3,2,1,0:T(4,128)S(1)}, u32[]{:S(2)}, u32[]{:S(2)}) async-start(f32[32,6,4,128]{3,2,1,0:T(4,128)} %copy.161), calls=%async_computation.9 | async-start | bytes 786432 | tf_op jit(solution)/shard_map/all_to_all | solution.py:150

commit v2 on v1

--- a/solution.py
+++ b/solution.py
@@ -165,9 +165,16 @@
     def to_column(z):
         return z.reshape(n_dev * per, rows, cols)[:lev]
 
+    lanes = cols if rows >= 4 else 1
+
     def slab(values):
-        flat = jnp.zeros((rows * cols,), jnp.float32).at[: values.shape[0]].set(values)
+        flat = jnp.repeat(values, lanes)
+        flat = jnp.zeros((rows * cols,), jnp.float32).at[: flat.shape[0]].set(flat)
         return jnp.broadcast_to(flat.reshape(1, 1, rows, cols), (n_dev, 1, rows, cols))
+
+    def totals(piece):
+        flat = piece.reshape(n_dev, rows * cols)[:, : 4 * lanes].reshape(n_dev, 4, lanes)
+        return jnp.sum(flat, axis=0)
 
     mirror_slab = jnp.zeros((1, 1, rows, cols), jnp.float32).at[0, 0, 0].set(
         mirror_map.astype(jnp.float32)
@@ -233,7 +240,7 @@
             parts.append(level_parts(psecond))
         got = exchange(jnp.concatenate(parts + [slab(sums)], axis=1))
         second_col = to_column(got[:, :per])
-        total = jnp.sum(got[:, len(parts) * per, 0, : sums.shape[0]], axis=0)
+        total = totals(got[:, len(parts) * per])
         sum_rr, sum_rf, sum_ff, sum_fs = total[0], total[1], total[2], total[3]
         determinant = sum_rf * sum_fs - sum_ff * sum_ff
         coef_one = (sum_fs * sum_rr - sum_ff * sum_rf) / determinant

time: 268 us -> 251 us (0.937)
  between operations: 17.2 us -> 1.94 us
    another operation x1 -> x3, other arithmetic: 0.67 us -> 5.84 us  [the longest x2 5.17 us: per_device(): jnp.stack([jnp.sum(residual * residual), jnp.sum(residual * first), jnp.s...]
    broadcast_in_dim x2 -> x0, other arithmetic: 5.17 us -> none  [slab(): jnp.broadcast_to(flat.reshape(1, 1, rows, cols), (n_dev, 1, rows, cols))]
where the time goes in v2:
time: 251 us; the launch traced here: 250 us
  blocking collectives  121 us (48%)
  waiting for transfers between devices  35.2 us (14%)
  Pallas kernels  32.3 us (13%)
  local copies, waits for them, and re-layouts  23.3 us (9%)
  other arithmetic  16.7 us (7%)
  starting transfers between devices  13 us (5%)
  matrix products  6.84 us (3%)
    all_to_all x7, blocking collectives, exchange(): return lax.all_to_all(parts, AXES, 0, 0, tiled=True)  121 us
    all_to_all x3, waiting for transfers between devices, exchange(): return lax.all_to_all(parts, AXES, 0, 0, tiled=True)  35.2 us
    pallas_call x5, Pallas kernels, level_apply(): pl.pallas_call(functools.partial(_kernel, mode, depth), out_shape=[jax.Sh...  32.3 us
    all_to_all x3, starting transfers between devices, exchange(): return lax.all_to_all(parts, AXES, 0, 0, tiled=True)  13 us
    reshape x8, local copies, waits for them, and re-layouts, level_parts(): v[:, :, :per].reshape(n_lat, rows, n_lon, per, cols)  9.04 us
    another operation x2, other arithmetic, per_device(): jnp.stack([jnp.sum(residual * residual), jnp.sum(residual * first), jnp.s...  5.17 us
  transfers between devices with their start and end apart: 3, of which 3 were waited for; matrix products, arithmetic and copies ran while one was open for 1% of the time, Pallas kernels for 0%

profile of v2, /device:TPU:1, one launch (start us, length us, event | category | flops | bytes accessed | tf_op | source)
XLA Modules:
  0.0 250.1 jit_solution(12102668131273650557)
XLA Ops:
  0.7 0.8 copy.115
  1.5 0.7 fusion.27
  2.2 0.7 divide_bitcast_fusion
  2.9 0.7 convert_bitcast_fusion
  3.6 1.0 pad.47
  4.7 0.9 pad_maximum_fusion.4
  5.5 7.1 %all-to-all-start = ((f32[32,7,4,128]{3,2,1,0:T(4,128)}), f32[32,7,4,128]{3,2,1,0:T(4,128)S(1)}, u32[]{:S(2)}, u32[]{:S(2)}) async-start(f32[32,7,4,128]{3,2,1,0:T(4,128)} %pad_maximum_fusion.4), calls=%async_computation | async-start | bytes 917504 | tf_op jit(solution)/shard_map/all_to_all | solution.py:150
  12.7 0.7 multiply_reduce_fusion.8
  14.7 11.9 %all-to-all-done = f32[32,7,4,128]{3,2,1,0:T(4,128)S(1)} async-done(((f32[32,7,4,128]{3,2,1,0:T(4,128)}), f32[32,7,4,128]{3,2,1,0:T(4,128)S(1)}, u32[]{:S(2)}, u32[]{:S(2)}) %all-to-all-start) | async-done | bytes 458784 | tf_op jit(solution)/shard_map/all_to_all | solution.py:150
  26.6 2.6 %fusion = f32[16,3,128,128]{3,0,2,1:T(8,128)S(1)} fusion(f32[16,33,1,1]{1,0,3,2:T(8,128)S(1)} %bitcast.210, s32[3,128,128]{2,1,0:T(8,128)S(1)} %subtract_abs_fusion), kind=kOutput, calls=%fused_computation.1 | convolution fusion | flops 313049088 | bytes 3344448 | tf_op jit(solution)/shard_map/pct,jt->jpc/dot_general | solution.py:37
  30.6 0.8 pad.48.refs_0_.refs_1_
  31.9 1.5 pad_maximum_fusion.refs_1_.refs_2_
  33.4 5.0 %shard_map.96 = f32[16,8,8,128]{3,2,1,0:T(8,128)} custom-call(f32[16,8,8,128]{3,2,1,0:T(8,128)} %pad.48.refs_0_.refs_1_, f32[16,2,128,128]{3,2,1,0:T(8,128)} %pad_maximum_fusion.refs_1_.refs_2_, s32[8,128]{1,0:T(8,128)} %add_select_fusion.refs_2_.refs_3_, f32[5]{0:T(128)} %broadcast_divide_fusion.refs_3_.refs_4_), custom_call_target="tpu_custom_call" | custom-call | tf_op jit(solution)/shard_map/pallas_call | solution.py:125
  38.4 1.3 copy.123
  39.9 14.5 %all_to_all.50 = f32[32,5,4,128]{3,2,1,0:T(4,128)S(1)} all-to-all(f32[32,5,4,128]{3,2,1,0:T(4,128)S(1)} %copy.124), channel_id=1, replica_groups=mesh['lon'=8,'lat'=4] {'lon','lat'}, dimensions={0} | all-to-all | bytes 655360 | tf_op jit(solution)/shard_map/all_to_all | solution.py:150
  55.7 14.1 %all_to_all.51 = f32[32,5,4,128]{3,2,1,0:T(4,128)S(1)} all-to-all(f32[32,5,4,128]{3,2,1,0:T(4,128)S(1)} %bitcast.190), channel_id=1, replica_groups=mesh['lon'=8,'lat'=4] {'lon','lat'}, dimensions={0} | all-to-all | bytes 655360 | tf_op jit(solution)/shard_map/all_to_all | solution.py:150
  70.0 0.8 pad.50.refs_0_
  70.9 7.4 %shard_map.97 = (f32[16,8,8,128]{3,2,1,0:T(8,128)}, f32[16,8,8,128]{3,2,1,0:T(8,128)}) custom-call(f32[16,8,8,128]{3,2,1,0:T(8,128)} %pad.50.refs_0_, f32[16,8,8,128]{3,2,1,0:T(8,128)} %pad.48.refs_0_.refs_1_, f32[16,2,128,128]{3,2,1,0:T(8,128)} %pad_maximum_fusion.refs_1_.refs_2_, s32[8,128]{1,0:T(8,128)} %add_select_fusion.refs_2_.refs_3_, ...), custom_call_target="tpu_custom_call" | custom-call | tf_op jit(solution)/shard_map/pallas_call | solution.py:125
  78.3 1.3 copy.132
  79.5 1.3 copy.131
  81.3 20.6 %all_to_all.52 = f32[32,10,4,128]{3,2,1,0:T(4,128)S(1)} all-to-all(f32[32,10,4,128]{3,2,1,0:T(4,128)S(1)} %copy.133), channel_id=1, replica_groups=mesh['lon'=8,'lat'=4] {'lon','lat'}, dimensions={0} | all-to-all | bytes 1310720 | tf_op jit(solution)/shard_map/all_to_all | solution.py:150
  103.2 14.5 %all_to_all.53 = f32[32,5,4,128]{3,2,1,0:T(4,128)S(1)} all-to-all(f32[32,5,4,128]{3,2,1,0:T(4,128)S(1)} %bitcast.192), channel_id=1, replica_groups=mesh['lon'=8,'lat'=4] {'lon','lat'}, dimensions={0} | all-to-all | bytes 655360 | tf_op jit(solution)/shard_map/all_to_all | solution.py:150
  118.0 0.9 pad.52.refs_0_
  118.8 7.4 %shard_map.98 = (f32[16,8,8,128]{3,2,1,0:T(8,128)}, f32[16,8,8,128]{3,2,1,0:T(8,128)}) custom-call(f32[16,8,8,128]{3,2,1,0:T(8,128)} %pad.52.refs_0_, f32[16,8,8,128]{3,2,1,0:T(8,128)} %get-tuple-element.73.refs_1_, f32[16,2,128,128]{3,2,1,0:T(8,128)} %pad_maximum_fusion.refs_1_.refs_2_, s32[8,128]{1,0:T(8,128)} %add_select_fusion.refs_2_.refs_3_, ...), custom_call_target="tpu_custom_call" | custom-call | tf_op jit(solution)/shard_map/pallas_call | solution.py:125
  126.2 1.9 multiply_reduce_fusion.7
  128.2 1.3 copy.140
  129.7 2.6 %pad_maximum_fusion.6 = f32[4]{0:T(128)S(1)} fusion(f32[1]{0:T(128)} %bitcast.53, f32[1]{0:T(128)} %bitcast.52, f32[1]{0:T(128)} %bitcast.51, f32[1]{0:T(128)} %bitcast.50), kind=kLoop, calls=%fused_computation.73 | loop fusion | flops 12 | bytes 32 | tf_op jit(solution)/shard_map/stack | solution.py:230
  132.8 22.0 %all_to_all.54 = f32[32,11,4,128]{3,2,1,0:T(4,128)S(1)} all-to-all(f32[32,11,4,128]{3,2,1,0:T(4,128)S(1)} %copy.142), channel_id=1, replica_groups=mesh['lon'=8,'lat'=4] {'lon','lat'}, dimensions={0} | all-to-all | bytes 1441792 | tf_op jit(solution)/shard_map/all_to_all | solution.py:150
  156.2 0.8 pad.53.clone
  156.9 3.2 %all-to-all-start.6 = ((f32[32,5,4,128]{3,2,1,0:T(4,128)}), f32[32,5,4,128]{3,2,1,0:T(4,128)S(1)}, u32[]{:S(2)}, u32[]{:S(2)}) async-start(f32[32,5,4,128]{3,2,1,0:T(4,128)} %bitcast.61), calls=%async_computation.6 | async-start | bytes 655360 | tf_op jit(solution)/shard_map/all_to_all | solution.py:150
  160.1 0.9 multiply_subtract_fusion.refs_1_
  161.0 10.6 %all-to-all-done.6 = f32[32,5,4,128]{3,2,1,0:T(4,128)S(1)} async-done(((f32[32,5,4,128]{3,2,1,0:T(4,128)}), f32[32,5,4,128]{3,2,1,0:T(4,128)S(1)}, u32[]{:S(2)}, u32[]{:S(2)}) %all-to-all-start.6) | async-done | bytes 327712 | tf_op jit(solution)/shard_map/all_to_all | solution.py:150
  171.9 0.8 pad.54.refs_0_
  172.8 7.4 %shard_map.99 = (f32[16,8,8,128]{3,2,1,0:T(8,128)}, f32[16,8,8,128]{3,2,1,0:T(8,128)}) custom-call(f32[16,8,8,128]{3,2,1,0:T(8,128)} %pad.54.refs_0_, f32[16,8,8,128]{3,2,1,0:T(8,128)} %multiply_subtract_fusion.refs_1_, f32[16,2,128,128]{3,2,1,0:T(8,128)} %pad_maximum_fusion.refs_1_.refs_2_, s32[8,128]{1,0:T(8,128)} %add_select_fusion.refs_2_.refs_3_, ...), custom_call_target="tpu_custom_call" | custom-call | tf_op jit(solution)/shard_map/pallas_call | solution.py:125
  180.2 1.3 copy.151
  181.4 1.3 copy.152
  183.2 20.6 %all_to_all.55 = f32[32,10,4,128]{3,2,1,0:T(4,128)S(1)} all-to-all(f32[32,10,4,128]{3,2,1,0:T(4,128)S(1)} %copy.153), channel_id=1, replica_groups=mesh['lon'=8,'lat'=4] {'lon','lat'}, dimensions={0} | all-to-all | bytes 1310720 | tf_op jit(solution)/shard_map/all_to_all | solution.py:150
  205.1 14.5 %all_to_all.56 = f32[32,5,4,128]{3,2,1,0:T(4,128)S(1)} all-to-all(f32[32,5,4,128]{3,2,1,0:T(4,128)S(1)} %bitcast.195), channel_id=1, replica_groups=mesh['lon'=8,'lat'=4] {'lon','lat'}, dimensions={0} | all-to-all | bytes 655360 | tf_op jit(solution)/shard_map/all_to_all | solution.py:150
  219.9 0.9 pad.56.refs_0_
  220.7 5.1 %shard_map.100 = f32[16,8,8,128]{3,2,1,0:T(8,128)} custom-call(f32[16,8,8,128]{3,2,1,0:T(8,128)} %pad.56.refs_0_, f32[16,8,8,128]{3,2,1,0:T(8,128)} %get-tuple-element.77.refs_1_, f32[16,2,128,128]{3,2,1,0:T(8,128)} %pad_maximum_fusion.refs_1_.refs_2_, s32[8,128]{1,0:T(8,128)} %add_select_fusion.refs_2_.refs_3_, f32[5]{0:T(128)} %broadcast_divide_fusion.refs_3_.refs_4_), custom_call_target="tpu_custom_call" | custom-call | tf_op jit(solution)/shard_map/pallas_call | solution.py:125
  225.9 1.9 multiply_reduce_fusion.3
  227.7 1.3 copy.160
  229.0 2.6 %pad_maximum_fusion.7 = f32[4]{0:T(128)S(1)} fusion(f32[1]{0:T(128)} %bitcast.85, f32[1]{0:T(128)} %bitcast.84, f32[1]{0:T(128)} %bitcast.83, f32[1]{0:T(128)} %bitcast.82), kind=kLoop, calls=%fused_computation.74 | loop fusion | flops 12 | bytes 32 | tf_op jit(solution)/shard_map/stack | solution.py:230
  231.7 1.0 copy.161
  232.7 2.7 %all-to-all-start.9 = ((f32[32,6,4,128]{3,2,1,0:T(4,128)}), f32[32,6,4,128]{3,2,1,0:T(4,128)S(1)}, u32[]{:S(2)}, u32[]{:S(2)}) async-start(f32[32,6,4,128]{3,2,1,0:T(4,128)} %copy.161), calls=%async_computation.9 | async-start | bytes 786432 | tf_op jit(solution)/shard_map/all_to_all | solution.py:150
  235.6 12.7 %all-to-all-done.9 = f32[32,6,4,128]{3,2,1,0:T(4,128)S(1)} async-done(((f32[32,6,4,128]{3,2,1,0:T(4,128)}), f32[32,6,4,128]{3,2,1,0:T(4,128)S(1)}, u32[]{:S(2)}, u32[]{:S(2)}) %all-to-all-start.9) | async-done | bytes 393248 | tf_op jit(solution)/shard_map/all_to_all | solution.py:150
  248.5 0.8 copy.166
  249.3 0.8 copy.167
  (91 shorter events, 11.0 us)
Async XLA Ops:
  0.6 53.8 %copy-start = (f32[137,137]{1,0:T(8,128)S(1)}, f32[137,137]{1,0:T(8,128)}, u32[]{:S(2)}) copy-start(f32[137,137]{1,0:T(8,128)} %param.25) | copy-start | bytes 225232
  0.6 12.0 %copy-start.8 = (f32[5]{0:T(128)S(1)}, f32[5]{0:T(128)}, u32[]{:S(2)}) copy-start(f32[5]{0:T(128)} %param.24) | copy-start | bytes 64
  5.5 21.0 %all-to-all-start = ((f32[32,7,4,128]{3,2,1,0:T(4,128)}), f32[32,7,4,128]{3,2,1,0:T(4,128)S(1)}, u32[]{:S(2)}, u32[]{:S(2)}) async-start(f32[32,7,4,128]{3,2,1,0:T(4,128)} %pad_maximum_fusion.4), calls=%async_computation | async-start | bytes 917504 | tf_op jit(solution)/shard_map/all_to_all | solution.py:150
  38.4 16.1 %copy-start.2 = (f32[137,4,128]{2,1,0:T(4,128)S(1)}, f32[137,4,128]{2,1,0:T(4,128)}, u32[]{:S(2)}) copy-start(f32[137,4,128]{2,1,0:T(4,128)} %param.20) | copy-start | bytes 841732
  118.0 8.3 %copy-start.1 = (f32[16,8,8,128]{3,2,1,0:T(8,128)S(1)}, f32[16,8,8,128]{3,2,1,0:T(8,128)}, u32[]{:S(2)}) copy-start(f32[16,8,8,128]{3,2,1,0:T(8,128)} %get-tuple-element.73.refs_1_) | copy-start | bytes 1572868
  126.2 3.2 %copy-start.7 = (f32[16,8,8,128]{3,2,1,0:T(8,128)S(1)}, f32[16,8,8,128]{3,2,1,0:T(8,128)}, u32[]{:S(2)}) copy-start(f32[16,8,8,128]{3,2,1,0:T(8,128)} %get-tuple-element.75) | copy-start | bytes 1572868
  154.9 5.2 %copy-start.4 = (f32[16,8,8,128]{3,2,1,0:T(8,128)S(1)}, f32[16,8,8,128]{3,2,1,0:T(8,128)}, u32[]{:S(2)}) copy-start(f32[16,8,8,128]{3,2,1,0:T(8,128)} %get-tuple-element.74) | copy-start | bytes 1572868
  156.9 14.7 %all-to-all-start.6 = ((f32[32,5,4,128]{3,2,1,0:T(4,128)}), f32[32,5,4,128]{3,2,1,0:T(4,128)S(1)}, u32[]{:S(2)}, u32[]{:S(2)}) async-start(f32[32,5,4,128]{3,2,1,0:T(4,128)} %bitcast.61), calls=%async_computation.6 | async-start | bytes 655360 | tf_op jit(solution)/shard_map/all_to_all | solution.py:150
  220.7 5.1 %copy-start.3 = (f32[16,8,8,128]{3,2,1,0:T(8,128)S(1)}, f32[16,8,8,128]{3,2,1,0:T(8,128)}, u32[]{:S(2)}) copy-start(f32[16,8,8,128]{3,2,1,0:T(8,128)} %get-tuple-element.77.refs_1_) | copy-start | bytes 1572868
  220.7 5.1 %copy-start.5 = (f32[16,8,8,128]{3,2,1,0:T(8,128)S(1)}, f32[16,8,8,128]{3,2,1,0:T(8,128)}, u32[]{:S(2)}) copy-start(f32[16,8,8,128]{3,2,1,0:T(8,128)} %multiply_subtract_fusion.refs_1_) | copy-start | bytes 1572868
  231.7 16.6 %copy-start.6 = (f32[137,4,128]{2,1,0:T(4,128)S(1)}, f32[137,4,128]{2,1,0:T(4,128)}, u32[]{:S(2)}) copy-start(f32[137,4,128]{2,1,0:T(4,128)} %param.19) | copy-start | bytes 841732
  232.7 15.5 %all-to-all-start.9 = ((f32[32,6,4,128]{3,2,1,0:T(4,128)}), f32[32,6,4,128]{3,2,1,0:T(4,128)S(1)}, u32[]{:S(2)}, u32[]{:S(2)}) async-start(f32[32,6,4,128]{3,2,1,0:T(4,128)} %copy.161), calls=%async_computation.9 | async-start | bytes 786432 | tf_op jit(solution)/shard_map/all_to_all | solution.py:150

commit v3 on v2

--- a/solution.py
+++ b/solution.py
@@ -98,38 +98,79 @@
         dst[j] = acc
 
 
-def _kernel(mode, depth, *refs):
+def _unpack(parts_ref, dst, n_lat):
+    _, per, rl, _ = parts_ref.shape
+    nb = dst.shape[1]
+
+    def one_block(b, carry):
+        for a in range(n_lat):
+            for lev in range(per):
+                tile = parts_ref[b * n_lat + a, lev]
+                for r in range(rl):
+                    dst[a * rl + r, pl.ds(b, 1), pl.ds(lev, 1), :] = tile[r : r + 1].reshape(1, 1, -1)
+        return carry
+
+    lax.fori_loop(0, nb, one_block, 0)
+
+
+def _pack(src, parts_ref, n_lat):
+    _, per, rl, _ = parts_ref.shape
+    nb = src.shape[1]
+
+    def one_block(b, carry):
+        for a in range(n_lat):
+            for lev in range(per):
+                tile = jnp.concatenate(
+                    [src[a * rl + r, pl.ds(b, 1), pl.ds(lev, 1), :].reshape(1, -1) for r in range(rl)],
+                    axis=0,
+                )
+                parts_ref[b * n_lat + a, lev] = tile
+        return carry
+
+    lax.fori_loop(0, nb, one_block, 0)
+
+
+def _kernel(mode, depth, n_lat, *refs):
     if mode == "p":
-        x_ref, table_ref, index_ref, w_ref, p_ref, tmp, mir = refs
-        _zonal_rows(x_ref, tmp, table_ref)
-        _merid_rows(tmp, p_ref, mir, index_ref, w_ref, depth)
+        x_ref, table_ref, index_ref, w_ref, p_ref, u, v, mir = refs
+        _unpack(x_ref, u, n_lat)
+        _zonal_rows(u, v, table_ref)
+        _merid_rows(v, u, mir, index_ref, w_ref, depth)
+        _pack(u, p_ref, n_lat)
         return
     a_ref, x_ref, table_ref, index_ref, w_ref = refs[:5]
     if mode == "q":
-        f_ref, tmp, mir = refs[5:]
+        f_ref, u, v, mir = refs[5:]
     else:
-        f_ref, p_ref, tmp, mir = refs[5:]
-    _merid_rows(a_ref, tmp, mir, index_ref, w_ref, depth)
-    _zonal_rows(tmp, f_ref, table_ref, add=x_ref)
+        f_ref, p_ref, u, v, mir = refs[5:]
+    _unpack(a_ref, u, n_lat)
+    _merid_rows(u, v, mir, index_ref, w_ref, depth)
+    _unpack(x_ref, u, n_lat)
+    _zonal_rows(v, v, table_ref, add=u)
+    _pack(v, f_ref, n_lat)
     if mode == "qp":
-        _zonal_rows(f_ref, tmp, table_ref)
-        _merid_rows(tmp, p_ref, mir, index_ref, w_ref, depth)
-
-
-def level_apply(mode, fields, table, index, merid_w):
+        _zonal_rows(v, u, table_ref)
+        _merid_rows(u, v, mir, index_ref, w_ref, depth)
+        _pack(v, p_ref, n_lat)
+
+
+def level_apply(mode, fields, table, index, merid_w, n_lat, padded):
     shape = fields[0].shape
-    rows, nb, lp, block = shape
+    n_dev, per, rl, block = shape
+    nb = n_dev // n_lat
+    level_shape = (n_lat * rl, nb, padded, block)
     depth = merid_w.shape[0] - 1
     vmem = pl.BlockSpec(memory_space=pltpu.MemorySpace.VMEM)
     outs = 2 if mode == "qp" else 1
     result = pl.pallas_call(
-        functools.partial(_kernel, mode, depth),
+        functools.partial(_kernel, mode, depth, n_lat),
         out_shape=[jax.ShapeDtypeStruct(shape, jnp.float32)] * outs,
         in_specs=[vmem] * (len(fields) + 2) + [pl.BlockSpec(memory_space=pltpu.MemorySpace.SMEM)],
         out_specs=[vmem] * outs,
         scratch_shapes=[
-            pltpu.VMEM(shape, jnp.float32),
-            pltpu.VMEM((2 * depth, nb, lp, block), jnp.float32),
+            pltpu.VMEM(level_shape, jnp.float32),
+            pltpu.VMEM(level_shape, jnp.float32),
+            pltpu.VMEM((2 * depth, nb, padded, block), jnp.float32),
         ],
         compiler_params=pltpu.CompilerParams(vmem_limit_bytes=60 * 1024 * 1024),
     )(*fields, table, index, merid_w)
@@ -153,15 +194,6 @@
         x = jnp.pad(x, ((0, n_dev * per - lev), (0, 0), (0, 0)))
         return x.reshape(n_dev, per, rows, cols)
 
-    def to_level(z):
-        z = z.reshape(n_lon, n_lat, per, rows, cols).transpose(1, 3, 0, 2, 4)
-        z = z.reshape(n_lat * rows, n_lon, per, cols)
-        return jnp.pad(z, ((0, 0), (0, 0), (0, padded - per), (0, 0)))
-
-    def level_parts(v):
-        v = v[:, :, :per].reshape(n_lat, rows, n_lon, per, cols).transpose(2, 0, 3, 1, 4)
-        return v.reshape(n_dev, per, rows, cols)
-
     def to_column(z):
         return z.reshape(n_dev * per, rows, cols)[:lev]
 
@@ -192,7 +224,7 @@
             axis=1,
         )
     )
-    residual = to_level(got[:, :per])
+    residual = got[:, :per]
     mirror_all = (
         got[:, per, 0, :].reshape(n_lon, n_lat, cols)[:, 0].reshape(n_lon * cols).astype(jnp.int32)
     )
@@ -205,22 +237,24 @@
     onehot = mirror_tables(mirror_all, cols)
 
     def forward(x):
-        return level_apply("p", (x,), table, onehot, merid_w)
+        return level_apply("p", (x,), table, onehot, merid_w, n_lat, padded)
 
     def middle(y):
         lifted = jnp.einsum("kl,lji->kji", vertical_map, y, precision=HI)
         return jnp.einsum("lk,lji->kji", vertical_map, obs_weight * lifted, precision=HI)
 
     def image(x, px_col, mode):
-        return level_apply(mode, (to_level(exchange(col_parts(middle(px_col)))), x), table, onehot, merid_w)
+        return level_apply(
+            mode, (exchange(col_parts(middle(px_col))), x), table, onehot, merid_w, n_lat, padded
+        )
 
     res_col = gradient
     inc_col = jnp.zeros_like(gradient)
-    pres_col = to_column(exchange(level_parts(forward(residual))))
+    pres_col = to_column(exchange(forward(residual)))
     for outer in range(OUTER):
         last = outer == OUTER - 1
         first, pfirst = image(residual, pres_col, "qp")
-        got = exchange(jnp.concatenate([level_parts(pfirst), level_parts(first)], axis=1))
+        got = exchange(jnp.concatenate([pfirst, first], axis=1))
         pfirst_col = to_column(got[:, :per])
         first_col = to_column(got[:, per:])
         if last:
@@ -235,9 +269,9 @@
                 jnp.sum(first * second),
             ]
         )
-        parts = [level_parts(second)]
+        parts = [(second)]
         if not last:
-            parts.append(level_parts(psecond))
+            parts.append((psecond))
         got = exchange(jnp.concatenate(parts + [slab(sums)], axis=1))
         second_col = to_column(got[:, :per])
         total = totals(got[:, len(parts) * per])

time: 251 us -> 244 us (0.972)
  local copies, waits for them, and re-layouts: 23.3 us -> 6.1 us
  blocking collectives: 121 us -> 137 us
  waiting for transfers between devices: 35.2 us -> 22.5 us
  other arithmetic: 16.7 us -> 23 us
  Pallas kernels: 32.3 us -> 36.2 us
  starting transfers between devices: 13 us -> 10.2 us
    all_to_all x7 -> x8, blocking collectives: 121 us -> 137 us  [exchange(): return lax.all_to_all(parts, AXES, 0, 0, tiled=True)]
    all_to_all x3 -> x2, waiting for transfers between devices: 35.2 us -> 22.5 us  [exchange(): return lax.all_to_all(parts, AXES, 0, 0, tiled=True)]
    reshape x9 -> x0, local copies, waits for them, and re-layouts: 9.26 us -> none  [the longest x8 9.04 us: level_parts(): v[:, :, :per].reshape(n_lat, rows, n_lon, per, cols)]
    pad x5 -> x0, local copies, waits for them, and re-layouts: 4.26 us -> none  [to_level(): return jnp.pad(z, ((0, 0), (0, 0), (0, padded - per), (0, 0)))]
    pallas_call x5, Pallas kernels: 32.3 us -> 36.2 us  [level_apply(): pl.pallas_call(functools.partial(_kernel, mode, depth, n_lat), out_shape=...]
    all_to_all x3 -> x2, starting transfers between devices: 13 us -> 10.2 us  [exchange(): return lax.all_to_all(parts, AXES, 0, 0, tiled=True)]
  transfers between devices with their start and end apart: 3 -> 2, of which waited for: 3 -> 2; matrix products, arithmetic and copies ran while one was open for 1% -> 1% of each run, Pallas kernels for 0% -> 0%
where the time goes in v3:
time: 244 us; the launch traced here: 243 us
  blocking collectives  137 us (56%)
  Pallas kernels  36.2 us (15%)
  other arithmetic  23 us (9%)
  waiting for transfers between devices  22.5 us (9%)
  starting transfers between devices  10.2 us (4%)
  matrix products  6.78 us (3%)
  local copies, waits for them, and re-layouts  6.1 us (2%)
    all_to_all x8, blocking collectives, exchange(): return lax.all_to_all(parts, AXES, 0, 0, tiled=True)  137 us
    pallas_call x5, Pallas kernels, level_apply(): pl.pallas_call(functools.partial(_kernel, mode, depth, n_lat), out_shape=...  36.2 us
    all_to_all x2, waiting for transfers between devices, exchange(): return lax.all_to_all(parts, AXES, 0, 0, tiled=True)  22.5 us
    all_to_all x2, starting transfers between devices, exchange(): return lax.all_to_all(parts, AXES, 0, 0, tiled=True)  10.2 us
    another operation x2, other arithmetic, per_device(): jnp.stack([jnp.sum(residual * residual), jnp.sum(residual * first), jnp.s...  5.2 us
  transfers between devices with their start and end apart: 2, of which 2 were waited for; matrix products, arithmetic and copies ran while one was open for 1% of the time, Pallas kernels for 0%

profile of v3, /device:TPU:1, one launch (start us, length us, event | category | flops | bytes accessed | tf_op | source)
XLA Modules:
  0.0 243.4 jit_solution(14434264485346290264)
XLA Ops:
  0.7 0.8 copy.26
  1.5 0.7 fusion.25
  2.2 0.7 divide_bitcast_fusion
  2.9 0.7 convert_bitcast_fusion
  3.6 1.0 pad.31
  4.7 0.9 pad_maximum_fusion.4
  5.5 7.1 %all-to-all-start = ((f32[32,7,4,128]{3,2,1,0:T(4,128)}), f32[32,7,4,128]{3,2,1,0:T(4,128)S(1)}, u32[]{:S(2)}, u32[]{:S(2)}) async-start(f32[32,7,4,128]{3,2,1,0:T(4,128)} %pad_maximum_fusion.4), calls=%async_computation | async-start | bytes 917504 | tf_op jit(solution)/shard_map/all_to_all | solution.py:191
  12.7 0.7 multiply_reduce_fusion.8
  14.1 0.5 broadcast_divide_fusion.refs_3_.refs_4_
  14.7 11.9 %all-to-all-done = f32[32,7,4,128]{3,2,1,0:T(4,128)S(1)} async-done(((f32[32,7,4,128]{3,2,1,0:T(4,128)}), f32[32,7,4,128]{3,2,1,0:T(4,128)S(1)}, u32[]{:S(2)}, u32[]{:S(2)}) %all-to-all-start) | async-done | bytes 458784 | tf_op jit(solution)/shard_map/all_to_all | solution.py:191
  26.6 2.6 %fusion = f32[16,3,128,128]{3,0,2,1:T(8,128)S(1)} fusion(f32[16,33,1,1]{1,0,3,2:T(8,128)S(1)} %bitcast.112, s32[3,128,128]{2,1,0:T(8,128)S(1)} %subtract_abs_fusion), kind=kOutput, calls=%fused_computation.1 | convolution fusion | flops 313049088 | bytes 3344448 | tf_op jit(solution)/shard_map/pct,jt->jpc/dot_general | solution.py:37
  29.7 0.6 add_select_fusion.refs_2_.refs_3_
  30.8 1.5 pad_maximum_fusion.refs_1_.refs_2_
  32.3 0.8 slice.219.refs_0_.refs_1_
  33.0 5.3 %shard_map.96 = f32[32,5,4,128]{3,2,1,0:T(4,128)} custom-call(f32[32,5,4,128]{3,2,1,0:T(4,128)} %slice.219.refs_0_.refs_1_, f32[16,2,128,128]{3,2,1,0:T(8,128)} %pad_maximum_fusion.refs_1_.refs_2_, s32[8,128]{1,0:T(8,128)} %add_select_fusion.refs_2_.refs_3_, f32[5]{0:T(128)} %broadcast_divide_fusion.refs_3_.refs_4_), custom_call_target="tpu_custom_call" | custom-call | tf_op jit(solution)/shard_map/pallas_call | solution.py:165
  38.3 14.7 %all_to_all.50 = f32[32,5,4,128]{3,2,1,0:T(4,128)S(1)} all-to-all(f32[32,5,4,128]{3,2,1,0:T(4,128)} %shard_map.96), channel_id=1, replica_groups=mesh['lon'=8,'lat'=4] {'lon','lat'}, dimensions={0} | all-to-all | bytes 655360 | tf_op jit(solution)/shard_map/all_to_all | solution.py:191
  53.1 0.4 fusion.8
  53.7 0.6 convolution_bitcast_fusion.3
  54.4 14.2 %all_to_all.51.refs_0_ = f32[32,5,4,128]{3,2,1,0:T(4,128)} all-to-all(f32[32,5,4,128]{3,2,1,0:T(4,128)S(1)} %bitcast.104), channel_id=1, replica_groups=mesh['lon'=8,'lat'=4] {'lon','lat'}, dimensions={0} | all-to-all | bytes 655360 | tf_op jit(solution)/shard_map/all_to_all | solution.py:191
  68.7 8.4 %shard_map.97 = (f32[32,5,4,128]{3,2,1,0:T(4,128)}, f32[32,5,4,128]{3,2,1,0:T(4,128)}) custom-call(f32[32,5,4,128]{3,2,1,0:T(4,128)} %all_to_all.51.refs_0_, f32[32,5,4,128]{3,2,1,0:T(4,128)} %slice.219.refs_0_.refs_1_, f32[16,2,128,128]{3,2,1,0:T(8,128)} %pad_maximum_fusion.refs_1_.refs_2_, s32[8,128]{1,0:T(8,128)} %add_select_fusion.refs_2_.refs_3_, ...), custom_call_target="tpu_custom_call" | custom-call | tf_op jit(solution)/shard_map/pallas_call | solution.py:165
  77.1 1.2 pad_maximum_fusion.2
  78.3 20.6 %all_to_all.52 = f32[32,10,4,128]{3,2,1,0:T(4,128)S(1)} all-to-all(f32[32,10,4,128]{3,2,1,0:T(4,128)S(1)} %pad_maximum_fusion.2), channel_id=1, replica_groups=mesh['lon'=8,'lat'=4] {'lon','lat'}, dimensions={0} | all-to-all | bytes 1310720 | tf_op jit(solution)/shard_map/all_to_all | solution.py:191
  99.0 0.4 fusion.6
  99.6 0.6 convolution_bitcast_fusion.2
  100.4 14.6 %all_to_all.53.refs_0_ = f32[32,5,4,128]{3,2,1,0:T(4,128)} all-to-all(f32[32,5,4,128]{3,2,1,0:T(4,128)S(1)} %bitcast.105), channel_id=1, replica_groups=mesh['lon'=8,'lat'=4] {'lon','lat'}, dimensions={0} | all-to-all | bytes 655360 | tf_op jit(solution)/shard_map/all_to_all | solution.py:191
  115.1 8.4 %shard_map.98 = (f32[32,5,4,128]{3,2,1,0:T(4,128)}, f32[32,5,4,128]{3,2,1,0:T(4,128)}) custom-call(f32[32,5,4,128]{3,2,1,0:T(4,128)} %all_to_all.53.refs_0_, f32[32,5,4,128]{3,2,1,0:T(4,128)} %get-tuple-element.73.refs_1_, f32[16,2,128,128]{3,2,1,0:T(8,128)} %pad_maximum_fusion.refs_1_.refs_2_, s32[8,128]{1,0:T(8,128)} %add_select_fusion.refs_2_.refs_3_, ...), custom_call_target="tpu_custom_call" | custom-call | tf_op jit(solution)/shard_map/pallas_call | solution.py:165
  123.5 1.9 multiply_reduce_fusion.7
  125.4 2.6 %pad_maximum_fusion.6 = f32[4]{0:T(128)S(1)} fusion(f32[1]{0:T(128)} %bitcast.29, f32[1]{0:T(128)} %bitcast.28, f32[1]{0:T(128)} %bitcast.27, f32[1]{0:T(128)} %bitcast.26), kind=kLoop, calls=%fused_computation.72 | loop fusion | flops 12 | bytes 32 | tf_op jit(solution)/shard_map/stack | solution.py:264
  128.1 1.2 pad_maximum_fusion.1
  129.3 22.0 %all_to_all.54 = f32[32,11,4,128]{3,2,1,0:T(4,128)S(1)} all-to-all(f32[32,11,4,128]{3,2,1,0:T(4,128)S(1)} %pad_maximum_fusion.1), channel_id=1, replica_groups=mesh['lon'=8,'lat'=4] {'lon','lat'}, dimensions={0} | all-to-all | bytes 1441792 | tf_op jit(solution)/shard_map/all_to_all | solution.py:191
  152.1 0.6 convolution_bitcast_fusion.1
  152.9 0.8 pad.34.clone
  153.7 3.2 %all-to-all-start.6 = ((f32[32,5,4,128]{3,2,1,0:T(4,128)}), f32[32,5,4,128]{3,2,1,0:T(4,128)S(1)}, u32[]{:S(2)}, u32[]{:S(2)}) async-start(f32[32,5,4,128]{3,2,1,0:T(4,128)} %bitcast.37), calls=%async_computation.6 | async-start | bytes 655360 | tf_op jit(solution)/shard_map/all_to_all | solution.py:191
  156.8 0.9 multiply_subtract_fusion.refs_1_
  157.7 10.7 %all-to-all-done.6.refs_0_ = f32[32,5,4,128]{3,2,1,0:T(4,128)S(1)} async-done(((f32[32,5,4,128]{3,2,1,0:T(4,128)}), f32[32,5,4,128]{3,2,1,0:T(4,128)S(1)}, u32[]{:S(2)}, u32[]{:S(2)}) %all-to-all-start.6) | async-done | bytes 327712 | tf_op jit(solution)/shard_map/all_to_all | solution.py:191
  168.4 0.7 copy-done.6
  169.1 8.4 %shard_map.99 = (f32[32,5,4,128]{3,2,1,0:T(4,128)}, f32[32,5,4,128]{3,2,1,0:T(4,128)}) custom-call(f32[32,5,4,128]{3,2,1,0:T(4,128)} %copy-done.6, f32[32,5,4,128]{3,2,1,0:T(4,128)} %multiply_subtract_fusion.refs_1_, f32[16,2,128,128]{3,2,1,0:T(8,128)} %pad_maximum_fusion.refs_1_.refs_2_, s32[8,128]{1,0:T(8,128)} %add_select_fusion.refs_2_.refs_3_, ...), custom_call_target="tpu_custom_call" | custom-call | tf_op jit(solution)/shard_map/pallas_call | solution.py:165
  177.5 1.2 pad_maximum_fusion.3
  178.8 20.6 %all_to_all.55 = f32[32,10,4,128]{3,2,1,0:T(4,128)S(1)} all-to-all(f32[32,10,4,128]{3,2,1,0:T(4,128)S(1)} %pad_maximum_fusion.3), channel_id=1, replica_groups=mesh['lon'=8,'lat'=4] {'lon','lat'}, dimensions={0} | all-to-all | bytes 1310720 | tf_op jit(solution)/shard_map/all_to_all | solution.py:191
  199.5 0.4 fusion.2
  200.1 0.6 convolution_bitcast_fusion
  200.9 14.6 %all_to_all.56.refs_0_ = f32[32,5,4,128]{3,2,1,0:T(4,128)} all-to-all(f32[32,5,4,128]{3,2,1,0:T(4,128)S(1)} %bitcast.103), channel_id=1, replica_groups=mesh['lon'=8,'lat'=4] {'lon','lat'}, dimensions={0} | all-to-all | bytes 655360 | tf_op jit(solution)/shard_map/all_to_all | solution.py:191
  215.5 5.6 %shard_map.100 = f32[32,5,4,128]{3,2,1,0:T(4,128)} custom-call(f32[32,5,4,128]{3,2,1,0:T(4,128)} %all_to_all.56.refs_0_, f32[32,5,4,128]{3,2,1,0:T(4,128)} %get-tuple-element.77.refs_1_, f32[16,2,128,128]{3,2,1,0:T(8,128)} %pad_maximum_fusion.refs_1_.refs_2_, s32[8,128]{1,0:T(8,128)} %add_select_fusion.refs_2_.refs_3_, f32[5]{0:T(128)} %broadcast_divide_fusion.refs_3_.refs_4_), custom_call_target="tpu_custom_call" | custom-call | tf_op jit(solution)/shard_map/pallas_call | solution.py:165
  221.2 2.0 multiply_reduce_fusion.3
  223.1 2.6 %pad_maximum_fusion.7 = f32[4]{0:T(128)S(1)} fusion(f32[1]{0:T(128)} %bitcast.46, f32[1]{0:T(128)} %bitcast.45, f32[1]{0:T(128)} %bitcast.44, f32[1]{0:T(128)} %bitcast.43), kind=kLoop, calls=%fused_computation.73 | loop fusion | flops 12 | bytes 32 | tf_op jit(solution)/shard_map/stack | solution.py:264
  225.8 1.1 pad_maximum_fusion.5
  226.9 15.3 %all_to_all.57 = f32[32,6,4,128]{3,2,1,0:T(4,128)S(1)} all-to-all(f32[32,6,4,128]{3,2,1,0:T(4,128)S(1)} %pad_maximum_fusion.5), channel_id=1, replica_groups=mesh['lon'=8,'lat'=4] {'lon','lat'}, dimensions={0} | all-to-all | bytes 786432 | tf_op jit(solution)/shard_map/all_to_all | solution.py:191
  242.3 1.1 fusion.14
  (60 shorter events, 3.4 us)
Async XLA Ops:
  0.6 52.4 %copy-start = (f32[137,137]{1,0:T(8,128)S(1)}, f32[137,137]{1,0:T(8,128)}, u32[]{:S(2)}) copy-start(f32[137,137]{1,0:T(8,128)} %param.25) | copy-start | bytes 225232
  0.6 12.0 %copy-start.8 = (f32[5]{0:T(128)S(1)}, f32[5]{0:T(128)}, u32[]{:S(2)}) copy-start(f32[5]{0:T(128)} %param.24) | copy-start | bytes 64
  5.5 21.0 %all-to-all-start = ((f32[32,7,4,128]{3,2,1,0:T(4,128)}), f32[32,7,4,128]{3,2,1,0:T(4,128)S(1)}, u32[]{:S(2)}, u32[]{:S(2)}) async-start(f32[32,7,4,128]{3,2,1,0:T(4,128)} %pad_maximum_fusion.4), calls=%async_computation | async-start | bytes 917504 | tf_op jit(solution)/shard_map/all_to_all | solution.py:191
  33.0 20.5 %copy-start.2 = (f32[137,4,128]{2,1,0:T(4,128)S(1)}, f32[137,4,128]{2,1,0:T(4,128)}, u32[]{:S(2)}) copy-start(f32[137,4,128]{2,1,0:T(4,128)} %param.20) | copy-start | bytes 841732
  100.3 23.1 %copy-start.1 = (f32[32,5,4,128]{3,2,1,0:T(4,128)S(1)}, f32[32,5,4,128]{3,2,1,0:T(4,128)}, u32[]{:S(2)}) copy-start(f32[32,5,4,128]{3,2,1,0:T(4,128)} %get-tuple-element.73.refs_1_) | copy-start | bytes 983044
  151.5 5.3 %copy-start.5 = (f32[32,5,4,128]{3,2,1,0:T(4,128)S(1)}, f32[32,5,4,128]{3,2,1,0:T(4,128)}, u32[]{:S(2)}) copy-start(f32[32,5,4,128]{3,2,1,0:T(4,128)} %get-tuple-element.74) | copy-start | bytes 983044
  153.7 14.7 %all-to-all-start.6 = ((f32[32,5,4,128]{3,2,1,0:T(4,128)}), f32[32,5,4,128]{3,2,1,0:T(4,128)S(1)}, u32[]{:S(2)}, u32[]{:S(2)}) async-start(f32[32,5,4,128]{3,2,1,0:T(4,128)} %bitcast.37), calls=%async_computation.6 | async-start | bytes 655360 | tf_op jit(solution)/shard_map/all_to_all | solution.py:191
  168.4 0.7 copy-start.6
  200.8 20.4 %copy-start.3 = (f32[32,5,4,128]{3,2,1,0:T(4,128)S(1)}, f32[32,5,4,128]{3,2,1,0:T(4,128)}, u32[]{:S(2)}) copy-start(f32[32,5,4,128]{3,2,1,0:T(4,128)} %get-tuple-element.77.refs_1_) | copy-start | bytes 983044
  200.8 20.4 %copy-start.4 = (f32[32,5,4,128]{3,2,1,0:T(4,128)S(1)}, f32[32,5,4,128]{3,2,1,0:T(4,128)}, u32[]{:S(2)}) copy-start(f32[32,5,4,128]{3,2,1,0:T(4,128)} %multiply_subtract_fusion.refs_1_) | copy-start | bytes 983044
  221.1 21.1 %copy-start.7 = (f32[137,4,128]{2,1,0:T(4,128)S(1)}, f32[137,4,128]{2,1,0:T(4,128)}, u32[]{:S(2)}) copy-start(f32[137,4,128]{2,1,0:T(4,128)} %param.19) | copy-start | bytes 841732

commit v4 on v3

--- a/solution.py
+++ b/solution.py
@@ -190,12 +190,19 @@
     def exchange(parts):
         return lax.all_to_all(parts, AXES, 0, 0, tiled=True)
 
+    padded_lev = n_dev * per
+
     def col_parts(x):
-        x = jnp.pad(x, ((0, n_dev * per - lev), (0, 0), (0, 0)))
+        x = jnp.pad(x, ((0, padded_lev - x.shape[0]), (0, 0), (0, 0)))
         return x.reshape(n_dev, per, rows, cols)
 
     def to_column(z):
-        return z.reshape(n_dev * per, rows, cols)[:lev]
+        return z.reshape(padded_lev, rows, cols)
+
+    def to_output(z):
+        return z.reshape(padded_lev, rows, cols)[:lev]
+
+    vertical_pad = jnp.pad(vertical_map, ((0, 0), (0, padded_lev - lev)))
 
     lanes = cols if rows >= 4 else 1
 
@@ -208,31 +215,21 @@
         flat = piece.reshape(n_dev, rows * cols)[:, : 4 * lanes].reshape(n_dev, 4, lanes)
         return jnp.sum(flat, axis=0)
 
-    mirror_slab = jnp.zeros((1, 1, rows, cols), jnp.float32).at[0, 0, 0].set(
-        mirror_map.astype(jnp.float32)
-    )
-    zonal_slab = jnp.zeros((1, 1, rows, cols), jnp.float32).at[0, 0, :, : width + 1].set(
-        zonal_weights(half_width, zonal_coef)
-    )
+    params = jnp.concatenate(
+        [mirror_map.astype(jnp.float32), zonal_weights(half_width, zonal_coef).reshape(-1)]
+    )
+    slab_count = -(-params.shape[0] // (rows * cols))
+    params = jnp.pad(params, (0, slab_count * rows * cols - params.shape[0]))
+    params = params.reshape(1, slab_count, rows, cols)
     got = exchange(
         jnp.concatenate(
-            [
-                col_parts(gradient),
-                jnp.broadcast_to(mirror_slab, (n_dev, 1, rows, cols)),
-                jnp.broadcast_to(zonal_slab, (n_dev, 1, rows, cols)),
-            ],
-            axis=1,
+            [col_parts(gradient), jnp.broadcast_to(params, (n_dev, slab_count, rows, cols))], axis=1
         )
     )
     residual = got[:, :per]
-    mirror_all = (
-        got[:, per, 0, :].reshape(n_lon, n_lat, cols)[:, 0].reshape(n_lon * cols).astype(jnp.int32)
-    )
-    zonal_all = (
-        got[:, per + 1, :, : width + 1]
-        .reshape(n_lon, n_lat, rows, width + 1)[0]
-        .reshape(n_lat * rows, width + 1)
-    )
+    received = got[:, per:].reshape(n_lon, n_lat, slab_count * rows * cols)
+    mirror_all = received[:, 0, :cols].reshape(n_lon * cols).astype(jnp.int32)
+    zonal_all = received[0, :, cols : cols + rows * (width + 1)].reshape(n_lat * rows, width + 1)
     table = zonal_tables(zonal_all, cols)
     onehot = mirror_tables(mirror_all, cols)
 
@@ -240,8 +237,8 @@
         return level_apply("p", (x,), table, onehot, merid_w, n_lat, padded)
 
     def middle(y):
-        lifted = jnp.einsum("kl,lji->kji", vertical_map, y, precision=HI)
-        return jnp.einsum("lk,lji->kji", vertical_map, obs_weight * lifted, precision=HI)
+        lifted = jnp.einsum("kl,lji->kji", vertical_pad, y, precision=HI)
+        return jnp.einsum("lk,lji->kji", vertical_pad, obs_weight * lifted, precision=HI)
 
     def image(x, px_col, mode):
         return level_apply(
@@ -256,7 +253,7 @@
         first, pfirst = image(residual, pres_col, "qp")
         got = exchange(jnp.concatenate([pfirst, first], axis=1))
         pfirst_col = to_column(got[:, :per])
-        first_col = to_column(got[:, per:])
+        first_col = to_output(got[:, per:])
         if last:
             second = image(first, pfirst_col, "q")
         else:
@@ -273,7 +270,7 @@
         if not last:
             parts.append((psecond))
         got = exchange(jnp.concatenate(parts + [slab(sums)], axis=1))
-        second_col = to_column(got[:, :per])
+        second_col = to_output(got[:, :per])
         total = totals(got[:, len(parts) * per])
         sum_rr, sum_rf, sum_ff, sum_fs = total[0], total[1], total[2], total[3]
         determinant = sum_rf * sum_fs - sum_ff * sum_ff

time: 244 us -> 242 us (level)
  no operation moved by 1% of the time
where the time goes in v4:
time: 242 us; the launch traced here: 241 us
  blocking collectives  136 us (56%)
  Pallas kernels  36.2 us (15%)
  other arithmetic  22.7 us (9%)
  waiting for transfers between devices  21.3 us (9%)
  starting transfers between devices  10.3 us (4%)
  matrix products  6.8 us (3%)
  local copies, waits for them, and re-layouts  5.63 us (2%)
    all_to_all x8, blocking collectives, exchange(): return lax.all_to_all(parts, AXES, 0, 0, tiled=True)  136 us
    pallas_call x5, Pallas kernels, level_apply(): pl.pallas_call(functools.partial(_kernel, mode, depth, n_lat), out_shape=...  36.2 us
    all_to_all x2, waiting for transfers between devices, exchange(): return lax.all_to_all(parts, AXES, 0, 0, tiled=True)  21.3 us
    all_to_all x2, starting transfers between devices, exchange(): return lax.all_to_all(parts, AXES, 0, 0, tiled=True)  10.3 us
    another operation x2, other arithmetic, per_device(): jnp.stack([jnp.sum(residual * residual), jnp.sum(residual * first), jnp.s...  5.2 us
  transfers between devices with their start and end apart: 2, of which 2 were waited for; matrix products, arithmetic and copies ran while one was open for 1% of the time, Pallas kernels for 0%

profile of v4, /device:TPU:1, one launch (start us, length us, event | category | flops | bytes accessed | tf_op | source)
XLA Modules:
  0.0 241.1 jit_solution(1098577411717314765)
XLA Ops:
  0.6 0.8 fusion.38
  1.8 0.8 broadcast_divide_fusion
  2.7 0.7 convert_element_type.17
  3.3 1.0 pad.19
  4.4 0.8 pad_maximum_fusion.4
  5.2 7.1 %all-to-all-start = ((f32[32,6,4,128]{3,2,1,0:T(4,128)}), f32[32,6,4,128]{3,2,1,0:T(4,128)S(1)}, u32[]{:S(2)}, u32[]{:S(2)}) async-start(f32[32,6,4,128]{3,2,1,0:T(4,128)} %pad_maximum_fusion.4), calls=%async_computation | async-start | bytes 786432 | tf_op jit(solution)/shard_map/all_to_all | solution.py:191
  12.3 0.7 multiply_reduce_fusion.9
  13.7 0.5 broadcast_divide_fusion.1.refs_3_.refs_4_
  14.4 10.7 %all-to-all-done = f32[32,6,4,128]{3,2,1,0:T(4,128)S(1)} async-done(((f32[32,6,4,128]{3,2,1,0:T(4,128)}), f32[32,6,4,128]{3,2,1,0:T(4,128)S(1)}, u32[]{:S(2)}, u32[]{:S(2)}) %all-to-all-start) | async-done | bytes 393248 | tf_op jit(solution)/shard_map/all_to_all | solution.py:191
  25.2 2.6 %fusion = f32[16,3,128,128]{3,0,2,1:T(8,128)S(1)} fusion(s32[3,128,128]{2,1,0:T(8,128)S(1)} %subtract_abs_fusion, f32[16,33,1,1]{1,0,2,3:T(8,128)S(1)} %reshape.364), kind=kOutput, calls=%fused_computation.1 | convolution fusion | flops 313049088 | bytes 3344448 | tf_op jit(solution)/shard_map/pct,jt->jpc/dot_general | solution.py:37
  28.4 0.6 add_select_fusion.refs_2_.refs_3_
  29.4 1.5 pad_maximum_fusion.refs_1_.refs_2_
  30.9 0.8 slice.146.refs_0_.refs_1_
  31.7 5.2 %shard_map.96 = f32[32,5,4,128]{3,2,1,0:T(4,128)} custom-call(f32[32,5,4,128]{3,2,1,0:T(4,128)} %slice.146.refs_0_.refs_1_, f32[16,2,128,128]{3,2,1,0:T(8,128)} %pad_maximum_fusion.refs_1_.refs_2_, s32[8,128]{1,0:T(8,128)} %add_select_fusion.refs_2_.refs_3_, f32[5]{0:T(128)} %broadcast_divide_fusion.1.refs_3_.refs_4_), custom_call_target="tpu_custom_call" | custom-call | tf_op jit(solution)/shard_map/pallas_call | solution.py:165
  36.9 14.5 %all_to_all.50 = f32[32,5,4,128]{3,2,1,0:T(4,128)S(1)} all-to-all(f32[32,5,4,128]{3,2,1,0:T(4,128)} %shard_map.96), channel_id=1, replica_groups=mesh['lon'=8,'lat'=4] {'lon','lat'}, dimensions={0} | all-to-all | bytes 655360 | tf_op jit(solution)/shard_map/all_to_all | solution.py:191
  51.4 0.4 convolution_multiply_fusion.3
  51.8 0.6 fusion.24
  52.7 14.2 %all_to_all.51.refs_0_ = f32[32,5,4,128]{3,2,1,0:T(4,128)} all-to-all(f32[32,5,4,128]{3,2,1,0:T(4,128)S(1)} %bitcast.77), channel_id=1, replica_groups=mesh['lon'=8,'lat'=4] {'lon','lat'}, dimensions={0} | all-to-all | bytes 655360 | tf_op jit(solution)/shard_map/all_to_all | solution.py:191
  66.9 8.4 %shard_map.97 = (f32[32,5,4,128]{3,2,1,0:T(4,128)}, f32[32,5,4,128]{3,2,1,0:T(4,128)}) custom-call(f32[32,5,4,128]{3,2,1,0:T(4,128)} %all_to_all.51.refs_0_, f32[32,5,4,128]{3,2,1,0:T(4,128)} %slice.146.refs_0_.refs_1_, f32[16,2,128,128]{3,2,1,0:T(8,128)} %pad_maximum_fusion.refs_1_.refs_2_, s32[8,128]{1,0:T(8,128)} %add_select_fusion.refs_2_.refs_3_, ...), custom_call_target="tpu_custom_call" | custom-call | tf_op jit(solution)/shard_map/pallas_call | solution.py:165
  75.3 1.2 pad_maximum_fusion.2
  76.6 20.6 %all_to_all.52 = f32[32,10,4,128]{3,2,1,0:T(4,128)S(1)} all-to-all(f32[32,10,4,128]{3,2,1,0:T(4,128)S(1)} %pad_maximum_fusion.2), channel_id=1, replica_groups=mesh['lon'=8,'lat'=4] {'lon','lat'}, dimensions={0} | all-to-all | bytes 1310720 | tf_op jit(solution)/shard_map/all_to_all | solution.py:191
  97.2 0.4 convolution_multiply_fusion.2
  97.7 0.6 fusion.21
  98.5 14.6 %all_to_all.53.refs_0_ = f32[32,5,4,128]{3,2,1,0:T(4,128)} all-to-all(f32[32,5,4,128]{3,2,1,0:T(4,128)S(1)} %bitcast.78), channel_id=1, replica_groups=mesh['lon'=8,'lat'=4] {'lon','lat'}, dimensions={0} | all-to-all | bytes 655360 | tf_op jit(solution)/shard_map/all_to_all | solution.py:191
  113.1 8.4 %shard_map.98 = (f32[32,5,4,128]{3,2,1,0:T(4,128)}, f32[32,5,4,128]{3,2,1,0:T(4,128)}) custom-call(f32[32,5,4,128]{3,2,1,0:T(4,128)} %all_to_all.53.refs_0_, f32[32,5,4,128]{3,2,1,0:T(4,128)} %get-tuple-element.49.refs_1_, f32[16,2,128,128]{3,2,1,0:T(8,128)} %pad_maximum_fusion.refs_1_.refs_2_, s32[8,128]{1,0:T(8,128)} %add_select_fusion.refs_2_.refs_3_, ...), custom_call_target="tpu_custom_call" | custom-call | tf_op jit(solution)/shard_map/pallas_call | solution.py:165
  121.6 1.9 multiply_reduce_fusion.7
  123.5 2.6 %pad_maximum_fusion.6 = f32[4]{0:T(128)S(1)} fusion(f32[1]{0:T(128)} %bitcast.17, f32[1]{0:T(128)} %bitcast.16, f32[1]{0:T(128)} %bitcast.15, f32[1]{0:T(128)} %bitcast.14), kind=kLoop, calls=%fused_computation.78 | loop fusion | flops 12 | bytes 32 | tf_op jit(solution)/shard_map/stack | solution.py:261
  126.1 1.2 pad_maximum_fusion.1
  127.4 22.0 %all_to_all.54 = f32[32,11,4,128]{3,2,1,0:T(4,128)S(1)} all-to-all(f32[32,11,4,128]{3,2,1,0:T(4,128)S(1)} %pad_maximum_fusion.1), channel_id=1, replica_groups=mesh['lon'=8,'lat'=4] {'lon','lat'}, dimensions={0} | all-to-all | bytes 1441792 | tf_op jit(solution)/shard_map/all_to_all | solution.py:191
  149.5 0.5 convolution_multiply_fusion.1
  150.0 0.6 fusion.18
  150.6 0.9 copy.69
  151.5 3.2 %all-to-all-start.6 = ((f32[32,5,4,128]{3,2,1,0:T(4,128)}), f32[32,5,4,128]{3,2,1,0:T(4,128)S(1)}, u32[]{:S(2)}, u32[]{:S(2)}) async-start(f32[32,5,4,128]{3,2,1,0:T(4,128)} %bitcast.22), calls=%async_computation.6 | async-start | bytes 655360 | tf_op jit(solution)/shard_map/all_to_all | solution.py:191
  154.7 0.9 multiply_subtract_fusion.refs_1_
  155.6 10.7 %all-to-all-done.6.refs_0_ = f32[32,5,4,128]{3,2,1,0:T(4,128)S(1)} async-done(((f32[32,5,4,128]{3,2,1,0:T(4,128)}), f32[32,5,4,128]{3,2,1,0:T(4,128)S(1)}, u32[]{:S(2)}, u32[]{:S(2)}) %all-to-all-start.6) | async-done | bytes 327712 | tf_op jit(solution)/shard_map/all_to_all | solution.py:191
  166.3 0.7 copy-done.6
  167.0 8.4 %shard_map.99 = (f32[32,5,4,128]{3,2,1,0:T(4,128)}, f32[32,5,4,128]{3,2,1,0:T(4,128)}) custom-call(f32[32,5,4,128]{3,2,1,0:T(4,128)} %copy-done.6, f32[32,5,4,128]{3,2,1,0:T(4,128)} %multiply_subtract_fusion.refs_1_, f32[16,2,128,128]{3,2,1,0:T(8,128)} %pad_maximum_fusion.refs_1_.refs_2_, s32[8,128]{1,0:T(8,128)} %add_select_fusion.refs_2_.refs_3_, ...), custom_call_target="tpu_custom_call" | custom-call | tf_op jit(solution)/shard_map/pallas_call | solution.py:165
  175.4 1.2 pad_maximum_fusion.3
  176.6 20.6 %all_to_all.55 = f32[32,10,4,128]{3,2,1,0:T(4,128)S(1)} all-to-all(f32[32,10,4,128]{3,2,1,0:T(4,128)S(1)} %pad_maximum_fusion.3), channel_id=1, replica_groups=mesh['lon'=8,'lat'=4] {'lon','lat'}, dimensions={0} | all-to-all | bytes 1310720 | tf_op jit(solution)/shard_map/all_to_all | solution.py:191
  197.3 0.4 convolution_multiply_fusion
  197.8 0.6 fusion.15
  198.6 14.6 %all_to_all.56.refs_0_ = f32[32,5,4,128]{3,2,1,0:T(4,128)} all-to-all(f32[32,5,4,128]{3,2,1,0:T(4,128)S(1)} %bitcast.79), channel_id=1, replica_groups=mesh['lon'=8,'lat'=4] {'lon','lat'}, dimensions={0} | all-to-all | bytes 655360 | tf_op jit(solution)/shard_map/all_to_all | solution.py:191
  213.2 5.6 %shard_map.100 = f32[32,5,4,128]{3,2,1,0:T(4,128)} custom-call(f32[32,5,4,128]{3,2,1,0:T(4,128)} %all_to_all.56.refs_0_, f32[32,5,4,128]{3,2,1,0:T(4,128)} %get-tuple-element.53.refs_1_, f32[16,2,128,128]{3,2,1,0:T(8,128)} %pad_maximum_fusion.refs_1_.refs_2_, s32[8,128]{1,0:T(8,128)} %add_select_fusion.refs_2_.refs_3_, f32[5]{0:T(128)} %broadcast_divide_fusion.1.refs_3_.refs_4_), custom_call_target="tpu_custom_call" | custom-call | tf_op jit(solution)/shard_map/pallas_call | solution.py:165
  218.9 2.0 multiply_reduce_fusion.3
  220.8 2.6 %pad_maximum_fusion.7 = f32[4]{0:T(128)S(1)} fusion(f32[1]{0:T(128)} %bitcast.28, f32[1]{0:T(128)} %bitcast.27, f32[1]{0:T(128)} %bitcast.26, f32[1]{0:T(128)} %bitcast.25), kind=kLoop, calls=%fused_computation.79 | loop fusion | flops 12 | bytes 32 | tf_op jit(solution)/shard_map/stack | solution.py:261
  223.5 1.1 pad_maximum_fusion.5
  224.6 15.3 %all_to_all.57 = f32[32,6,4,128]{3,2,1,0:T(4,128)S(1)} all-to-all(f32[32,6,4,128]{3,2,1,0:T(4,128)S(1)} %pad_maximum_fusion.5), channel_id=1, replica_groups=mesh['lon'=8,'lat'=4] {'lon','lat'}, dimensions={0} | all-to-all | bytes 786432 | tf_op jit(solution)/shard_map/all_to_all | solution.py:191
  240.0 1.1 fusion.11
  (49 shorter events, 2.8 us)
Async XLA Ops:
  0.6 11.7 %copy-start.8 = (f32[5]{0:T(128)S(1)}, f32[5]{0:T(128)}, u32[]{:S(2)}) copy-start(f32[5]{0:T(128)} %param.20) | copy-start | bytes 64
  5.2 19.8 %all-to-all-start = ((f32[32,6,4,128]{3,2,1,0:T(4,128)}), f32[32,6,4,128]{3,2,1,0:T(4,128)S(1)}, u32[]{:S(2)}, u32[]{:S(2)}) async-start(f32[32,6,4,128]{3,2,1,0:T(4,128)} %pad_maximum_fusion.4), calls=%async_computation | async-start | bytes 786432 | tf_op jit(solution)/shard_map/all_to_all | solution.py:191
  30.9 20.5 %copy-start = (f32[137,137]{1,0:T(8,128)S(1)}, f32[137,137]{1,0:T(8,128)}, u32[]{:S(2)}) copy-start(f32[137,137]{1,0:T(8,128)} %param.21) | copy-start | bytes 225232
  30.9 20.5 %copy-start.2 = (f32[137,4,128]{2,1,0:T(4,128)S(1)}, f32[137,4,128]{2,1,0:T(4,128)}, u32[]{:S(2)}) copy-start(f32[137,4,128]{2,1,0:T(4,128)} %param.16) | copy-start | bytes 841732
  98.3 23.3 %copy-start.1 = (f32[32,5,4,128]{3,2,1,0:T(4,128)S(1)}, f32[32,5,4,128]{3,2,1,0:T(4,128)}, u32[]{:S(2)}) copy-start(f32[32,5,4,128]{3,2,1,0:T(4,128)} %get-tuple-element.49.refs_1_) | copy-start | bytes 983044
  149.5 5.2 %copy-start.5 = (f32[32,5,4,128]{3,2,1,0:T(4,128)S(1)}, f32[32,5,4,128]{3,2,1,0:T(4,128)}, u32[]{:S(2)}) copy-start(f32[32,5,4,128]{3,2,1,0:T(4,128)} %get-tuple-element.50) | copy-start | bytes 983044
  151.5 14.7 %all-to-all-start.6 = ((f32[32,5,4,128]{3,2,1,0:T(4,128)}), f32[32,5,4,128]{3,2,1,0:T(4,128)S(1)}, u32[]{:S(2)}, u32[]{:S(2)}) async-start(f32[32,5,4,128]{3,2,1,0:T(4,128)} %bitcast.22), calls=%async_computation.6 | async-start | bytes 655360 | tf_op jit(solution)/shard_map/all_to_all | solution.py:191
  166.3 0.7 copy-start.6
  198.4 20.5 %copy-start.3 = (f32[32,5,4,128]{3,2,1,0:T(4,128)S(1)}, f32[32,5,4,128]{3,2,1,0:T(4,128)}, u32[]{:S(2)}) copy-start(f32[32,5,4,128]{3,2,1,0:T(4,128)} %get-tuple-element.53.refs_1_) | copy-start | bytes 983044
  198.4 20.5 %copy-start.4 = (f32[32,5,4,128]{3,2,1,0:T(4,128)S(1)}, f32[32,5,4,128]{3,2,1,0:T(4,128)}, u32[]{:S(2)}) copy-start(f32[32,5,4,128]{3,2,1,0:T(4,128)} %multiply_subtract_fusion.refs_1_) | copy-start | bytes 983044
  218.9 21.1 %copy-start.7 = (f32[137,4,128]{2,1,0:T(4,128)S(1)}, f32[137,4,128]{2,1,0:T(4,128)}, u32[]{:S(2)}) copy-start(f32[137,4,128]{2,1,0:T(4,128)} %param.15) | copy-start | bytes 841732

commit v5 on v4

--- a/solution.py
+++ b/solution.py
@@ -98,14 +98,14 @@
         dst[j] = acc
 
 
-def _unpack(parts_ref, dst, n_lat):
-    _, per, rl, _ = parts_ref.shape
+def _unpack(parts_ref, off, dst, n_lat, per):
+    rl = parts_ref.shape[2]
     nb = dst.shape[1]
 
     def one_block(b, carry):
         for a in range(n_lat):
             for lev in range(per):
-                tile = parts_ref[b * n_lat + a, lev]
+                tile = parts_ref[b * n_lat + a, off + lev]
                 for r in range(rl):
                     dst[a * rl + r, pl.ds(b, 1), pl.ds(lev, 1), :] = tile[r : r + 1].reshape(1, 1, -1)
         return carry
@@ -113,8 +113,8 @@
     lax.fori_loop(0, nb, one_block, 0)
 
 
-def _pack(src, parts_ref, n_lat):
-    _, per, rl, _ = parts_ref.shape
+def _pack(src, parts_ref, off, n_lat, per):
+    rl = parts_ref.shape[2]
     nb = src.shape[1]
 
     def one_block(b, carry):
@@ -124,49 +124,65 @@
                     [src[a * rl + r, pl.ds(b, 1), pl.ds(lev, 1), :].reshape(1, -1) for r in range(rl)],
                     axis=0,
                 )
-                parts_ref[b * n_lat + a, lev] = tile
+                parts_ref[b * n_lat + a, off + lev] = tile
         return carry
 
     lax.fori_loop(0, nb, one_block, 0)
 
 
-def _kernel(mode, depth, n_lat, *refs):
-    if mode == "p":
-        x_ref, table_ref, index_ref, w_ref, p_ref, u, v, mir = refs
-        _unpack(x_ref, u, n_lat)
+def _kernel(spec, *refs):
+    depth, n_lat, per, x_off, r_off, offsets, has_a, has_r = spec
+    refs = list(refs)
+    a_ref = refs.pop(0) if has_a else None
+    x_ref = refs.pop(0)
+    r_ref = refs.pop(0) if has_r else None
+    table_ref, index_ref, w_ref, out_ref, u, v, mir = refs
+    if a_ref is None:
+        _unpack(x_ref, x_off, u, n_lat, per)
         _zonal_rows(u, v, table_ref)
         _merid_rows(v, u, mir, index_ref, w_ref, depth)
-        _pack(u, p_ref, n_lat)
+        _pack(u, out_ref, offsets["p"], n_lat, per)
         return
-    a_ref, x_ref, table_ref, index_ref, w_ref = refs[:5]
-    if mode == "q":
-        f_ref, u, v, mir = refs[5:]
-    else:
-        f_ref, p_ref, u, v, mir = refs[5:]
-    _unpack(a_ref, u, n_lat)
+    _unpack(a_ref, 0, u, n_lat, per)
     _merid_rows(u, v, mir, index_ref, w_ref, depth)
-    _unpack(x_ref, u, n_lat)
+    _unpack(x_ref, x_off, u, n_lat, per)
     _zonal_rows(v, v, table_ref, add=u)
-    _pack(v, f_ref, n_lat)
-    if mode == "qp":
+    _pack(v, out_ref, offsets["f"], n_lat, per)
+    if "p" in offsets:
         _zonal_rows(v, u, table_ref)
         _merid_rows(u, v, mir, index_ref, w_ref, depth)
-        _pack(v, p_ref, n_lat)
-
-
-def level_apply(mode, fields, table, index, merid_w, n_lat, padded):
-    shape = fields[0].shape
-    n_dev, per, rl, block = shape
+        _pack(v, out_ref, offsets["p"], n_lat, per)
+    if "slab" in offsets:
+        res = r_ref[:, pl.ds(r_off, per)]
+        fst = x_ref[:, pl.ds(x_off, per)]
+        snd = out_ref[:, pl.ds(offsets["f"], per)]
+        sums = [jnp.sum(res * res), jnp.sum(res * fst), jnp.sum(fst * fst), jnp.sum(fst * snd)]
+        n_dev, _, rl, block = out_ref.shape
+        row = lax.broadcasted_iota(jnp.int32, (rl, block), 0)
+        tile = jnp.zeros((rl, block), jnp.float32)
+        for i, value in enumerate(sums):
+            tile = jnp.where(row == i, value, tile)
+        out_ref[:, offsets["slab"]] = jnp.broadcast_to(tile[None], (n_dev, rl, block))
+
+
+def level_apply(sections, a, x, x_off, r, r_off, table, index, merid_w, n_lat, per, padded):
+    n_dev, _, rl, block = x.shape
     nb = n_dev // n_lat
     level_shape = (n_lat * rl, nb, padded, block)
     depth = merid_w.shape[0] - 1
+    offsets = {}
+    levels = 0
+    for name in sections:
+        offsets[name] = levels
+        levels += 1 if name == "slab" else per
+    spec = (depth, n_lat, per, x_off, r_off, offsets, a is not None, r is not None)
+    fields = [f for f in (a, x, r) if f is not None]
     vmem = pl.BlockSpec(memory_space=pltpu.MemorySpace.VMEM)
-    outs = 2 if mode == "qp" else 1
-    result = pl.pallas_call(
-        functools.partial(_kernel, mode, depth, n_lat),
-        out_shape=[jax.ShapeDtypeStruct(shape, jnp.float32)] * outs,
+    return pl.pallas_call(
+        functools.partial(_kernel, spec),
+        out_shape=jax.ShapeDtypeStruct((n_dev, levels, rl, block), jnp.float32),
         in_specs=[vmem] * (len(fields) + 2) + [pl.BlockSpec(memory_space=pltpu.MemorySpace.SMEM)],
-        out_specs=[vmem] * outs,
+        out_specs=vmem,
         scratch_shapes=[
             pltpu.VMEM(level_shape, jnp.float32),
             pltpu.VMEM(level_shape, jnp.float32),
@@ -174,7 +190,6 @@
         ],
         compiler_params=pltpu.CompilerParams(vmem_limit_bytes=60 * 1024 * 1024),
     )(*fields, table, index, merid_w)
-    return result if outs == 2 else result[0]
 
 
 def per_device(gradient, obs_weight, half_width, zonal_coef, mirror_map, merid_coef, vertical_map):
@@ -211,6 +226,9 @@
         flat = jnp.zeros((rows * cols,), jnp.float32).at[: flat.shape[0]].set(flat)
         return jnp.broadcast_to(flat.reshape(1, 1, rows, cols), (n_dev, 1, rows, cols))
 
+    def levels_of(sections):
+        return sum(1 if name == "slab" else per for name in sections)
+
     def totals(piece):
         flat = piece.reshape(n_dev, rows * cols)[:, : 4 * lanes].reshape(n_dev, 4, lanes)
         return jnp.sum(flat, axis=0)
@@ -226,52 +244,39 @@
             [col_parts(gradient), jnp.broadcast_to(params, (n_dev, slab_count, rows, cols))], axis=1
         )
     )
-    residual = got[:, :per]
     received = got[:, per:].reshape(n_lon, n_lat, slab_count * rows * cols)
     mirror_all = received[:, 0, :cols].reshape(n_lon * cols).astype(jnp.int32)
     zonal_all = received[0, :, cols : cols + rows * (width + 1)].reshape(n_lat * rows, width + 1)
     table = zonal_tables(zonal_all, cols)
     onehot = mirror_tables(mirror_all, cols)
 
-    def forward(x):
-        return level_apply("p", (x,), table, onehot, merid_w, n_lat, padded)
+    def apply(sections, a, x, x_off, r=None, r_off=0):
+        return level_apply(
+            sections, a, x, x_off, r, r_off, table, onehot, merid_w, n_lat, per, padded
+        )
 
     def middle(y):
         lifted = jnp.einsum("kl,lji->kji", vertical_pad, y, precision=HI)
         return jnp.einsum("lk,lji->kji", vertical_pad, obs_weight * lifted, precision=HI)
 
-    def image(x, px_col, mode):
-        return level_apply(
-            mode, (exchange(col_parts(middle(px_col))), x), table, onehot, merid_w, n_lat, padded
-        )
+    def lowered(px_col):
+        return exchange(col_parts(middle(px_col)))
 
     res_col = gradient
     inc_col = jnp.zeros_like(gradient)
-    pres_col = to_column(exchange(forward(residual)))
+    res_buf = got
+    pres_col = to_column(exchange(apply(("p",), None, res_buf, 0)))
     for outer in range(OUTER):
         last = outer == OUTER - 1
-        first, pfirst = image(residual, pres_col, "qp")
-        got = exchange(jnp.concatenate([pfirst, first], axis=1))
+        first_buf = apply(("p", "f"), lowered(pres_col), res_buf, 0)
+        got = exchange(first_buf)
         pfirst_col = to_column(got[:, :per])
         first_col = to_output(got[:, per:])
-        if last:
-            second = image(first, pfirst_col, "q")
-        else:
-            second, psecond = image(first, pfirst_col, "qp")
-        sums = jnp.stack(
-            [
-                jnp.sum(residual * residual),
-                jnp.sum(residual * first),
-                jnp.sum(first * first),
-                jnp.sum(first * second),
-            ]
-        )
-        parts = [(second)]
-        if not last:
-            parts.append((psecond))
-        got = exchange(jnp.concatenate(parts + [slab(sums)], axis=1))
+        sections = ("f", "slab") if last else ("f", "p", "slab")
+        second_buf = apply(sections, lowered(pfirst_col), first_buf, per, res_buf, 0)
+        got = exchange(second_buf)
         second_col = to_output(got[:, :per])
-        total = totals(got[:, len(parts) * per])
+        total = totals(got[:, levels_of(sections) - 1])
         sum_rr, sum_rf, sum_ff, sum_fs = total[0], total[1], total[2], total[3]
         determinant = sum_rf * sum_fs - sum_ff * sum_ff
         coef_one = (sum_fs * sum_rr - sum_ff * sum_rf) / determinant
@@ -280,7 +285,11 @@
         res_col = res_col - coef_one * first_col - coef_two * second_col
         if not last:
             psecond_col = to_column(got[:, per : 2 * per])
-            residual = residual - coef_one * first - coef_two * second
+            res_buf = (
+                res_buf[:, :per]
+                - coef_one * first_buf[:, per : 2 * per]
+                - coef_two * second_buf[:, :per]
+            )
             pres_col = pres_col - coef_one * pfirst_col - coef_two * psecond_col
     return (inc_col, res_col)
 

time: 242 us -> 229 us (0.946)
  other arithmetic: 22.7 us -> 9.83 us
    another operation x2 -> x0, other arithmetic: 5.2 us -> none  [per_device(): jnp.stack([jnp.sum(residual * residual), jnp.sum(residual * first), jnp.s...]
    concatenate x4 -> x0, other arithmetic: 4.72 us -> none  [the longest x2 2.43 us: per_device(): got = exchange(jnp.concatenate([pfirst, first], axis=1))]
    reduce_sum x2 -> x0, other arithmetic: 3.88 us -> none  [per_device(): jnp.sum(residual * residual)]
where the time goes in v5:
time: 229 us; the launch traced here: 228 us
  blocking collectives  137 us (60%)
  Pallas kernels  37.6 us (16%)
  waiting for transfers between devices  20.4 us (9%)
  starting transfers between devices  10.3 us (4%)
  other arithmetic  9.83 us (4%)
  matrix products  6.81 us (3%)
  local copies, waits for them, and re-layouts  4.68 us (2%)
    all_to_all x8, blocking collectives, exchange(): return lax.all_to_all(parts, AXES, 0, 0, tiled=True)  137 us
    pallas_call x5, Pallas kernels, level_apply(): pl.pallas_call(functools.partial(_kernel, spec), out_shape=jax.ShapeDtype...  37.6 us
    all_to_all x2, waiting for transfers between devices, exchange(): return lax.all_to_all(parts, AXES, 0, 0, tiled=True)  20.4 us
    all_to_all x2, starting transfers between devices, exchange(): return lax.all_to_all(parts, AXES, 0, 0, tiled=True)  10.3 us
  transfers between devices with their start and end apart: 2, of which 2 were waited for; matrix products, arithmetic and copies ran while one was open for 1% of the time, Pallas kernels for 0%

profile of v5, /device:TPU:1, one launch (start us, length us, event | category | flops | bytes accessed | tf_op | source)
XLA Modules:
  0.0 228.5 jit_solution(1390480506578673102)
XLA Ops:
  0.6 0.8 fusion.40
  1.4 0.2 multiply_reduce_fusion
  1.6 0.1 copy.54
  1.7 0.1 sqrt_reduce_fusion
  1.8 0.8 broadcast_divide_fusion
  2.7 0.7 convert_element_type.17
  3.3 1.0 pad.13
  4.4 0.8 pad_maximum_fusion.1
  5.2 7.1 %all-to-all-start = ((f32[32,6,4,128]{3,2,1,0:T(4,128)}), f32[32,6,4,128]{3,2,1,0:T(4,128)S(1)}, u32[]{:S(2)}, u32[]{:S(2)}) async-start(f32[32,6,4,128]{3,2,1,0:T(4,128)} %pad_maximum_fusion.1), calls=%async_computation | async-start | bytes 786432 | tf_op jit(solution)/shard_map/all_to_all | solution.py:206
  12.3 0.7 multiply_reduce_fusion.1
  13.7 0.5 broadcast_divide_fusion.1.refs_3_.refs_4_.refs_5_
  14.2 0.1 subtract_abs_fusion
  14.4 10.7 %all-to-all-done.refs_0_.refs_1_.refs_2_ = f32[32,6,4,128]{3,2,1,0:T(4,128)S(1)} async-done(((f32[32,6,4,128]{3,2,1,0:T(4,128)}), f32[32,6,4,128]{3,2,1,0:T(4,128)S(1)}, u32[]{:S(2)}, u32[]{:S(2)}) %all-to-all-start) | async-done | bytes 393248 | tf_op jit(solution)/shard_map/all_to_all | solution.py:206
  25.2 2.6 %fusion = f32[16,3,128,128]{3,0,2,1:T(8,128)S(1)} fusion(s32[3,128,128]{2,1,0:T(8,128)S(1)} %subtract_abs_fusion, f32[16,33,1,1]{1,0,2,3:T(8,128)S(1)} %reshape.302), kind=kOutput, calls=%fused_computation.1 | convolution fusion | flops 313049088 | bytes 3344448 | tf_op jit(solution)/shard_map/pct,jt->jpc/dot_general | solution.py:37
  28.0 0.3 copy.74
  28.4 0.6 add_select_fusion.refs_2_.refs_3_.refs_4_
  29.0 0.3 copy_bitcast_fusion
  29.4 1.5 pad_maximum_fusion.refs_1_.refs_2_.refs_3_
  30.9 5.3 %shard_map.86 = f32[32,5,4,128]{3,2,1,0:T(4,128)} custom-call(f32[32,6,4,128]{3,2,1,0:T(4,128)} %copy-done, f32[16,2,128,128]{3,2,1,0:T(8,128)} %pad_maximum_fusion.refs_1_.refs_2_.refs_3_, s32[8,128]{1,0:T(8,128)} %add_select_fusion.refs_2_.refs_3_.refs_4_, f32[5]{0:T(128)} %broadcast_divide_fusion.1.refs_3_.refs_4_.refs_5_), custom_call_target="tpu_custom_call" | custom-call | tf_op jit(solution)/shard_map/pallas_call | solution.py:181
  36.2 14.5 %all_to_all.50 = f32[32,5,4,128]{3,2,1,0:T(4,128)S(1)} all-to-all(f32[32,5,4,128]{3,2,1,0:T(4,128)} %shard_map.86), channel_id=1, replica_groups=mesh['lon'=8,'lat'=4] {'lon','lat'}, dimensions={0} | all-to-all | bytes 655360 | tf_op jit(solution)/shard_map/all_to_all | solution.py:206
  50.7 0.4 convolution_multiply_fusion.3
  51.1 0.6 fusion.26
  51.7 0.2 copy.61
  52.0 14.2 %all_to_all.51.refs_0_ = f32[32,5,4,128]{3,2,1,0:T(4,128)} all-to-all(f32[32,5,4,128]{3,2,1,0:T(4,128)S(1)} %bitcast.69), channel_id=1, replica_groups=mesh['lon'=8,'lat'=4] {'lon','lat'}, dimensions={0} | all-to-all | bytes 655360 | tf_op jit(solution)/shard_map/all_to_all | solution.py:206
  66.2 8.5 %shard_map.87.refs_1_ = f32[32,10,4,128]{3,2,1,0:T(4,128)} custom-call(f32[32,5,4,128]{3,2,1,0:T(4,128)} %all_to_all.51.refs_0_, f32[32,6,4,128]{3,2,1,0:T(4,128)} %copy-done, f32[16,2,128,128]{3,2,1,0:T(8,128)} %pad_maximum_fusion.refs_1_.refs_2_.refs_3_, s32[8,128]{1,0:T(8,128)} %add_select_fusion.refs_2_.refs_3_.refs_4_, ...), custom_call_target="tpu_custom_call" | custom-call | tf_op jit(solution)/shard_map/pallas_call | solution.py:181
  74.7 20.8 %all_to_all.52 = f32[32,10,4,128]{3,2,1,0:T(4,128)S(1)} all-to-all(f32[32,10,4,128]{3,2,1,0:T(4,128)} %shard_map.87.refs_1_), channel_id=1, replica_groups=mesh['lon'=8,'lat'=4] {'lon','lat'}, dimensions={0} | all-to-all | bytes 1310720 | tf_op jit(solution)/shard_map/all_to_all | solution.py:206
  95.5 0.4 convolution_multiply_fusion.2
  96.0 0.6 fusion.23
  96.6 0.2 copy.64
  96.8 14.6 %all_to_all.53.refs_0_ = f32[32,5,4,128]{3,2,1,0:T(4,128)} all-to-all(f32[32,5,4,128]{3,2,1,0:T(4,128)S(1)} %bitcast.70), channel_id=1, replica_groups=mesh['lon'=8,'lat'=4] {'lon','lat'}, dimensions={0} | all-to-all | bytes 655360 | tf_op jit(solution)/shard_map/all_to_all | solution.py:206
  111.4 9.1 %shard_map.88 = f32[32,11,4,128]{3,2,1,0:T(4,128)} custom-call(f32[32,5,4,128]{3,2,1,0:T(4,128)} %all_to_all.53.refs_0_, f32[32,10,4,128]{3,2,1,0:T(4,128)} %shard_map.87.refs_1_, f32[32,6,4,128]{3,2,1,0:T(4,128)} %copy-done, f32[16,2,128,128]{3,2,1,0:T(8,128)} %pad_maximum_fusion.refs_1_.refs_2_.refs_3_, s32[8,128]{1,0:T(8,128)} %add_select_fusion.refs_2_.refs_3_.refs_4_, ...), custom_call_target="tpu_custom_call" | custom-call | tf_op jit(solution)/shard_map/pallas_call | solution.py:181
  120.5 22.2 %all_to_all.54 = f32[32,11,4,128]{3,2,1,0:T(4,128)S(1)} all-to-all(f32[32,11,4,128]{3,2,1,0:T(4,128)} %shard_map.88), channel_id=1, replica_groups=mesh['lon'=8,'lat'=4] {'lon','lat'}, dimensions={0} | all-to-all | bytes 1441792 | tf_op jit(solution)/shard_map/all_to_all | solution.py:206
  142.8 0.5 convolution_multiply_fusion.1
  143.3 0.6 fusion.20
  143.9 0.9 copy.69
  144.8 3.2 %all-to-all-start.6 = ((f32[32,5,4,128]{3,2,1,0:T(4,128)}), f32[32,5,4,128]{3,2,1,0:T(4,128)S(1)}, u32[]{:S(2)}, u32[]{:S(2)}) async-start(f32[32,5,4,128]{3,2,1,0:T(4,128)} %bitcast.18), calls=%async_computation.6 | async-start | bytes 655360 | tf_op jit(solution)/shard_map/all_to_all | solution.py:206
  148.0 1.8 fusion.2.refs_1_.refs_2_
  149.9 9.7 %all-to-all-done.6.refs_0_ = f32[32,5,4,128]{3,2,1,0:T(4,128)S(1)} async-done(((f32[32,5,4,128]{3,2,1,0:T(4,128)}), f32[32,5,4,128]{3,2,1,0:T(4,128)S(1)}, u32[]{:S(2)}, u32[]{:S(2)}) %all-to-all-start.6) | async-done | bytes 327712 | tf_op jit(solution)/shard_map/all_to_all | solution.py:206
  159.6 0.7 copy-done.5
  160.3 8.5 %shard_map.89.refs_1_ = f32[32,10,4,128]{3,2,1,0:T(4,128)} custom-call(f32[32,5,4,128]{3,2,1,0:T(4,128)} %copy-done.5, f32[32,5,4,128]{3,2,1,0:T(4,128)} %fusion.2.refs_1_.refs_2_, f32[16,2,128,128]{3,2,1,0:T(8,128)} %pad_maximum_fusion.refs_1_.refs_2_.refs_3_, s32[8,128]{1,0:T(8,128)} %add_select_fusion.refs_2_.refs_3_.refs_4_, ...), custom_call_target="tpu_custom_call" | custom-call | tf_op jit(solution)/shard_map/pallas_call | solution.py:181
  168.8 20.8 %all_to_all.55 = f32[32,10,4,128]{3,2,1,0:T(4,128)S(1)} all-to-all(f32[32,10,4,128]{3,2,1,0:T(4,128)} %shard_map.89.refs_1_), channel_id=1, replica_groups=mesh['lon'=8,'lat'=4] {'lon','lat'}, dimensions={0} | all-to-all | bytes 1310720 | tf_op jit(solution)/shard_map/all_to_all | solution.py:206
  189.7 0.4 convolution_multiply_fusion
  190.1 0.6 fusion.17
  190.7 0.2 copy.72
  190.9 14.6 %all_to_all.56.refs_0_ = f32[32,5,4,128]{3,2,1,0:T(4,128)} all-to-all(f32[32,5,4,128]{3,2,1,0:T(4,128)S(1)} %bitcast.71), channel_id=1, replica_groups=mesh['lon'=8,'lat'=4] {'lon','lat'}, dimensions={0} | all-to-all | bytes 655360 | tf_op jit(solution)/shard_map/all_to_all | solution.py:206
  205.6 6.3 %shard_map.90 = f32[32,6,4,128]{3,2,1,0:T(4,128)} custom-call(f32[32,5,4,128]{3,2,1,0:T(4,128)} %all_to_all.56.refs_0_, f32[32,10,4,128]{3,2,1,0:T(4,128)} %shard_map.89.refs_1_, f32[32,5,4,128]{3,2,1,0:T(4,128)} %fusion.2.refs_1_.refs_2_, f32[16,2,128,128]{3,2,1,0:T(8,128)} %pad_maximum_fusion.refs_1_.refs_2_.refs_3_, ...), custom_call_target="tpu_custom_call" | custom-call | tf_op jit(solution)/shard_map/pallas_call | solution.py:181
  211.8 15.5 %all_to_all.57 = f32[32,6,4,128]{3,2,1,0:T(4,128)S(1)} all-to-all(f32[32,6,4,128]{3,2,1,0:T(4,128)} %shard_map.90), channel_id=1, replica_groups=mesh['lon'=8,'lat'=4] {'lon','lat'}, dimensions={0} | all-to-all | bytes 786432 | tf_op jit(solution)/shard_map/all_to_all | solution.py:206
  227.4 1.1 fusion.13
  (36 shorter events, 0.8 us)
Async XLA Ops:
  0.6 11.7 %copy-start.7 = (f32[5]{0:T(128)S(1)}, f32[5]{0:T(128)}, u32[]{:S(2)}) copy-start(f32[5]{0:T(128)} %param.12) | copy-start | bytes 64
  5.2 19.8 %all-to-all-start = ((f32[32,6,4,128]{3,2,1,0:T(4,128)}), f32[32,6,4,128]{3,2,1,0:T(4,128)S(1)}, u32[]{:S(2)}, u32[]{:S(2)}) async-start(f32[32,6,4,128]{3,2,1,0:T(4,128)} %pad_maximum_fusion.1), calls=%async_computation | async-start | bytes 786432 | tf_op jit(solution)/shard_map/all_to_all | solution.py:206
  25.0 2.9 %copy-start = (f32[32,6,4,128]{3,2,1,0:T(4,128)}, f32[32,6,4,128]{3,2,1,0:T(4,128)S(1)}, u32[]{:S(2)}) copy-start(f32[32,6,4,128]{3,2,1,0:T(4,128)S(1)} %all-to-all-done.refs_0_.refs_1_.refs_2_) | copy-start | bytes 1179652
  30.9 19.8 %copy-start.2 = (f32[137,137]{1,0:T(8,128)S(1)}, f32[137,137]{1,0:T(8,128)}, u32[]{:S(2)}) copy-start(f32[137,137]{1,0:T(8,128)} %param.13) | copy-start | bytes 225232
  30.9 19.8 %copy-start.4 = (f32[137,4,128]{2,1,0:T(4,128)S(1)}, f32[137,4,128]{2,1,0:T(4,128)}, u32[]{:S(2)}) copy-start(f32[137,4,128]{2,1,0:T(4,128)} %param.8) | copy-start | bytes 841732
  142.8 5.2 %copy-start.1 = (f32[32,6,4,128]{3,2,1,0:T(4,128)S(1)}, f32[32,6,4,128]{3,2,1,0:T(4,128)}, u32[]{:S(2)}) copy-start(f32[32,6,4,128]{3,2,1,0:T(4,128)} %copy-done) | copy-start | bytes 1179652
  142.8 5.2 %copy-start.3 = (f32[32,10,4,128]{3,2,1,0:T(4,128)S(1)}, f32[32,10,4,128]{3,2,1,0:T(4,128)}, u32[]{:S(2)}) copy-start(f32[32,10,4,128]{3,2,1,0:T(4,128)} %shard_map.87.refs_1_) | copy-start | bytes 1966084
  144.8 14.7 %all-to-all-start.6 = ((f32[32,5,4,128]{3,2,1,0:T(4,128)}), f32[32,5,4,128]{3,2,1,0:T(4,128)S(1)}, u32[]{:S(2)}, u32[]{:S(2)}) async-start(f32[32,5,4,128]{3,2,1,0:T(4,128)} %bitcast.18), calls=%async_computation.6 | async-start | bytes 655360 | tf_op jit(solution)/shard_map/all_to_all | solution.py:206
  159.6 0.7 copy-start.5
  205.6 21.9 %copy-start.6 = (f32[137,4,128]{2,1,0:T(4,128)S(1)}, f32[137,4,128]{2,1,0:T(4,128)}, u32[]{:S(2)}) copy-start(f32[137,4,128]{2,1,0:T(4,128)} %param.7) | copy-start | bytes 841732

commit v6 on v5

--- a/solution.py
+++ b/solution.py
@@ -38,7 +38,7 @@
     table = table.reshape(weights.shape[0], 3, block, block)
     half = block // 2
     outer = jnp.concatenate([table[:, 2, :half], table[:, 0, half:]], axis=1)
-    return jnp.stack([table[:, 1], outer], axis=1)
+    return jnp.concatenate([table[:, 1], outer], axis=1)
 
 
 def mirror_tables(mirror_all, block):
@@ -59,7 +59,7 @@
         outer = jnp.where(
             lane >= block // 2, prev.reshape(nb * lp, block), nxt.reshape(nb * lp, block)
         )
-        acc = _dot(mid.reshape(nb * lp, block), table_ref[j, 0]) + _dot(outer, table_ref[j, 1])
+        acc = _dot(jnp.concatenate([mid.reshape(nb * lp, block), outer], axis=1), table_ref[j])
         acc = acc.reshape(nb, lp, block)
         if add is not None:
             acc = acc + add[j]
@@ -77,8 +77,13 @@
             axis=0,
         )
         source = lax.broadcasted_iota(jnp.int32, (block, block), 0)
-        onehot = (source == index_ref[pl.ds(b, 1), :]).astype(jnp.float32)
-        out = _dot(polar.reshape(2 * depth * lp, block), onehot)
+        onehot = (source == index_ref[pl.ds(b, 1), :]).astype(jnp.bfloat16)
+        polar = polar.reshape(2 * depth * lp, block)
+        high = polar.astype(jnp.bfloat16)
+        low = (polar - high.astype(jnp.float32)).astype(jnp.bfloat16)
+        out = jnp.dot(high, onehot, preferred_element_type=jnp.float32) + jnp.dot(
+            low, onehot, preferred_element_type=jnp.float32
+        )
         mir[:, pl.ds(b, 1)] = out.reshape(2 * depth, 1, lp, block)
         return carry
 

time: 229 us -> 225 us (0.983)
  Pallas kernels: 37.6 us -> 33.4 us
    pallas_call x5, Pallas kernels: 37.6 us -> 33.4 us  [level_apply(): pl.pallas_call(functools.partial(_kernel, spec), out_shape=jax.ShapeDtype...]
where the time goes in v6:
time: 225 us; the launch traced here: 224 us
  blocking collectives  137 us (61%)
  Pallas kernels  33.4 us (15%)
  waiting for transfers between devices  20.4 us (9%)
  starting transfers between devices  10.2 us (5%)
  other arithmetic  9.76 us (4%)
  matrix products  6.82 us (3%)
  local copies, waits for them, and re-layouts  4.68 us (2%)
    all_to_all x8, blocking collectives, exchange(): return lax.all_to_all(parts, AXES, 0, 0, tiled=True)  137 us
    pallas_call x5, Pallas kernels, level_apply(): pl.pallas_call(functools.partial(_kernel, spec), out_shape=jax.ShapeDtype...  33.4 us
    all_to_all x2, waiting for transfers between devices, exchange(): return lax.all_to_all(parts, AXES, 0, 0, tiled=True)  20.4 us
    all_to_all x2, starting transfers between devices, exchange(): return lax.all_to_all(parts, AXES, 0, 0, tiled=True)  10.2 us
  transfers between devices with their start and end apart: 2, of which 2 were waited for; matrix products, arithmetic and copies ran while one was open for 1% of the time, Pallas kernels for 0%

profile of v6, /device:TPU:1, one launch (start us, length us, event | category | flops | bytes accessed | tf_op | source)
XLA Modules:
  0.0 224.2 jit_solution(8321019847870285584)
XLA Ops:
  0.6 0.8 fusion.40
  1.4 0.2 multiply_reduce_fusion
  1.6 0.1 copy.54
  1.7 0.1 sqrt_reduce_fusion
  1.8 0.8 broadcast_divide_fusion
  2.7 0.7 convert_element_type.17
  3.3 1.0 pad.13
  4.4 0.8 pad_maximum_fusion.1
  5.2 7.1 %all-to-all-start = ((f32[32,6,4,128]{3,2,1,0:T(4,128)}), f32[32,6,4,128]{3,2,1,0:T(4,128)S(1)}, u32[]{:S(2)}, u32[]{:S(2)}) async-start(f32[32,6,4,128]{3,2,1,0:T(4,128)} %pad_maximum_fusion.1), calls=%async_computation | async-start | bytes 786432 | tf_op jit(solution)/shard_map/all_to_all | solution.py:211
  12.3 0.7 multiply_reduce_fusion.1
  13.7 0.5 broadcast_divide_fusion.1.refs_3_.refs_4_.refs_5_
  14.2 0.1 subtract_abs_fusion
  14.4 10.7 %all-to-all-done.refs_0_.refs_1_.refs_2_ = f32[32,6,4,128]{3,2,1,0:T(4,128)S(1)} async-done(((f32[32,6,4,128]{3,2,1,0:T(4,128)}), f32[32,6,4,128]{3,2,1,0:T(4,128)S(1)}, u32[]{:S(2)}, u32[]{:S(2)}) %all-to-all-start) | async-done | bytes 393248 | tf_op jit(solution)/shard_map/all_to_all | solution.py:211
  25.2 2.6 %fusion = f32[16,3,128,128]{3,0,2,1:T(8,128)S(1)} fusion(s32[3,128,128]{2,1,0:T(8,128)S(1)} %subtract_abs_fusion, f32[16,33,1,1]{1,0,2,3:T(8,128)S(1)} %reshape.302), kind=kOutput, calls=%fused_computation.1 | convolution fusion | flops 313049088 | bytes 3344448 | tf_op jit(solution)/shard_map/pct,jt->jpc/dot_general | solution.py:37
  28.0 0.3 copy.103
  28.4 0.6 add_select_fusion.refs_2_.refs_3_.refs_4_
  29.0 0.3 copy_bitcast_fusion.1
  29.3 1.5 pad_maximum_fusion.refs_1_.refs_2_.refs_3_
  30.8 4.8 %shard_map.86 = f32[32,5,4,128]{3,2,1,0:T(4,128)} custom-call(f32[32,6,4,128]{3,2,1,0:T(4,128)} %copy-done, f32[16,256,128]{2,1,0:T(8,128)} %pad_maximum_fusion.refs_1_.refs_2_.refs_3_, s32[8,128]{1,0:T(8,128)} %add_select_fusion.refs_2_.refs_3_.refs_4_, f32[5]{0:T(128)} %broadcast_divide_fusion.1.refs_3_.refs_4_.refs_5_), custom_call_target="tpu_custom_call" | custom-call | tf_op jit(solution)/shard_map/pallas_call | solution.py:186
  35.6 14.5 %all_to_all.50 = f32[32,5,4,128]{3,2,1,0:T(4,128)S(1)} all-to-all(f32[32,5,4,128]{3,2,1,0:T(4,128)} %shard_map.86), channel_id=1, replica_groups=mesh['lon'=8,'lat'=4] {'lon','lat'}, dimensions={0} | all-to-all | bytes 655360 | tf_op jit(solution)/shard_map/all_to_all | solution.py:211
  50.1 0.4 convolution_multiply_fusion.3
  50.5 0.6 fusion.26
  51.1 0.2 copy.61
  51.3 14.2 %all_to_all.51.refs_0_ = f32[32,5,4,128]{3,2,1,0:T(4,128)} all-to-all(f32[32,5,4,128]{3,2,1,0:T(4,128)S(1)} %bitcast.71), channel_id=1, replica_groups=mesh['lon'=8,'lat'=4] {'lon','lat'}, dimensions={0} | all-to-all | bytes 655360 | tf_op jit(solution)/shard_map/all_to_all | solution.py:211
  65.6 7.4 %shard_map.87.refs_1_ = f32[32,10,4,128]{3,2,1,0:T(4,128)} custom-call(f32[32,5,4,128]{3,2,1,0:T(4,128)} %all_to_all.51.refs_0_, f32[32,6,4,128]{3,2,1,0:T(4,128)} %copy-done, f32[16,256,128]{2,1,0:T(8,128)} %pad_maximum_fusion.refs_1_.refs_2_.refs_3_, s32[8,128]{1,0:T(8,128)} %add_select_fusion.refs_2_.refs_3_.refs_4_, ...), custom_call_target="tpu_custom_call" | custom-call | tf_op jit(solution)/shard_map/pallas_call | solution.py:186
  73.0 20.8 %all_to_all.52 = f32[32,10,4,128]{3,2,1,0:T(4,128)S(1)} all-to-all(f32[32,10,4,128]{3,2,1,0:T(4,128)} %shard_map.87.refs_1_), channel_id=1, replica_groups=mesh['lon'=8,'lat'=4] {'lon','lat'}, dimensions={0} | all-to-all | bytes 1310720 | tf_op jit(solution)/shard_map/all_to_all | solution.py:211
  93.9 0.4 convolution_multiply_fusion.2
  94.3 0.6 fusion.23
  94.9 0.2 copy.64
  95.1 14.6 %all_to_all.53.refs_0_ = f32[32,5,4,128]{3,2,1,0:T(4,128)} all-to-all(f32[32,5,4,128]{3,2,1,0:T(4,128)S(1)} %bitcast.72), channel_id=1, replica_groups=mesh['lon'=8,'lat'=4] {'lon','lat'}, dimensions={0} | all-to-all | bytes 655360 | tf_op jit(solution)/shard_map/all_to_all | solution.py:211
  109.8 8.0 %shard_map.88 = f32[32,11,4,128]{3,2,1,0:T(4,128)} custom-call(f32[32,5,4,128]{3,2,1,0:T(4,128)} %all_to_all.53.refs_0_, f32[32,10,4,128]{3,2,1,0:T(4,128)} %shard_map.87.refs_1_, f32[32,6,4,128]{3,2,1,0:T(4,128)} %copy-done, f32[16,256,128]{2,1,0:T(8,128)} %pad_maximum_fusion.refs_1_.refs_2_.refs_3_, s32[8,128]{1,0:T(8,128)} %add_select_fusion.refs_2_.refs_3_.refs_4_, ...), custom_call_target="tpu_custom_call" | custom-call | tf_op jit(solution)/shard_map/pallas_call | solution.py:186
  117.8 22.2 %all_to_all.54 = f32[32,11,4,128]{3,2,1,0:T(4,128)S(1)} all-to-all(f32[32,11,4,128]{3,2,1,0:T(4,128)} %shard_map.88), channel_id=1, replica_groups=mesh['lon'=8,'lat'=4] {'lon','lat'}, dimensions={0} | all-to-all | bytes 1441792 | tf_op jit(solution)/shard_map/all_to_all | solution.py:211
  140.1 0.5 convolution_multiply_fusion.1
  140.6 0.6 fusion.20
  141.2 0.9 copy.69
  142.1 3.2 %all-to-all-start.6 = ((f32[32,5,4,128]{3,2,1,0:T(4,128)}), f32[32,5,4,128]{3,2,1,0:T(4,128)S(1)}, u32[]{:S(2)}, u32[]{:S(2)}) async-start(f32[32,5,4,128]{3,2,1,0:T(4,128)} %bitcast.18), calls=%async_computation.6 | async-start | bytes 655360 | tf_op jit(solution)/shard_map/all_to_all | solution.py:211
  145.3 1.8 fusion.2.refs_1_.refs_2_
  147.2 9.7 %all-to-all-done.6.refs_0_ = f32[32,5,4,128]{3,2,1,0:T(4,128)S(1)} async-done(((f32[32,5,4,128]{3,2,1,0:T(4,128)}), f32[32,5,4,128]{3,2,1,0:T(4,128)S(1)}, u32[]{:S(2)}, u32[]{:S(2)}) %all-to-all-start.6) | async-done | bytes 327712 | tf_op jit(solution)/shard_map/all_to_all | solution.py:211
  156.9 0.7 copy-done.5
  157.6 7.4 %shard_map.89.refs_1_ = f32[32,10,4,128]{3,2,1,0:T(4,128)} custom-call(f32[32,5,4,128]{3,2,1,0:T(4,128)} %copy-done.5, f32[32,5,4,128]{3,2,1,0:T(4,128)} %fusion.2.refs_1_.refs_2_, f32[16,256,128]{2,1,0:T(8,128)} %pad_maximum_fusion.refs_1_.refs_2_.refs_3_, s32[8,128]{1,0:T(8,128)} %add_select_fusion.refs_2_.refs_3_.refs_4_, ...), custom_call_target="tpu_custom_call" | custom-call | tf_op jit(solution)/shard_map/pallas_call | solution.py:186
  165.0 20.8 %all_to_all.55 = f32[32,10,4,128]{3,2,1,0:T(4,128)S(1)} all-to-all(f32[32,10,4,128]{3,2,1,0:T(4,128)} %shard_map.89.refs_1_), channel_id=1, replica_groups=mesh['lon'=8,'lat'=4] {'lon','lat'}, dimensions={0} | all-to-all | bytes 1310720 | tf_op jit(solution)/shard_map/all_to_all | solution.py:211
  185.9 0.4 convolution_multiply_fusion
  186.3 0.6 fusion.17
  186.9 0.2 copy.72
  187.2 14.6 %all_to_all.56.refs_0_ = f32[32,5,4,128]{3,2,1,0:T(4,128)} all-to-all(f32[32,5,4,128]{3,2,1,0:T(4,128)S(1)} %bitcast.73), channel_id=1, replica_groups=mesh['lon'=8,'lat'=4] {'lon','lat'}, dimensions={0} | all-to-all | bytes 655360 | tf_op jit(solution)/shard_map/all_to_all | solution.py:211
  201.8 5.7 %shard_map.90 = f32[32,6,4,128]{3,2,1,0:T(4,128)} custom-call(f32[32,5,4,128]{3,2,1,0:T(4,128)} %all_to_all.56.refs_0_, f32[32,10,4,128]{3,2,1,0:T(4,128)} %shard_map.89.refs_1_, f32[32,5,4,128]{3,2,1,0:T(4,128)} %fusion.2.refs_1_.refs_2_, f32[16,256,128]{2,1,0:T(8,128)} %pad_maximum_fusion.refs_1_.refs_2_.refs_3_, ...), custom_call_target="tpu_custom_call" | custom-call | tf_op jit(solution)/shard_map/pallas_call | solution.py:186
  207.5 15.5 %all_to_all.57 = f32[32,6,4,128]{3,2,1,0:T(4,128)S(1)} all-to-all(f32[32,6,4,128]{3,2,1,0:T(4,128)} %shard_map.90), channel_id=1, replica_groups=mesh['lon'=8,'lat'=4] {'lon','lat'}, dimensions={0} | all-to-all | bytes 786432 | tf_op jit(solution)/shard_map/all_to_all | solution.py:211
  223.1 1.1 fusion.13
  (35 shorter events, 0.7 us)
Async XLA Ops:
  0.6 11.7 %copy-start.7 = (f32[5]{0:T(128)S(1)}, f32[5]{0:T(128)}, u32[]{:S(2)}) copy-start(f32[5]{0:T(128)} %param.12) | copy-start | bytes 64
  5.2 19.8 %all-to-all-start = ((f32[32,6,4,128]{3,2,1,0:T(4,128)}), f32[32,6,4,128]{3,2,1,0:T(4,128)S(1)}, u32[]{:S(2)}, u32[]{:S(2)}) async-start(f32[32,6,4,128]{3,2,1,0:T(4,128)} %pad_maximum_fusion.1), calls=%async_computation | async-start | bytes 786432 | tf_op jit(solution)/shard_map/all_to_all | solution.py:211
  25.0 2.9 %copy-start = (f32[32,6,4,128]{3,2,1,0:T(4,128)}, f32[32,6,4,128]{3,2,1,0:T(4,128)S(1)}, u32[]{:S(2)}) copy-start(f32[32,6,4,128]{3,2,1,0:T(4,128)S(1)} %all-to-all-done.refs_0_.refs_1_.refs_2_) | copy-start | bytes 1179652
  30.8 19.3 %copy-start.2 = (f32[137,137]{1,0:T(8,128)S(1)}, f32[137,137]{1,0:T(8,128)}, u32[]{:S(2)}) copy-start(f32[137,137]{1,0:T(8,128)} %param.13) | copy-start | bytes 225232
  30.8 19.3 %copy-start.4 = (f32[137,4,128]{2,1,0:T(4,128)S(1)}, f32[137,4,128]{2,1,0:T(4,128)}, u32[]{:S(2)}) copy-start(f32[137,4,128]{2,1,0:T(4,128)} %param.8) | copy-start | bytes 841732
  140.1 5.2 %copy-start.1 = (f32[32,6,4,128]{3,2,1,0:T(4,128)S(1)}, f32[32,6,4,128]{3,2,1,0:T(4,128)}, u32[]{:S(2)}) copy-start(f32[32,6,4,128]{3,2,1,0:T(4,128)} %copy-done) | copy-start | bytes 1179652
  140.1 5.2 %copy-start.3 = (f32[32,10,4,128]{3,2,1,0:T(4,128)S(1)}, f32[32,10,4,128]{3,2,1,0:T(4,128)}, u32[]{:S(2)}) copy-start(f32[32,10,4,128]{3,2,1,0:T(4,128)} %shard_map.87.refs_1_) | copy-start | bytes 1966084
  142.1 14.7 %all-to-all-start.6 = ((f32[32,5,4,128]{3,2,1,0:T(4,128)}), f32[32,5,4,128]{3,2,1,0:T(4,128)S(1)}, u32[]{:S(2)}, u32[]{:S(2)}) async-start(f32[32,5,4,128]{3,2,1,0:T(4,128)} %bitcast.18), calls=%async_computation.6 | async-start | bytes 655360 | tf_op jit(solution)/shard_map/all_to_all | solution.py:211
  156.9 0.7 copy-start.5
  201.8 21.3 %copy-start.6 = (f32[137,4,128]{2,1,0:T(4,128)S(1)}, f32[137,4,128]{2,1,0:T(4,128)}, u32[]{:S(2)}) copy-start(f32[137,4,128]{2,1,0:T(4,128)} %param.7) | copy-start | bytes 841732

commit v7 on v6

--- a/solution.py
+++ b/solution.py
@@ -87,7 +87,7 @@
         mir[:, pl.ds(b, 1)] = out.reshape(2 * depth, 1, lp, block)
         return carry
 
-    lax.fori_loop(0, nb, mirror_block, 0)
+    lax.fori_loop(0, nb, mirror_block, 0, unroll=nb <= 16)
 
     def row(k):
         if k < 0:
@@ -115,7 +115,7 @@
                     dst[a * rl + r, pl.ds(b, 1), pl.ds(lev, 1), :] = tile[r : r + 1].reshape(1, 1, -1)
         return carry
 
-    lax.fori_loop(0, nb, one_block, 0)
+    lax.fori_loop(0, nb, one_block, 0, unroll=nb <= 16)
 
 
 def _pack(src, parts_ref, off, n_lat, per):
@@ -132,7 +132,7 @@
                 parts_ref[b * n_lat + a, off + lev] = tile
         return carry
 
-    lax.fori_loop(0, nb, one_block, 0)
+    lax.fori_loop(0, nb, one_block, 0, unroll=nb <= 16)
 
 
 def _kernel(spec, *refs):

time: 225 us -> 216 us (0.960)
  Pallas kernels: 33.4 us -> 24.6 us
    pallas_call x5, Pallas kernels: 33.4 us -> 24.6 us  [level_apply(): pl.pallas_call(functools.partial(_kernel, spec), out_shape=jax.ShapeDtype...]
where the time goes in v7:
time: 216 us; the launch traced here: 215 us
  blocking collectives  137 us (63%)
  Pallas kernels  24.6 us (11%)
  waiting for transfers between devices  20.4 us (9%)
  starting transfers between devices  10.3 us (5%)
  other arithmetic  9.76 us (5%)
  matrix products  6.82 us (3%)
  local copies, waits for them, and re-layouts  4.68 us (2%)
    all_to_all x8, blocking collectives, exchange(): return lax.all_to_all(parts, AXES, 0, 0, tiled=True)  137 us
    pallas_call x5, Pallas kernels, level_apply(): pl.pallas_call(functools.partial(_kernel, spec), out_shape=jax.ShapeDtype...  24.6 us
    all_to_all x2, waiting for transfers between devices, exchange(): return lax.all_to_all(parts, AXES, 0, 0, tiled=True)  20.4 us
    all_to_all x2, starting transfers between devices, exchange(): return lax.all_to_all(parts, AXES, 0, 0, tiled=True)  10.3 us
  transfers between devices with their start and end apart: 2, of which 2 were waited for; matrix products, arithmetic and copies ran while one was open for 1% of the time, Pallas kernels for 0%

profile of v7, /device:TPU:1, one launch (start us, length us, event | category | flops | bytes accessed | tf_op | source)
XLA Modules:
  0.0 215.4 jit_solution(11386556697090164536)
XLA Ops:
  0.6 0.8 fusion.40
  1.4 0.2 multiply_reduce_fusion
  1.6 0.1 copy.54
  1.7 0.1 sqrt_reduce_fusion
  1.8 0.8 broadcast_divide_fusion
  2.7 0.7 convert_element_type.17
  3.3 1.0 pad.13
  4.4 0.8 pad_maximum_fusion.1
  5.2 7.1 %all-to-all-start = ((f32[32,6,4,128]{3,2,1,0:T(4,128)}), f32[32,6,4,128]{3,2,1,0:T(4,128)S(1)}, u32[]{:S(2)}, u32[]{:S(2)}) async-start(f32[32,6,4,128]{3,2,1,0:T(4,128)} %pad_maximum_fusion.1), calls=%async_computation | async-start | bytes 786432 | tf_op jit(solution)/shard_map/all_to_all | solution.py:211
  12.3 0.7 multiply_reduce_fusion.1
  13.7 0.5 broadcast_divide_fusion.1.refs_3_.refs_4_.refs_5_
  14.2 0.1 subtract_abs_fusion
  14.4 10.7 %all-to-all-done.refs_0_.refs_1_.refs_2_ = f32[32,6,4,128]{3,2,1,0:T(4,128)S(1)} async-done(((f32[32,6,4,128]{3,2,1,0:T(4,128)}), f32[32,6,4,128]{3,2,1,0:T(4,128)S(1)}, u32[]{:S(2)}, u32[]{:S(2)}) %all-to-all-start) | async-done | bytes 393248 | tf_op jit(solution)/shard_map/all_to_all | solution.py:211
  25.2 2.6 %fusion = f32[16,3,128,128]{3,0,2,1:T(8,128)S(1)} fusion(s32[3,128,128]{2,1,0:T(8,128)S(1)} %subtract_abs_fusion, f32[16,33,1,1]{1,0,2,3:T(8,128)S(1)} %reshape.302), kind=kOutput, calls=%fused_computation.1 | convolution fusion | flops 313049088 | bytes 3344448 | tf_op jit(solution)/shard_map/pct,jt->jpc/dot_general | solution.py:37
  28.0 0.3 copy.103
  28.4 0.6 add_select_fusion.refs_2_.refs_3_.refs_4_
  29.0 0.3 copy_bitcast_fusion.1
  29.3 1.5 pad_maximum_fusion.refs_1_.refs_2_.refs_3_
  30.8 3.7 %shard_map.86 = f32[32,5,4,128]{3,2,1,0:T(4,128)} custom-call(f32[32,6,4,128]{3,2,1,0:T(4,128)} %copy-done, f32[16,256,128]{2,1,0:T(8,128)} %pad_maximum_fusion.refs_1_.refs_2_.refs_3_, s32[8,128]{1,0:T(8,128)} %add_select_fusion.refs_2_.refs_3_.refs_4_, f32[5]{0:T(128)} %broadcast_divide_fusion.1.refs_3_.refs_4_.refs_5_), custom_call_target="tpu_custom_call" | custom-call | tf_op jit(solution)/shard_map/pallas_call | solution.py:186
  34.5 14.5 %all_to_all.50 = f32[32,5,4,128]{3,2,1,0:T(4,128)S(1)} all-to-all(f32[32,5,4,128]{3,2,1,0:T(4,128)} %shard_map.86), channel_id=1, replica_groups=mesh['lon'=8,'lat'=4] {'lon','lat'}, dimensions={0} | all-to-all | bytes 655360 | tf_op jit(solution)/shard_map/all_to_all | solution.py:211
  49.0 0.4 convolution_multiply_fusion.3
  49.5 0.6 fusion.26
  50.1 0.2 copy.61
  50.3 14.2 %all_to_all.51.refs_0_ = f32[32,5,4,128]{3,2,1,0:T(4,128)} all-to-all(f32[32,5,4,128]{3,2,1,0:T(4,128)S(1)} %bitcast.71), channel_id=1, replica_groups=mesh['lon'=8,'lat'=4] {'lon','lat'}, dimensions={0} | all-to-all | bytes 655360 | tf_op jit(solution)/shard_map/all_to_all | solution.py:211
  64.5 5.3 %shard_map.87.refs_1_ = f32[32,10,4,128]{3,2,1,0:T(4,128)} custom-call(f32[32,5,4,128]{3,2,1,0:T(4,128)} %all_to_all.51.refs_0_, f32[32,6,4,128]{3,2,1,0:T(4,128)} %copy-done, f32[16,256,128]{2,1,0:T(8,128)} %pad_maximum_fusion.refs_1_.refs_2_.refs_3_, s32[8,128]{1,0:T(8,128)} %add_select_fusion.refs_2_.refs_3_.refs_4_, ...), custom_call_target="tpu_custom_call" | custom-call | tf_op jit(solution)/shard_map/pallas_call | solution.py:186
  69.8 20.8 %all_to_all.52 = f32[32,10,4,128]{3,2,1,0:T(4,128)S(1)} all-to-all(f32[32,10,4,128]{3,2,1,0:T(4,128)} %shard_map.87.refs_1_), channel_id=1, replica_groups=mesh['lon'=8,'lat'=4] {'lon','lat'}, dimensions={0} | all-to-all | bytes 1310720 | tf_op jit(solution)/shard_map/all_to_all | solution.py:211
  90.7 0.4 convolution_multiply_fusion.2
  91.1 0.6 fusion.23
  91.7 0.2 copy.64
  91.9 14.6 %all_to_all.53.refs_0_ = f32[32,5,4,128]{3,2,1,0:T(4,128)} all-to-all(f32[32,5,4,128]{3,2,1,0:T(4,128)S(1)} %bitcast.72), channel_id=1, replica_groups=mesh['lon'=8,'lat'=4] {'lon','lat'}, dimensions={0} | all-to-all | bytes 655360 | tf_op jit(solution)/shard_map/all_to_all | solution.py:211
  106.6 5.8 %shard_map.88 = f32[32,11,4,128]{3,2,1,0:T(4,128)} custom-call(f32[32,5,4,128]{3,2,1,0:T(4,128)} %all_to_all.53.refs_0_, f32[32,10,4,128]{3,2,1,0:T(4,128)} %shard_map.87.refs_1_, f32[32,6,4,128]{3,2,1,0:T(4,128)} %copy-done, f32[16,256,128]{2,1,0:T(8,128)} %pad_maximum_fusion.refs_1_.refs_2_.refs_3_, s32[8,128]{1,0:T(8,128)} %add_select_fusion.refs_2_.refs_3_.refs_4_, ...), custom_call_target="tpu_custom_call" | custom-call | tf_op jit(solution)/shard_map/pallas_call | solution.py:186
  112.4 22.2 %all_to_all.54 = f32[32,11,4,128]{3,2,1,0:T(4,128)S(1)} all-to-all(f32[32,11,4,128]{3,2,1,0:T(4,128)} %shard_map.88), channel_id=1, replica_groups=mesh['lon'=8,'lat'=4] {'lon','lat'}, dimensions={0} | all-to-all | bytes 1441792 | tf_op jit(solution)/shard_map/all_to_all | solution.py:211
  134.7 0.5 convolution_multiply_fusion.1
  135.2 0.6 fusion.20
  135.8 0.9 copy.69
  136.7 3.2 %all-to-all-start.6 = ((f32[32,5,4,128]{3,2,1,0:T(4,128)}), f32[32,5,4,128]{3,2,1,0:T(4,128)S(1)}, u32[]{:S(2)}, u32[]{:S(2)}) async-start(f32[32,5,4,128]{3,2,1,0:T(4,128)} %bitcast.18), calls=%async_computation.6 | async-start | bytes 655360 | tf_op jit(solution)/shard_map/all_to_all | solution.py:211
  139.9 1.8 fusion.2.refs_1_.refs_2_
  141.7 9.7 %all-to-all-done.6.refs_0_ = f32[32,5,4,128]{3,2,1,0:T(4,128)S(1)} async-done(((f32[32,5,4,128]{3,2,1,0:T(4,128)}), f32[32,5,4,128]{3,2,1,0:T(4,128)S(1)}, u32[]{:S(2)}, u32[]{:S(2)}) %all-to-all-start.6) | async-done | bytes 327712 | tf_op jit(solution)/shard_map/all_to_all | solution.py:211
  151.4 0.7 copy-done.5
  152.2 5.3 %shard_map.89.refs_1_ = f32[32,10,4,128]{3,2,1,0:T(4,128)} custom-call(f32[32,5,4,128]{3,2,1,0:T(4,128)} %copy-done.5, f32[32,5,4,128]{3,2,1,0:T(4,128)} %fusion.2.refs_1_.refs_2_, f32[16,256,128]{2,1,0:T(8,128)} %pad_maximum_fusion.refs_1_.refs_2_.refs_3_, s32[8,128]{1,0:T(8,128)} %add_select_fusion.refs_2_.refs_3_.refs_4_, ...), custom_call_target="tpu_custom_call" | custom-call | tf_op jit(solution)/shard_map/pallas_call | solution.py:186
  157.4 20.8 %all_to_all.55 = f32[32,10,4,128]{3,2,1,0:T(4,128)S(1)} all-to-all(f32[32,10,4,128]{3,2,1,0:T(4,128)} %shard_map.89.refs_1_), channel_id=1, replica_groups=mesh['lon'=8,'lat'=4] {'lon','lat'}, dimensions={0} | all-to-all | bytes 1310720 | tf_op jit(solution)/shard_map/all_to_all | solution.py:211
  178.3 0.4 convolution_multiply_fusion
  178.8 0.6 fusion.17
  179.4 0.2 copy.72
  179.6 14.6 %all_to_all.56.refs_0_ = f32[32,5,4,128]{3,2,1,0:T(4,128)} all-to-all(f32[32,5,4,128]{3,2,1,0:T(4,128)S(1)} %bitcast.73), channel_id=1, replica_groups=mesh['lon'=8,'lat'=4] {'lon','lat'}, dimensions={0} | all-to-all | bytes 655360 | tf_op jit(solution)/shard_map/all_to_all | solution.py:211
  194.2 4.5 %shard_map.90 = f32[32,6,4,128]{3,2,1,0:T(4,128)} custom-call(f32[32,5,4,128]{3,2,1,0:T(4,128)} %all_to_all.56.refs_0_, f32[32,10,4,128]{3,2,1,0:T(4,128)} %shard_map.89.refs_1_, f32[32,5,4,128]{3,2,1,0:T(4,128)} %fusion.2.refs_1_.refs_2_, f32[16,256,128]{2,1,0:T(8,128)} %pad_maximum_fusion.refs_1_.refs_2_.refs_3_, ...), custom_call_target="tpu_custom_call" | custom-call | tf_op jit(solution)/shard_map/pallas_call | solution.py:186
  198.7 15.5 %all_to_all.57 = f32[32,6,4,128]{3,2,1,0:T(4,128)S(1)} all-to-all(f32[32,6,4,128]{3,2,1,0:T(4,128)} %shard_map.90), channel_id=1, replica_groups=mesh['lon'=8,'lat'=4] {'lon','lat'}, dimensions={0} | all-to-all | bytes 786432 | tf_op jit(solution)/shard_map/all_to_all | solution.py:211
  214.3 1.1 fusion.13
  (35 shorter events, 0.7 us)
Async XLA Ops:
  0.6 11.7 %copy-start.7 = (f32[5]{0:T(128)S(1)}, f32[5]{0:T(128)}, u32[]{:S(2)}) copy-start(f32[5]{0:T(128)} %param.12) | copy-start | bytes 64
  5.2 19.8 %all-to-all-start = ((f32[32,6,4,128]{3,2,1,0:T(4,128)}), f32[32,6,4,128]{3,2,1,0:T(4,128)S(1)}, u32[]{:S(2)}, u32[]{:S(2)}) async-start(f32[32,6,4,128]{3,2,1,0:T(4,128)} %pad_maximum_fusion.1), calls=%async_computation | async-start | bytes 786432 | tf_op jit(solution)/shard_map/all_to_all | solution.py:211
  25.0 2.9 %copy-start = (f32[32,6,4,128]{3,2,1,0:T(4,128)}, f32[32,6,4,128]{3,2,1,0:T(4,128)S(1)}, u32[]{:S(2)}) copy-start(f32[32,6,4,128]{3,2,1,0:T(4,128)S(1)} %all-to-all-done.refs_0_.refs_1_.refs_2_) | copy-start | bytes 1179652
  30.8 18.3 %copy-start.2 = (f32[137,137]{1,0:T(8,128)S(1)}, f32[137,137]{1,0:T(8,128)}, u32[]{:S(2)}) copy-start(f32[137,137]{1,0:T(8,128)} %param.13) | copy-start | bytes 225232
  30.8 18.3 %copy-start.4 = (f32[137,4,128]{2,1,0:T(4,128)S(1)}, f32[137,4,128]{2,1,0:T(4,128)}, u32[]{:S(2)}) copy-start(f32[137,4,128]{2,1,0:T(4,128)} %param.8) | copy-start | bytes 841732
  134.7 5.2 %copy-start.1 = (f32[32,6,4,128]{3,2,1,0:T(4,128)S(1)}, f32[32,6,4,128]{3,2,1,0:T(4,128)}, u32[]{:S(2)}) copy-start(f32[32,6,4,128]{3,2,1,0:T(4,128)} %copy-done) | copy-start | bytes 1179652
  134.7 5.2 %copy-start.3 = (f32[32,10,4,128]{3,2,1,0:T(4,128)S(1)}, f32[32,10,4,128]{3,2,1,0:T(4,128)}, u32[]{:S(2)}) copy-start(f32[32,10,4,128]{3,2,1,0:T(4,128)} %shard_map.87.refs_1_) | copy-start | bytes 1966084
  136.7 14.7 %all-to-all-start.6 = ((f32[32,5,4,128]{3,2,1,0:T(4,128)}), f32[32,5,4,128]{3,2,1,0:T(4,128)S(1)}, u32[]{:S(2)}, u32[]{:S(2)}) async-start(f32[32,5,4,128]{3,2,1,0:T(4,128)} %bitcast.18), calls=%async_computation.6 | async-start | bytes 655360 | tf_op jit(solution)/shard_map/all_to_all | solution.py:211
  151.4 0.7 copy-start.5
  194.2 20.1 %copy-start.6 = (f32[137,4,128]{2,1,0:T(4,128)S(1)}, f32[137,4,128]{2,1,0:T(4,128)}, u32[]{:S(2)}) copy-start(f32[137,4,128]{2,1,0:T(4,128)} %param.7) | copy-start | bytes 841732

commit v8 on v7

--- a/solution.py
+++ b/solution.py
@@ -29,16 +29,14 @@
 
 def zonal_tables(weights, block):
     width = weights.shape[1] - 1
-    positions = jnp.arange(3 * block, dtype=jnp.int32)
+    source = jnp.arange(2 * block, dtype=jnp.int32)
+    lane = source % block
+    shift = jnp.where(source < block, 0, jnp.where(lane < block // 2, block, -block))
     columns = jnp.arange(block, dtype=jnp.int32)
     tap_ids = jnp.arange(width + 1, dtype=jnp.int32)
-    distance = jnp.abs(positions[:, None] - block - columns[None, :])
+    distance = jnp.abs((lane + shift)[:, None] - columns[None, :])
     selector = (distance[:, :, None] == tap_ids[None, None, :]).astype(jnp.float32)
-    table = jnp.einsum("pct,jt->jpc", selector, weights, precision=HI)
-    table = table.reshape(weights.shape[0], 3, block, block)
-    half = block // 2
-    outer = jnp.concatenate([table[:, 2, :half], table[:, 0, half:]], axis=1)
-    return jnp.concatenate([table[:, 1], outer], axis=1)
+    return jnp.einsum("pct,jt->jpc", selector, weights, precision=HI)
 
 
 def mirror_tables(mirror_all, block):
@@ -261,8 +259,10 @@
         )
 
     def middle(y):
-        lifted = jnp.einsum("kl,lji->kji", vertical_pad, y, precision=HI)
-        return jnp.einsum("lk,lji->kji", vertical_pad, obs_weight * lifted, precision=HI)
+        lifted = jnp.einsum("kl,lji->kji", vertical_pad, y, precision=KERNEL_PRECISION)
+        return jnp.einsum(
+            "lk,lji->kji", vertical_pad, obs_weight * lifted, precision=KERNEL_PRECISION
+        )
 
     def lowered(px_col):
         return exchange(col_parts(middle(px_col)))

time: 216 us -> 214 us (level)
  matrix products: 6.82 us -> 4.62 us
    dot_general x9, matrix products: 6.82 us -> 4.62 us  [the longest x1 1.83 us: zonal_tables(): return jnp.einsum('pct,jt->jpc', selector, weights, precision=HI)]
where the time goes in v8:
time: 214 us; the launch traced here: 213 us
  blocking collectives  137 us (64%)
  Pallas kernels  24.5 us (11%)
  waiting for transfers between devices  20.4 us (10%)
  starting transfers between devices  10.2 us (5%)
  other arithmetic  8.27 us (4%)
  local copies, waits for them, and re-layouts  5.86 us (3%)
  matrix products  4.62 us (2%)
    all_to_all x8, blocking collectives, exchange(): return lax.all_to_all(parts, AXES, 0, 0, tiled=True)  137 us
    pallas_call x5, Pallas kernels, level_apply(): pl.pallas_call(functools.partial(_kernel, spec), out_shape=jax.ShapeDtype...  24.5 us
    all_to_all x2, waiting for transfers between devices, exchange(): return lax.all_to_all(parts, AXES, 0, 0, tiled=True)  20.4 us
    all_to_all x2, starting transfers between devices, exchange(): return lax.all_to_all(parts, AXES, 0, 0, tiled=True)  10.2 us
  transfers between devices with their start and end apart: 2, of which 2 were waited for; matrix products, arithmetic and copies ran while one was open for 1% of the time, Pallas kernels for 0%

profile of v8, /device:TPU:1, one launch (start us, length us, event | category | flops | bytes accessed | tf_op | source)
XLA Modules:
  0.0 212.8 jit_solution(13497835847540792024)
XLA Ops:
  0.6 0.8 fusion.39
  1.4 0.2 multiply_reduce_fusion
  1.6 0.1 copy.60
  1.7 0.1 sqrt_reduce_fusion
  1.8 0.8 broadcast_divide_fusion
  2.6 0.1 reshape.291
  2.7 0.7 convert_element_type.17
  3.3 1.0 pad.13
  4.4 0.8 pad_maximum_fusion
  5.2 7.1 %all-to-all-start = ((f32[32,6,4,128]{3,2,1,0:T(4,128)}), f32[32,6,4,128]{3,2,1,0:T(4,128)S(1)}, u32[]{:S(2)}, u32[]{:S(2)}) async-start(f32[32,6,4,128]{3,2,1,0:T(4,128)} %pad_maximum_fusion), calls=%async_computation | async-start | bytes 786432 | tf_op jit(solution)/shard_map/all_to_all | solution.py:209
  12.4 0.7 multiply_reduce_fusion.1
  13.7 0.5 broadcast_divide_fusion.1.refs_3_.refs_4_.refs_5_
  14.3 0.1 subtract_abs_fusion
  14.4 10.7 %all-to-all-done.refs_0_.refs_1_.refs_2_ = f32[32,6,4,128]{3,2,1,0:T(4,128)S(1)} async-done(((f32[32,6,4,128]{3,2,1,0:T(4,128)}), f32[32,6,4,128]{3,2,1,0:T(4,128)S(1)}, u32[]{:S(2)}, u32[]{:S(2)}) %all-to-all-start) | async-done | bytes 393248 | tf_op jit(solution)/shard_map/all_to_all | solution.py:209
  25.1 0.1 reshape.305
  25.2 1.8 fusion
  27.1 2.0 copy.62.refs_1_.refs_2_.refs_3_
  29.0 0.6 add_select_fusion.refs_2_.refs_3_.refs_4_
  29.6 3.7 %shard_map.86 = f32[32,5,4,128]{3,2,1,0:T(4,128)} custom-call(f32[32,6,4,128]{3,2,1,0:T(4,128)} %copy-done, f32[16,256,128]{2,1,0:T(8,128)} %copy.62.refs_1_.refs_2_.refs_3_, s32[8,128]{1,0:T(8,128)} %add_select_fusion.refs_2_.refs_3_.refs_4_, f32[5]{0:T(128)} %broadcast_divide_fusion.1.refs_3_.refs_4_.refs_5_), custom_call_target="tpu_custom_call" | custom-call | tf_op jit(solution)/shard_map/pallas_call | solution.py:184
  33.3 14.5 %all_to_all.50 = f32[32,5,4,128]{3,2,1,0:T(4,128)S(1)} all-to-all(f32[32,5,4,128]{3,2,1,0:T(4,128)} %shard_map.86), channel_id=1, replica_groups=mesh['lon'=8,'lat'=4] {'lon','lat'}, dimensions={0} | all-to-all | bytes 655360 | tf_op jit(solution)/shard_map/all_to_all | solution.py:209
  47.8 0.3 convolution_multiply_fusion.3
  48.1 0.4 fusion.26
  48.5 0.2 copy.65
  48.8 14.2 %all_to_all.51.refs_0_ = f32[32,5,4,128]{3,2,1,0:T(4,128)} all-to-all(f32[32,5,4,128]{3,2,1,0:T(4,128)S(1)} %bitcast.61), channel_id=1, replica_groups=mesh['lon'=8,'lat'=4] {'lon','lat'}, dimensions={0} | all-to-all | bytes 655360 | tf_op jit(solution)/shard_map/all_to_all | solution.py:209
  63.0 5.3 %shard_map.87.refs_1_ = f32[32,10,4,128]{3,2,1,0:T(4,128)} custom-call(f32[32,5,4,128]{3,2,1,0:T(4,128)} %all_to_all.51.refs_0_, f32[32,6,4,128]{3,2,1,0:T(4,128)} %copy-done, f32[16,256,128]{2,1,0:T(8,128)} %copy.62.refs_1_.refs_2_.refs_3_, s32[8,128]{1,0:T(8,128)} %add_select_fusion.refs_2_.refs_3_.refs_4_, f32[5]{0:T(128)} %broadcast_divide_fusion.1.refs_3_.refs_4_.refs_5_), custom_call_target="tpu_custom_call" | custom-call | tf_op jit(solution)/shard_map/pallas_call | solution.py:184
  68.2 20.8 %all_to_all.52 = f32[32,10,4,128]{3,2,1,0:T(4,128)S(1)} all-to-all(f32[32,10,4,128]{3,2,1,0:T(4,128)} %shard_map.87.refs_1_), channel_id=1, replica_groups=mesh['lon'=8,'lat'=4] {'lon','lat'}, dimensions={0} | all-to-all | bytes 1310720 | tf_op jit(solution)/shard_map/all_to_all | solution.py:209
  89.1 0.3 convolution_multiply_fusion.2
  89.4 0.4 fusion.23
  89.8 0.2 copy.69
  90.0 14.6 %all_to_all.53.refs_0_ = f32[32,5,4,128]{3,2,1,0:T(4,128)} all-to-all(f32[32,5,4,128]{3,2,1,0:T(4,128)S(1)} %bitcast.62), channel_id=1, replica_groups=mesh['lon'=8,'lat'=4] {'lon','lat'}, dimensions={0} | all-to-all | bytes 655360 | tf_op jit(solution)/shard_map/all_to_all | solution.py:209
  104.7 5.8 %shard_map.88 = f32[32,11,4,128]{3,2,1,0:T(4,128)} custom-call(f32[32,5,4,128]{3,2,1,0:T(4,128)} %all_to_all.53.refs_0_, f32[32,10,4,128]{3,2,1,0:T(4,128)} %shard_map.87.refs_1_, f32[32,6,4,128]{3,2,1,0:T(4,128)} %copy-done, f32[16,256,128]{2,1,0:T(8,128)} %copy.62.refs_1_.refs_2_.refs_3_, s32[8,128]{1,0:T(8,128)} %add_select_fusion.refs_2_.refs_3_.refs_4_, ...), custom_call_target="tpu_custom_call" | custom-call | tf_op jit(solution)/shard_map/pallas_call | solution.py:184
  110.5 22.2 %all_to_all.54 = f32[32,11,4,128]{3,2,1,0:T(4,128)S(1)} all-to-all(f32[32,11,4,128]{3,2,1,0:T(4,128)} %shard_map.88), channel_id=1, replica_groups=mesh['lon'=8,'lat'=4] {'lon','lat'}, dimensions={0} | all-to-all | bytes 1441792 | tf_op jit(solution)/shard_map/all_to_all | solution.py:209
  132.8 0.3 convolution_multiply_fusion.1
  133.1 0.4 fusion.20
  133.5 0.9 copy.75
  134.5 3.2 %all-to-all-start.6 = ((f32[32,5,4,128]{3,2,1,0:T(4,128)}), f32[32,5,4,128]{3,2,1,0:T(4,128)S(1)}, u32[]{:S(2)}, u32[]{:S(2)}) async-start(f32[32,5,4,128]{3,2,1,0:T(4,128)} %bitcast.14), calls=%async_computation.6 | async-start | bytes 655360 | tf_op jit(solution)/shard_map/all_to_all | solution.py:209
  137.7 1.8 fusion.2.refs_1_.refs_2_
  139.5 9.7 %all-to-all-done.6.refs_0_ = f32[32,5,4,128]{3,2,1,0:T(4,128)S(1)} async-done(((f32[32,5,4,128]{3,2,1,0:T(4,128)}), f32[32,5,4,128]{3,2,1,0:T(4,128)S(1)}, u32[]{:S(2)}, u32[]{:S(2)}) %all-to-all-start.6) | async-done | bytes 327712 | tf_op jit(solution)/shard_map/all_to_all | solution.py:209
  149.2 0.7 copy-done.5
  149.9 5.2 %shard_map.89.refs_1_ = f32[32,10,4,128]{3,2,1,0:T(4,128)} custom-call(f32[32,5,4,128]{3,2,1,0:T(4,128)} %copy-done.5, f32[32,5,4,128]{3,2,1,0:T(4,128)} %fusion.2.refs_1_.refs_2_, f32[16,256,128]{2,1,0:T(8,128)} %copy.62.refs_1_.refs_2_.refs_3_, s32[8,128]{1,0:T(8,128)} %add_select_fusion.refs_2_.refs_3_.refs_4_, ...), custom_call_target="tpu_custom_call" | custom-call | tf_op jit(solution)/shard_map/pallas_call | solution.py:184
  155.2 20.8 %all_to_all.55 = f32[32,10,4,128]{3,2,1,0:T(4,128)S(1)} all-to-all(f32[32,10,4,128]{3,2,1,0:T(4,128)} %shard_map.89.refs_1_), channel_id=1, replica_groups=mesh['lon'=8,'lat'=4] {'lon','lat'}, dimensions={0} | all-to-all | bytes 1310720 | tf_op jit(solution)/shard_map/all_to_all | solution.py:209
  176.1 0.3 convolution_multiply_fusion
  176.3 0.4 fusion.17
  176.8 0.2 copy.79
  177.0 14.6 %all_to_all.56.refs_0_ = f32[32,5,4,128]{3,2,1,0:T(4,128)} all-to-all(f32[32,5,4,128]{3,2,1,0:T(4,128)S(1)} %bitcast.63), channel_id=1, replica_groups=mesh['lon'=8,'lat'=4] {'lon','lat'}, dimensions={0} | all-to-all | bytes 655360 | tf_op jit(solution)/shard_map/all_to_all | solution.py:209
  191.6 4.5 %shard_map.90 = f32[32,6,4,128]{3,2,1,0:T(4,128)} custom-call(f32[32,5,4,128]{3,2,1,0:T(4,128)} %all_to_all.56.refs_0_, f32[32,10,4,128]{3,2,1,0:T(4,128)} %shard_map.89.refs_1_, f32[32,5,4,128]{3,2,1,0:T(4,128)} %fusion.2.refs_1_.refs_2_, f32[16,256,128]{2,1,0:T(8,128)} %copy.62.refs_1_.refs_2_.refs_3_, s32[8,128]{1,0:T(8,128)} %add_select_fusion.refs_2_.refs_3_.refs_4_, ...), custom_call_target="tpu_custom_call" | custom-call | tf_op jit(solution)/shard_map/pallas_call | solution.py:184
  196.1 15.5 %all_to_all.57 = f32[32,6,4,128]{3,2,1,0:T(4,128)S(1)} all-to-all(f32[32,6,4,128]{3,2,1,0:T(4,128)} %shard_map.90), channel_id=1, replica_groups=mesh['lon'=8,'lat'=4] {'lon','lat'}, dimensions={0} | all-to-all | bytes 786432 | tf_op jit(solution)/shard_map/all_to_all | solution.py:209
  211.7 1.1 fusion.13
  (31 shorter events, 0.4 us)
Async XLA Ops:
  0.6 11.7 %copy-start.7 = (f32[5]{0:T(128)S(1)}, f32[5]{0:T(128)}, u32[]{:S(2)}) copy-start(f32[5]{0:T(128)} %param.12) | copy-start | bytes 64
  5.2 19.8 %all-to-all-start = ((f32[32,6,4,128]{3,2,1,0:T(4,128)}), f32[32,6,4,128]{3,2,1,0:T(4,128)S(1)}, u32[]{:S(2)}, u32[]{:S(2)}) async-start(f32[32,6,4,128]{3,2,1,0:T(4,128)} %pad_maximum_fusion), calls=%async_computation | async-start | bytes 786432 | tf_op jit(solution)/shard_map/all_to_all | solution.py:209
  25.1 4.0 %copy-start = (f32[32,6,4,128]{3,2,1,0:T(4,128)}, f32[32,6,4,128]{3,2,1,0:T(4,128)S(1)}, u32[]{:S(2)}) copy-start(f32[32,6,4,128]{3,2,1,0:T(4,128)S(1)} %all-to-all-done.refs_0_.refs_1_.refs_2_) | copy-start | bytes 1179652
  29.0 18.8 %copy-start.2 = (f32[137,137]{1,0:T(8,128)S(1)}, f32[137,137]{1,0:T(8,128)}, u32[]{:S(2)}) copy-start(f32[137,137]{1,0:T(8,128)} %param.13) | copy-start | bytes 225232
  29.0 18.8 %copy-start.4 = (f32[137,4,128]{2,1,0:T(4,128)S(1)}, f32[137,4,128]{2,1,0:T(4,128)}, u32[]{:S(2)}) copy-start(f32[137,4,128]{2,1,0:T(4,128)} %param.8) | copy-start | bytes 841732
  132.8 4.9 %copy-start.1 = (f32[32,6,4,128]{3,2,1,0:T(4,128)S(1)}, f32[32,6,4,128]{3,2,1,0:T(4,128)}, u32[]{:S(2)}) copy-start(f32[32,6,4,128]{3,2,1,0:T(4,128)} %copy-done) | copy-start | bytes 1179652
  132.8 4.9 %copy-start.3 = (f32[32,10,4,128]{3,2,1,0:T(4,128)S(1)}, f32[32,10,4,128]{3,2,1,0:T(4,128)}, u32[]{:S(2)}) copy-start(f32[32,10,4,128]{3,2,1,0:T(4,128)} %shard_map.87.refs_1_) | copy-start | bytes 1966084
  134.5 14.7 %all-to-all-start.6 = ((f32[32,5,4,128]{3,2,1,0:T(4,128)}), f32[32,5,4,128]{3,2,1,0:T(4,128)S(1)}, u32[]{:S(2)}, u32[]{:S(2)}) async-start(f32[32,5,4,128]{3,2,1,0:T(4,128)} %bitcast.14), calls=%async_computation.6 | async-start | bytes 655360 | tf_op jit(solution)/shard_map/all_to_all | solution.py:209
  149.2 0.7 copy-start.5
  191.6 20.1 %copy-start.6 = (f32[137,4,128]{2,1,0:T(4,128)S(1)}, f32[137,4,128]{2,1,0:T(4,128)}, u32[]{:S(2)}) copy-start(f32[137,4,128]{2,1,0:T(4,128)} %param.7) | copy-start | bytes 841732

commit v9 on v8

--- a/solution.py
+++ b/solution.py
@@ -36,7 +36,7 @@
     tap_ids = jnp.arange(width + 1, dtype=jnp.int32)
     distance = jnp.abs((lane + shift)[:, None] - columns[None, :])
     selector = (distance[:, :, None] == tap_ids[None, None, :]).astype(jnp.float32)
-    return jnp.einsum("pct,jt->jpc", selector, weights, precision=HI)
+    return jnp.einsum("pct,jt->jpc", selector, weights, precision=KERNEL_PRECISION)
 
 
 def mirror_tables(mirror_all, block):

time: 214 us -> 213 us (level)
  no operation moved by 1% of the time
where the time goes in v9:
time: 213 us; the launch traced here: 212 us
  blocking collectives  137 us (64%)
  Pallas kernels  24.5 us (12%)
  waiting for transfers between devices  20.4 us (10%)
  starting transfers between devices  10.2 us (5%)
  other arithmetic  8.27 us (4%)
  local copies, waits for them, and re-layouts  5.86 us (3%)
  matrix products  4.24 us (2%)
    all_to_all x8, blocking collectives, exchange(): return lax.all_to_all(parts, AXES, 0, 0, tiled=True)  137 us
    pallas_call x5, Pallas kernels, level_apply(): pl.pallas_call(functools.partial(_kernel, spec), out_shape=jax.ShapeDtype...  24.5 us
    all_to_all x2, waiting for transfers between devices, exchange(): return lax.all_to_all(parts, AXES, 0, 0, tiled=True)  20.4 us
    all_to_all x2, starting transfers between devices, exchange(): return lax.all_to_all(parts, AXES, 0, 0, tiled=True)  10.2 us
  transfers between devices with their start and end apart: 2, of which 2 were waited for; matrix products, arithmetic and copies ran while one was open for 1% of the time, Pallas kernels for 0%

profile of v9, /device:TPU:1, one launch (start us, length us, event | category | flops | bytes accessed | tf_op | source)
XLA Modules:
  0.0 212.4 jit_solution(17665906949287025575)
XLA Ops:
  0.6 0.8 fusion.39
  1.4 0.2 multiply_reduce_fusion
  1.6 0.1 copy.60
  1.7 0.1 sqrt_reduce_fusion
  1.8 0.8 broadcast_divide_fusion
  2.6 0.1 reshape.291
  2.7 0.7 convert_element_type.17
  3.3 1.0 pad.13
  4.4 0.8 pad_maximum_fusion
  5.2 7.1 %all-to-all-start = ((f32[32,6,4,128]{3,2,1,0:T(4,128)}), f32[32,6,4,128]{3,2,1,0:T(4,128)S(1)}, u32[]{:S(2)}, u32[]{:S(2)}) async-start(f32[32,6,4,128]{3,2,1,0:T(4,128)} %pad_maximum_fusion), calls=%async_computation | async-start | bytes 786432 | tf_op jit(solution)/shard_map/all_to_all | solution.py:209
  12.4 0.7 multiply_reduce_fusion.1
  13.7 0.5 broadcast_divide_fusion.1.refs_3_.refs_4_.refs_5_
  14.3 0.1 subtract_abs_fusion
  14.4 10.7 %all-to-all-done.refs_0_.refs_1_.refs_2_ = f32[32,6,4,128]{3,2,1,0:T(4,128)S(1)} async-done(((f32[32,6,4,128]{3,2,1,0:T(4,128)}), f32[32,6,4,128]{3,2,1,0:T(4,128)S(1)}, u32[]{:S(2)}, u32[]{:S(2)}) %all-to-all-start) | async-done | bytes 393248 | tf_op jit(solution)/shard_map/all_to_all | solution.py:209
  25.1 0.1 reshape.305
  25.2 1.4 fusion
  26.7 2.0 copy.62.refs_1_.refs_2_.refs_3_
  28.6 0.6 add_select_fusion.refs_2_.refs_3_.refs_4_
  29.3 3.7 %shard_map.86 = f32[32,5,4,128]{3,2,1,0:T(4,128)} custom-call(f32[32,6,4,128]{3,2,1,0:T(4,128)} %copy-done, f32[16,256,128]{2,1,0:T(8,128)} %copy.62.refs_1_.refs_2_.refs_3_, s32[8,128]{1,0:T(8,128)} %add_select_fusion.refs_2_.refs_3_.refs_4_, f32[5]{0:T(128)} %broadcast_divide_fusion.1.refs_3_.refs_4_.refs_5_), custom_call_target="tpu_custom_call" | custom-call | tf_op jit(solution)/shard_map/pallas_call | solution.py:184
  32.9 14.5 %all_to_all.50 = f32[32,5,4,128]{3,2,1,0:T(4,128)S(1)} all-to-all(f32[32,5,4,128]{3,2,1,0:T(4,128)} %shard_map.86), channel_id=1, replica_groups=mesh['lon'=8,'lat'=4] {'lon','lat'}, dimensions={0} | all-to-all | bytes 655360 | tf_op jit(solution)/shard_map/all_to_all | solution.py:209
  47.5 0.3 convolution_multiply_fusion.3
  47.7 0.4 fusion.26
  48.2 0.2 copy.65
  48.4 14.2 %all_to_all.51.refs_0_ = f32[32,5,4,128]{3,2,1,0:T(4,128)} all-to-all(f32[32,5,4,128]{3,2,1,0:T(4,128)S(1)} %bitcast.61), channel_id=1, replica_groups=mesh['lon'=8,'lat'=4] {'lon','lat'}, dimensions={0} | all-to-all | bytes 655360 | tf_op jit(solution)/shard_map/all_to_all | solution.py:209
  62.6 5.3 %shard_map.87.refs_1_ = f32[32,10,4,128]{3,2,1,0:T(4,128)} custom-call(f32[32,5,4,128]{3,2,1,0:T(4,128)} %all_to_all.51.refs_0_, f32[32,6,4,128]{3,2,1,0:T(4,128)} %copy-done, f32[16,256,128]{2,1,0:T(8,128)} %copy.62.refs_1_.refs_2_.refs_3_, s32[8,128]{1,0:T(8,128)} %add_select_fusion.refs_2_.refs_3_.refs_4_, f32[5]{0:T(128)} %broadcast_divide_fusion.1.refs_3_.refs_4_.refs_5_), custom_call_target="tpu_custom_call" | custom-call | tf_op jit(solution)/shard_map/pallas_call | solution.py:184
  67.9 20.8 %all_to_all.52 = f32[32,10,4,128]{3,2,1,0:T(4,128)S(1)} all-to-all(f32[32,10,4,128]{3,2,1,0:T(4,128)} %shard_map.87.refs_1_), channel_id=1, replica_groups=mesh['lon'=8,'lat'=4] {'lon','lat'}, dimensions={0} | all-to-all | bytes 1310720 | tf_op jit(solution)/shard_map/all_to_all | solution.py:209
  88.7 0.3 convolution_multiply_fusion.2
  89.0 0.4 fusion.23
  89.4 0.2 copy.69
  89.6 14.6 %all_to_all.53.refs_0_ = f32[32,5,4,128]{3,2,1,0:T(4,128)} all-to-all(f32[32,5,4,128]{3,2,1,0:T(4,128)S(1)} %bitcast.62), channel_id=1, replica_groups=mesh['lon'=8,'lat'=4] {'lon','lat'}, dimensions={0} | all-to-all | bytes 655360 | tf_op jit(solution)/shard_map/all_to_all | solution.py:209
  104.3 5.8 %shard_map.88 = f32[32,11,4,128]{3,2,1,0:T(4,128)} custom-call(f32[32,5,4,128]{3,2,1,0:T(4,128)} %all_to_all.53.refs_0_, f32[32,10,4,128]{3,2,1,0:T(4,128)} %shard_map.87.refs_1_, f32[32,6,4,128]{3,2,1,0:T(4,128)} %copy-done, f32[16,256,128]{2,1,0:T(8,128)} %copy.62.refs_1_.refs_2_.refs_3_, s32[8,128]{1,0:T(8,128)} %add_select_fusion.refs_2_.refs_3_.refs_4_, ...), custom_call_target="tpu_custom_call" | custom-call | tf_op jit(solution)/shard_map/pallas_call | solution.py:184
  110.1 22.2 %all_to_all.54 = f32[32,11,4,128]{3,2,1,0:T(4,128)S(1)} all-to-all(f32[32,11,4,128]{3,2,1,0:T(4,128)} %shard_map.88), channel_id=1, replica_groups=mesh['lon'=8,'lat'=4] {'lon','lat'}, dimensions={0} | all-to-all | bytes 1441792 | tf_op jit(solution)/shard_map/all_to_all | solution.py:209
  132.4 0.3 convolution_multiply_fusion.1
  132.7 0.4 fusion.20
  133.1 0.9 copy.75
  134.1 3.2 %all-to-all-start.6 = ((f32[32,5,4,128]{3,2,1,0:T(4,128)}), f32[32,5,4,128]{3,2,1,0:T(4,128)S(1)}, u32[]{:S(2)}, u32[]{:S(2)}) async-start(f32[32,5,4,128]{3,2,1,0:T(4,128)} %bitcast.14), calls=%async_computation.6 | async-start | bytes 655360 | tf_op jit(solution)/shard_map/all_to_all | solution.py:209
  137.3 1.8 fusion.2.refs_1_.refs_2_
  139.1 9.7 %all-to-all-done.6.refs_0_ = f32[32,5,4,128]{3,2,1,0:T(4,128)S(1)} async-done(((f32[32,5,4,128]{3,2,1,0:T(4,128)}), f32[32,5,4,128]{3,2,1,0:T(4,128)S(1)}, u32[]{:S(2)}, u32[]{:S(2)}) %all-to-all-start.6) | async-done | bytes 327712 | tf_op jit(solution)/shard_map/all_to_all | solution.py:209
  148.8 0.7 copy-done.5
  149.5 5.2 %shard_map.89.refs_1_ = f32[32,10,4,128]{3,2,1,0:T(4,128)} custom-call(f32[32,5,4,128]{3,2,1,0:T(4,128)} %copy-done.5, f32[32,5,4,128]{3,2,1,0:T(4,128)} %fusion.2.refs_1_.refs_2_, f32[16,256,128]{2,1,0:T(8,128)} %copy.62.refs_1_.refs_2_.refs_3_, s32[8,128]{1,0:T(8,128)} %add_select_fusion.refs_2_.refs_3_.refs_4_, ...), custom_call_target="tpu_custom_call" | custom-call | tf_op jit(solution)/shard_map/pallas_call | solution.py:184
  154.8 20.8 %all_to_all.55 = f32[32,10,4,128]{3,2,1,0:T(4,128)S(1)} all-to-all(f32[32,10,4,128]{3,2,1,0:T(4,128)} %shard_map.89.refs_1_), channel_id=1, replica_groups=mesh['lon'=8,'lat'=4] {'lon','lat'}, dimensions={0} | all-to-all | bytes 1310720 | tf_op jit(solution)/shard_map/all_to_all | solution.py:209
  175.7 0.3 convolution_multiply_fusion
  176.0 0.4 fusion.17
  176.4 0.2 copy.79
  176.6 14.6 %all_to_all.56.refs_0_ = f32[32,5,4,128]{3,2,1,0:T(4,128)} all-to-all(f32[32,5,4,128]{3,2,1,0:T(4,128)S(1)} %bitcast.63), channel_id=1, replica_groups=mesh['lon'=8,'lat'=4] {'lon','lat'}, dimensions={0} | all-to-all | bytes 655360 | tf_op jit(solution)/shard_map/all_to_all | solution.py:209
  191.2 4.5 %shard_map.90 = f32[32,6,4,128]{3,2,1,0:T(4,128)} custom-call(f32[32,5,4,128]{3,2,1,0:T(4,128)} %all_to_all.56.refs_0_, f32[32,10,4,128]{3,2,1,0:T(4,128)} %shard_map.89.refs_1_, f32[32,5,4,128]{3,2,1,0:T(4,128)} %fusion.2.refs_1_.refs_2_, f32[16,256,128]{2,1,0:T(8,128)} %copy.62.refs_1_.refs_2_.refs_3_, s32[8,128]{1,0:T(8,128)} %add_select_fusion.refs_2_.refs_3_.refs_4_, ...), custom_call_target="tpu_custom_call" | custom-call | tf_op jit(solution)/shard_map/pallas_call | solution.py:184
  195.8 15.5 %all_to_all.57 = f32[32,6,4,128]{3,2,1,0:T(4,128)S(1)} all-to-all(f32[32,6,4,128]{3,2,1,0:T(4,128)} %shard_map.90), channel_id=1, replica_groups=mesh['lon'=8,'lat'=4] {'lon','lat'}, dimensions={0} | all-to-all | bytes 786432 | tf_op jit(solution)/shard_map/all_to_all | solution.py:209
  211.4 1.1 fusion.13
  (31 shorter events, 0.4 us)
Async XLA Ops:
  0.6 11.7 %copy-start.7 = (f32[5]{0:T(128)S(1)}, f32[5]{0:T(128)}, u32[]{:S(2)}) copy-start(f32[5]{0:T(128)} %param.12) | copy-start | bytes 64
  5.2 19.8 %all-to-all-start = ((f32[32,6,4,128]{3,2,1,0:T(4,128)}), f32[32,6,4,128]{3,2,1,0:T(4,128)S(1)}, u32[]{:S(2)}, u32[]{:S(2)}) async-start(f32[32,6,4,128]{3,2,1,0:T(4,128)} %pad_maximum_fusion), calls=%async_computation | async-start | bytes 786432 | tf_op jit(solution)/shard_map/all_to_all | solution.py:209
  25.1 3.6 %copy-start = (f32[32,6,4,128]{3,2,1,0:T(4,128)}, f32[32,6,4,128]{3,2,1,0:T(4,128)S(1)}, u32[]{:S(2)}) copy-start(f32[32,6,4,128]{3,2,1,0:T(4,128)S(1)} %all-to-all-done.refs_0_.refs_1_.refs_2_) | copy-start | bytes 1179652
  28.6 18.8 %copy-start.2 = (f32[137,137]{1,0:T(8,128)S(1)}, f32[137,137]{1,0:T(8,128)}, u32[]{:S(2)}) copy-start(f32[137,137]{1,0:T(8,128)} %param.13) | copy-start | bytes 225232
  28.6 18.8 %copy-start.4 = (f32[137,4,128]{2,1,0:T(4,128)S(1)}, f32[137,4,128]{2,1,0:T(4,128)}, u32[]{:S(2)}) copy-start(f32[137,4,128]{2,1,0:T(4,128)} %param.8) | copy-start | bytes 841732
  132.4 4.9 %copy-start.1 = (f32[32,6,4,128]{3,2,1,0:T(4,128)S(1)}, f32[32,6,4,128]{3,2,1,0:T(4,128)}, u32[]{:S(2)}) copy-start(f32[32,6,4,128]{3,2,1,0:T(4,128)} %copy-done) | copy-start | bytes 1179652
  132.4 4.9 %copy-start.3 = (f32[32,10,4,128]{3,2,1,0:T(4,128)S(1)}, f32[32,10,4,128]{3,2,1,0:T(4,128)}, u32[]{:S(2)}) copy-start(f32[32,10,4,128]{3,2,1,0:T(4,128)} %shard_map.87.refs_1_) | copy-start | bytes 1966084
  134.1 14.7 %all-to-all-start.6 = ((f32[32,5,4,128]{3,2,1,0:T(4,128)}), f32[32,5,4,128]{3,2,1,0:T(4,128)S(1)}, u32[]{:S(2)}, u32[]{:S(2)}) async-start(f32[32,5,4,128]{3,2,1,0:T(4,128)} %bitcast.14), calls=%async_computation.6 | async-start | bytes 655360 | tf_op jit(solution)/shard_map/all_to_all | solution.py:209
  148.8 0.7 copy-start.5
  191.2 20.1 %copy-start.6 = (f32[137,4,128]{2,1,0:T(4,128)S(1)}, f32[137,4,128]{2,1,0:T(4,128)}, u32[]{:S(2)}) copy-start(f32[137,4,128]{2,1,0:T(4,128)} %param.7) | copy-start | bytes 841732

commit v10 on v9

--- a/solution.py
+++ b/solution.py
@@ -79,8 +79,10 @@
         polar = polar.reshape(2 * depth * lp, block)
         high = polar.astype(jnp.bfloat16)
         low = (polar - high.astype(jnp.float32)).astype(jnp.bfloat16)
-        out = jnp.dot(high, onehot, preferred_element_type=jnp.float32) + jnp.dot(
-            low, onehot, preferred_element_type=jnp.float32
+        out = jnp.dot(
+            jnp.concatenate([high, low], axis=1),
+            jnp.concatenate([onehot, onehot], axis=0),
+            preferred_element_type=jnp.float32,
         )
         mir[:, pl.ds(b, 1)] = out.reshape(2 * depth, 1, lp, block)
         return carry

time: 213 us -> 213 us (level)
  no operation moved by 1% of the time
where the time goes in v10:
time: 213 us; the launch traced here: 212 us
  blocking collectives  137 us (64%)
  Pallas kernels  24.4 us (11%)
  waiting for transfers between devices  20.4 us (10%)
  starting transfers between devices  10.2 us (5%)
  other arithmetic  8.27 us (4%)
  local copies, waits for them, and re-layouts  5.86 us (3%)
  matrix products  4.24 us (2%)
    all_to_all x8, blocking collectives, exchange(): return lax.all_to_all(parts, AXES, 0, 0, tiled=True)  137 us
    pallas_call x5, Pallas kernels, level_apply(): pl.pallas_call(functools.partial(_kernel, spec), out_shape=jax.ShapeDtype...  24.4 us
    all_to_all x2, waiting for transfers between devices, exchange(): return lax.all_to_all(parts, AXES, 0, 0, tiled=True)  20.4 us
    all_to_all x2, starting transfers between devices, exchange(): return lax.all_to_all(parts, AXES, 0, 0, tiled=True)  10.2 us
  transfers between devices with their start and end apart: 2, of which 2 were waited for; matrix products, arithmetic and copies ran while one was open for 1% of the time, Pallas kernels for 0%

profile of v10, /device:TPU:1, one launch (start us, length us, event | category | flops | bytes accessed | tf_op | source)
XLA Modules:
  0.0 212.3 jit_solution(13802331346185181983)
XLA Ops:
  0.6 0.8 fusion.39
  1.4 0.2 multiply_reduce_fusion
  1.6 0.1 copy.60
  1.7 0.1 sqrt_reduce_fusion
  1.8 0.8 broadcast_divide_fusion
  2.6 0.1 reshape.291
  2.7 0.7 convert_element_type.17
  3.3 1.0 pad.13
  4.4 0.8 pad_maximum_fusion
  5.2 7.1 %all-to-all-start = ((f32[32,6,4,128]{3,2,1,0:T(4,128)}), f32[32,6,4,128]{3,2,1,0:T(4,128)S(1)}, u32[]{:S(2)}, u32[]{:S(2)}) async-start(f32[32,6,4,128]{3,2,1,0:T(4,128)} %pad_maximum_fusion), calls=%async_computation | async-start | bytes 786432 | tf_op jit(solution)/shard_map/all_to_all | solution.py:211
  12.4 0.7 multiply_reduce_fusion.1
  13.7 0.5 broadcast_divide_fusion.1.refs_3_.refs_4_.refs_5_
  14.3 0.1 subtract_abs_fusion
  14.4 10.7 %all-to-all-done.refs_0_.refs_1_.refs_2_ = f32[32,6,4,128]{3,2,1,0:T(4,128)S(1)} async-done(((f32[32,6,4,128]{3,2,1,0:T(4,128)}), f32[32,6,4,128]{3,2,1,0:T(4,128)S(1)}, u32[]{:S(2)}, u32[]{:S(2)}) %all-to-all-start) | async-done | bytes 393248 | tf_op jit(solution)/shard_map/all_to_all | solution.py:211
  25.1 0.1 reshape.305
  25.2 1.4 fusion
  26.7 2.0 copy.62.refs_1_.refs_2_.refs_3_
  28.6 0.6 add_select_fusion.refs_2_.refs_3_.refs_4_
  29.3 3.7 %shard_map.86 = f32[32,5,4,128]{3,2,1,0:T(4,128)} custom-call(f32[32,6,4,128]{3,2,1,0:T(4,128)} %copy-done, f32[16,256,128]{2,1,0:T(8,128)} %copy.62.refs_1_.refs_2_.refs_3_, s32[8,128]{1,0:T(8,128)} %add_select_fusion.refs_2_.refs_3_.refs_4_, f32[5]{0:T(128)} %broadcast_divide_fusion.1.refs_3_.refs_4_.refs_5_), custom_call_target="tpu_custom_call" | custom-call | tf_op jit(solution)/shard_map/pallas_call | solution.py:186
  32.9 14.5 %all_to_all.50 = f32[32,5,4,128]{3,2,1,0:T(4,128)S(1)} all-to-all(f32[32,5,4,128]{3,2,1,0:T(4,128)} %shard_map.86), channel_id=1, replica_groups=mesh['lon'=8,'lat'=4] {'lon','lat'}, dimensions={0} | all-to-all | bytes 655360 | tf_op jit(solution)/shard_map/all_to_all | solution.py:211
  47.4 0.3 convolution_multiply_fusion.3
  47.7 0.4 fusion.26
  48.1 0.2 copy.65
  48.4 14.2 %all_to_all.51.refs_0_ = f32[32,5,4,128]{3,2,1,0:T(4,128)} all-to-all(f32[32,5,4,128]{3,2,1,0:T(4,128)S(1)} %bitcast.61), channel_id=1, replica_groups=mesh['lon'=8,'lat'=4] {'lon','lat'}, dimensions={0} | all-to-all | bytes 655360 | tf_op jit(solution)/shard_map/all_to_all | solution.py:211
  62.6 5.2 %shard_map.87.refs_1_ = f32[32,10,4,128]{3,2,1,0:T(4,128)} custom-call(f32[32,5,4,128]{3,2,1,0:T(4,128)} %all_to_all.51.refs_0_, f32[32,6,4,128]{3,2,1,0:T(4,128)} %copy-done, f32[16,256,128]{2,1,0:T(8,128)} %copy.62.refs_1_.refs_2_.refs_3_, s32[8,128]{1,0:T(8,128)} %add_select_fusion.refs_2_.refs_3_.refs_4_, f32[5]{0:T(128)} %broadcast_divide_fusion.1.refs_3_.refs_4_.refs_5_), custom_call_target="tpu_custom_call" | custom-call | tf_op jit(solution)/shard_map/pallas_call | solution.py:186
  67.8 20.8 %all_to_all.52 = f32[32,10,4,128]{3,2,1,0:T(4,128)S(1)} all-to-all(f32[32,10,4,128]{3,2,1,0:T(4,128)} %shard_map.87.refs_1_), channel_id=1, replica_groups=mesh['lon'=8,'lat'=4] {'lon','lat'}, dimensions={0} | all-to-all | bytes 1310720 | tf_op jit(solution)/shard_map/all_to_all | solution.py:211
  88.7 0.3 convolution_multiply_fusion.2
  89.0 0.4 fusion.23
  89.4 0.2 copy.69
  89.6 14.6 %all_to_all.53.refs_0_ = f32[32,5,4,128]{3,2,1,0:T(4,128)} all-to-all(f32[32,5,4,128]{3,2,1,0:T(4,128)S(1)} %bitcast.62), channel_id=1, replica_groups=mesh['lon'=8,'lat'=4] {'lon','lat'}, dimensions={0} | all-to-all | bytes 655360 | tf_op jit(solution)/shard_map/all_to_all | solution.py:211
  104.2 5.8 %shard_map.88 = f32[32,11,4,128]{3,2,1,0:T(4,128)} custom-call(f32[32,5,4,128]{3,2,1,0:T(4,128)} %all_to_all.53.refs_0_, f32[32,10,4,128]{3,2,1,0:T(4,128)} %shard_map.87.refs_1_, f32[32,6,4,128]{3,2,1,0:T(4,128)} %copy-done, f32[16,256,128]{2,1,0:T(8,128)} %copy.62.refs_1_.refs_2_.refs_3_, s32[8,128]{1,0:T(8,128)} %add_select_fusion.refs_2_.refs_3_.refs_4_, ...), custom_call_target="tpu_custom_call" | custom-call | tf_op jit(solution)/shard_map/pallas_call | solution.py:186
  110.0 22.2 %all_to_all.54 = f32[32,11,4,128]{3,2,1,0:T(4,128)S(1)} all-to-all(f32[32,11,4,128]{3,2,1,0:T(4,128)} %shard_map.88), channel_id=1, replica_groups=mesh['lon'=8,'lat'=4] {'lon','lat'}, dimensions={0} | all-to-all | bytes 1441792 | tf_op jit(solution)/shard_map/all_to_all | solution.py:211
  132.3 0.3 convolution_multiply_fusion.1
  132.6 0.4 fusion.20
  133.0 0.9 copy.75
  134.0 3.2 %all-to-all-start.6 = ((f32[32,5,4,128]{3,2,1,0:T(4,128)}), f32[32,5,4,128]{3,2,1,0:T(4,128)S(1)}, u32[]{:S(2)}, u32[]{:S(2)}) async-start(f32[32,5,4,128]{3,2,1,0:T(4,128)} %bitcast.14), calls=%async_computation.6 | async-start | bytes 655360 | tf_op jit(solution)/shard_map/all_to_all | solution.py:211
  137.2 1.8 fusion.2.refs_1_.refs_2_
  139.0 9.7 %all-to-all-done.6.refs_0_ = f32[32,5,4,128]{3,2,1,0:T(4,128)S(1)} async-done(((f32[32,5,4,128]{3,2,1,0:T(4,128)}), f32[32,5,4,128]{3,2,1,0:T(4,128)S(1)}, u32[]{:S(2)}, u32[]{:S(2)}) %all-to-all-start.6) | async-done | bytes 327712 | tf_op jit(solution)/shard_map/all_to_all | solution.py:211
  148.7 0.7 copy-done.5
  149.4 5.2 %shard_map.89.refs_1_ = f32[32,10,4,128]{3,2,1,0:T(4,128)} custom-call(f32[32,5,4,128]{3,2,1,0:T(4,128)} %copy-done.5, f32[32,5,4,128]{3,2,1,0:T(4,128)} %fusion.2.refs_1_.refs_2_, f32[16,256,128]{2,1,0:T(8,128)} %copy.62.refs_1_.refs_2_.refs_3_, s32[8,128]{1,0:T(8,128)} %add_select_fusion.refs_2_.refs_3_.refs_4_, ...), custom_call_target="tpu_custom_call" | custom-call | tf_op jit(solution)/shard_map/pallas_call | solution.py:186
  154.7 20.8 %all_to_all.55 = f32[32,10,4,128]{3,2,1,0:T(4,128)S(1)} all-to-all(f32[32,10,4,128]{3,2,1,0:T(4,128)} %shard_map.89.refs_1_), channel_id=1, replica_groups=mesh['lon'=8,'lat'=4] {'lon','lat'}, dimensions={0} | all-to-all | bytes 1310720 | tf_op jit(solution)/shard_map/all_to_all | solution.py:211
  175.5 0.3 convolution_multiply_fusion
  175.8 0.4 fusion.17
  176.2 0.2 copy.79
  176.5 14.6 %all_to_all.56.refs_0_ = f32[32,5,4,128]{3,2,1,0:T(4,128)} all-to-all(f32[32,5,4,128]{3,2,1,0:T(4,128)S(1)} %bitcast.63), channel_id=1, replica_groups=mesh['lon'=8,'lat'=4] {'lon','lat'}, dimensions={0} | all-to-all | bytes 655360 | tf_op jit(solution)/shard_map/all_to_all | solution.py:211
  191.1 4.6 %shard_map.90 = f32[32,6,4,128]{3,2,1,0:T(4,128)} custom-call(f32[32,5,4,128]{3,2,1,0:T(4,128)} %all_to_all.56.refs_0_, f32[32,10,4,128]{3,2,1,0:T(4,128)} %shard_map.89.refs_1_, f32[32,5,4,128]{3,2,1,0:T(4,128)} %fusion.2.refs_1_.refs_2_, f32[16,256,128]{2,1,0:T(8,128)} %copy.62.refs_1_.refs_2_.refs_3_, s32[8,128]{1,0:T(8,128)} %add_select_fusion.refs_2_.refs_3_.refs_4_, ...), custom_call_target="tpu_custom_call" | custom-call | tf_op jit(solution)/shard_map/pallas_call | solution.py:186
  195.6 15.5 %all_to_all.57 = f32[32,6,4,128]{3,2,1,0:T(4,128)S(1)} all-to-all(f32[32,6,4,128]{3,2,1,0:T(4,128)} %shard_map.90), channel_id=1, replica_groups=mesh['lon'=8,'lat'=4] {'lon','lat'}, dimensions={0} | all-to-all | bytes 786432 | tf_op jit(solution)/shard_map/all_to_all | solution.py:211
  211.2 1.1 fusion.13
  (31 shorter events, 0.4 us)
Async XLA Ops:
  0.6 11.7 %copy-start.7 = (f32[5]{0:T(128)S(1)}, f32[5]{0:T(128)}, u32[]{:S(2)}) copy-start(f32[5]{0:T(128)} %param.12) | copy-start | bytes 64
  5.2 19.8 %all-to-all-start = ((f32[32,6,4,128]{3,2,1,0:T(4,128)}), f32[32,6,4,128]{3,2,1,0:T(4,128)S(1)}, u32[]{:S(2)}, u32[]{:S(2)}) async-start(f32[32,6,4,128]{3,2,1,0:T(4,128)} %pad_maximum_fusion), calls=%async_computation | async-start | bytes 786432 | tf_op jit(solution)/shard_map/all_to_all | solution.py:211
  25.1 3.6 %copy-start = (f32[32,6,4,128]{3,2,1,0:T(4,128)}, f32[32,6,4,128]{3,2,1,0:T(4,128)S(1)}, u32[]{:S(2)}) copy-start(f32[32,6,4,128]{3,2,1,0:T(4,128)S(1)} %all-to-all-done.refs_0_.refs_1_.refs_2_) | copy-start | bytes 1179652
  28.6 18.8 %copy-start.2 = (f32[137,137]{1,0:T(8,128)S(1)}, f32[137,137]{1,0:T(8,128)}, u32[]{:S(2)}) copy-start(f32[137,137]{1,0:T(8,128)} %param.13) | copy-start | bytes 225232
  28.6 18.8 %copy-start.4 = (f32[137,4,128]{2,1,0:T(4,128)S(1)}, f32[137,4,128]{2,1,0:T(4,128)}, u32[]{:S(2)}) copy-start(f32[137,4,128]{2,1,0:T(4,128)} %param.8) | copy-start | bytes 841732
  132.3 4.9 %copy-start.1 = (f32[32,6,4,128]{3,2,1,0:T(4,128)S(1)}, f32[32,6,4,128]{3,2,1,0:T(4,128)}, u32[]{:S(2)}) copy-start(f32[32,6,4,128]{3,2,1,0:T(4,128)} %copy-done) | copy-start | bytes 1179652
  132.3 4.9 %copy-start.3 = (f32[32,10,4,128]{3,2,1,0:T(4,128)S(1)}, f32[32,10,4,128]{3,2,1,0:T(4,128)}, u32[]{:S(2)}) copy-start(f32[32,10,4,128]{3,2,1,0:T(4,128)} %shard_map.87.refs_1_) | copy-start | bytes 1966084
  134.0 14.7 %all-to-all-start.6 = ((f32[32,5,4,128]{3,2,1,0:T(4,128)}), f32[32,5,4,128]{3,2,1,0:T(4,128)S(1)}, u32[]{:S(2)}, u32[]{:S(2)}) async-start(f32[32,5,4,128]{3,2,1,0:T(4,128)} %bitcast.14), calls=%async_computation.6 | async-start | bytes 655360 | tf_op jit(solution)/shard_map/all_to_all | solution.py:211
  148.7 0.7 copy-start.5
  191.1 20.1 %copy-start.6 = (f32[137,4,128]{2,1,0:T(4,128)S(1)}, f32[137,4,128]{2,1,0:T(4,128)}, u32[]{:S(2)}) copy-start(f32[137,4,128]{2,1,0:T(4,128)} %param.7) | copy-start | bytes 841732
